TPU v7x, 512 devices: a whole 4x8x8 slice. The times are simulated.
512 devices in a mesh: row: 32 (over z_lo, y), col: 16 (over x, z_hi, core).
Axes of the slice: x: 4, y: 8, z: 8 (z_hi: 2, z_lo: 4; z = z_hi * 4 + z_lo), core: 2. Of those that a mesh axis runs over, the one named last changes fastest.
Arguments:
- queries: bfloat16 [1, 32, 32, 64, 2048], P(None, 'row', 'col'), may hold values from -17 to 17
- keys: bfloat16 [1, 32, 32, 64, 2048], P(None, 'row', 'col'), may hold values from -5.5 to 5.5
- values: bfloat16 [1, 32, 32, 64, 2048], P(None, 'row', 'col'), may hold values from -6 to 6
- pool_keys: bfloat16 [1024, 16, 2048], P(('row', 'col')), may hold values from -6 to 6
- pool_values: bfloat16 [1024, 16, 2048], P(('row', 'col')), may hold values from -6 to 6
- top_keys: bfloat16 [1, 128, 2048], P(None, 'col'), may hold values from -6 to 6
- top_values: bfloat16 [1, 128, 2048], P(None, 'col'), may hold values from -6 to 6
- coarse_ids: int32 [1, 32, 32, 8], P(None, 'row', 'col'), may hold values from 0 to 1023, as said below
Outputs:
- attended: bfloat16 [1, 32, 32, 64, 2048], P(None, 'row', 'col')
Inputs may be any that keep to these rules, and one draw needn't show every extreme that they name: Entry coarse_ids[n, i, j, c] names a pool block held by the device that holds fine block (i, j) or by one of its eight neighbours in the mesh (no wrap); the device with row index r and col index q holds pool blocks (r * 16 + q) * 2 to (r * 16 + q + 1) * 2 - 1. The 8 entries of a fine block differ.
All inputs are finite; a program needn't handle non-finite values.
Results may differ from a plain program's by a relative error of at most 0.0049.
Values may be sent and summed in bfloat16 or wider, within the bound.
No kernel may reach another device: no remote copies, remote signals or barrier semaphores. Data moves between devices by JAX's collectives and lax.ppermute only.
A program may use at most 64 MiB of HBM per device.

v0:
```python
import math

import jax
import jax.numpy as jnp
from jax import lax
from jax.sharding import PartitionSpec as P

HEADS = 16


NEG_FILL = -1e30


def extended(block, sides, width):
    for axis, dim in sides:
        count = lax.axis_size(axis)
        forward = [(i, i + 1) for i in range(count - 1)]
        backward = [(target, source) for source, target in forward]
        low = lax.ppermute(
            lax.slice_in_dim(block, block.shape[dim] - width, None, axis=dim), axis, forward
        )
        high = lax.ppermute(lax.slice_in_dim(block, 0, width, axis=dim), axis, backward)
        block = jnp.concatenate([low, block, high], axis=dim)
    return block


def body(queries, keys, values, pool_keys, pool_values, top_keys, top_values, coarse_ids):
    images, brow_count, bcol_count, block_tokens, model_width = queries.shape
    head_count = HEADS
    head_width = model_width // head_count
    score_scale = 1.0 / math.sqrt(head_width)
    pool_blocks = pool_keys.shape[0]
    pool_tokens = pool_keys.shape[1]
    row_count = lax.axis_size("row")
    col_count = lax.axis_size("col")
    row_index = lax.axis_index("row")
    col_index = lax.axis_index("col")
    pool_key_grid = pool_keys.reshape(1, 1, 1, pool_blocks * pool_tokens, model_width)
    pool_value_grid = pool_values.reshape(1, 1, 1, pool_blocks * pool_tokens, model_width)
    near_keys, near_values = (
        extended(keys, (("row", 1), ("col", 2)), 1),
        extended(values, (("row", 1), ("col", 2)), 1),
    )
    around_keys, around_values = (
        extended(pool_key_grid, (("row", 1), ("col", 2)), 1),
        extended(pool_value_grid, (("row", 1), ("col", 2)), 1),
    )
    around_keys = around_keys.reshape(9 * pool_blocks, pool_tokens, model_width)
    around_values = around_values.reshape(9 * pool_blocks, pool_tokens, model_width)
    top_all_keys, top_all_values = (
        lax.all_gather(top_keys, "col", axis=1, tiled=True),
        lax.all_gather(top_values, "col", axis=1, tiled=True),
    )
    owner_device = coarse_ids // pool_blocks
    owner_row = owner_device // col_count
    owner_col = owner_device % col_count
    local_slot = (
        (owner_row - row_index + 1) * 3 + (owner_col - col_index + 1)
    ) * pool_blocks + coarse_ids % pool_blocks
    global_row = row_index * brow_count + jnp.arange(brow_count, dtype=jnp.int32)
    global_col = col_index * bcol_count + jnp.arange(bcol_count, dtype=jnp.int32)
    total_rows = brow_count * row_count
    total_cols = bcol_count * col_count
    blocks = brow_count * bcol_count
    coarse_length = coarse_ids.shape[-1] * pool_tokens
    valid_parts = []
    for row_step in range(3):
        row_valid = (global_row + row_step - 1 >= 0) & (global_row + row_step - 1 < total_rows)
        for col_step in range(3):
            col_valid = (global_col + col_step - 1 >= 0) & (global_col + col_step - 1 < total_cols)
            part_valid = (row_valid[:, None] & col_valid[None, :]).reshape(blocks, 1)
            valid_parts.append(jnp.broadcast_to(part_valid, (blocks, block_tokens)))
    valid_parts.append(jnp.ones((blocks, coarse_length), dtype=bool))
    list_valid = jnp.concatenate(valid_parts, axis=1).reshape(blocks, 1, 1, -1)

    def attend_image(image_items):
        query_image, key_image, value_image, slot_image, top_key_image, top_value_image = (
            image_items
        )
        query_heads = query_image.reshape(blocks, block_tokens, head_count, head_width)
        key_lists = []
        value_lists = []
        for row_step in range(3):
            for col_step in range(3):
                key_lists.append(
                    key_image[
                        row_step : row_step + brow_count, col_step : col_step + bcol_count
                    ].reshape(blocks, block_tokens, model_width)
                )
                value_lists.append(
                    value_image[
                        row_step : row_step + brow_count, col_step : col_step + bcol_count
                    ].reshape(blocks, block_tokens, model_width)
                )
        key_lists.append(around_keys[slot_image].reshape(blocks, coarse_length, model_width))
        value_lists.append(around_values[slot_image].reshape(blocks, coarse_length, model_width))
        key_list = jnp.concatenate(key_lists, axis=1).reshape(blocks, -1, head_count, head_width)
        value_list = jnp.concatenate(value_lists, axis=1).reshape(
            blocks, -1, head_count, head_width
        )
        near_scores = (
            jnp.einsum("bqhd,bkhd->bhqk", query_heads, key_list, preferred_element_type=jnp.float32)
            * score_scale
        )
        near_scores = jnp.where(list_valid, near_scores, NEG_FILL)
        top_key_heads = top_key_image.reshape(-1, head_count, head_width)
        top_value_heads = top_value_image.reshape(-1, head_count, head_width)
        top_scores = (
            jnp.einsum(
                "bqhd,khd->bhqk", query_heads, top_key_heads, preferred_element_type=jnp.float32
            )
            * score_scale
        )
        row_peak = jnp.maximum(
            jnp.max(near_scores, axis=-1, keepdims=True),
            jnp.max(top_scores, axis=-1, keepdims=True),
        )
        near_exponent = jnp.exp(near_scores - row_peak)
        top_exponent = jnp.exp(top_scores - row_peak)
        row_total = jnp.sum(near_exponent, axis=-1, keepdims=True) + jnp.sum(
            top_exponent, axis=-1, keepdims=True
        )
        near_weights = (near_exponent / row_total).astype(jnp.bfloat16)
        top_weights = (top_exponent / row_total).astype(jnp.bfloat16)
        result = jnp.einsum(
            "bhqk,bkhd->bqhd", near_weights, value_list, preferred_element_type=jnp.float32
        )
        result = result + jnp.einsum(
            "bhqk,khd->bqhd", top_weights, top_value_heads, preferred_element_type=jnp.float32
        )
        return result.reshape(brow_count, bcol_count, block_tokens, model_width).astype(
            jnp.bfloat16
        )

    return lax.map(
        attend_image, (queries, near_keys, near_values, local_slot, top_all_keys, top_all_values)
    )


def solution(mesh):
    placed = (
        P(None, "row", "col", None, None),
        P(None, "row", "col", None, None),
        P(None, "row", "col", None, None),
        P(("row", "col"), None, None),
        P(("row", "col"), None, None),
        P(None, "col", None),
        P(None, "col", None),
        P(None, "row", "col", None),
    )
    return jax.shard_map(
        body,
        mesh=mesh,
        in_specs=placed,
        out_specs=P(None, "row", "col", None, None),
        check_vma=False,
    )
```

profile of v0, /device:TPU:6, one launch (start us, length us, event | category | flops | bytes accessed | tf_op | source)
XLA Modules:
  0.0 241.0 jit_solution(14862765426312695609)
XLA Ops:
  0.0 3.6 %collective-permute-start = (bf16[1,1,2,64,2048]{4,3,2,1,0:T(8,128)(2,1)}, bf16[1,1,2,64,2048]{4,3,2,1,0:T(8,128)(2,1)S(1)}, u32[]{:S(2)}, u32[]{:S(2)}) collective-permute-start(bf16[1,1,2,64,2048]{4,3,2,1,0:T(8,128)(2,1)} %param.10), channel_id=1, source_target_pairs={{0,16},{16,32},{32,48},{48,64},{64,80},{80,96},{96,112},{112,128},... | collective-permute-start | bytes 1572872 | tf_op jit(solution)/shard_map/ppermute | solution.py:19
  6.2 5.8 %collective-permute-start.4 = (bf16[1,1,1,32,2048]{4,3,2,1,0:T(8,128)(2,1)}, bf16[1,1,1,32,2048]{4,3,2,1,0:T(8,128)(2,1)}, u32[]{:S(2)}, u32[]{:S(2)}) collective-permute-start(bf16[1,1,1,32,2048]{4,3,2,1,0:T(8,128)(2,1)} %bitcast.215), channel_id=1, source_target_pairs={{0,16},{16,32},{32,48},{48,64},{64,80},{80,96},{96,112},{112,128},... | collective-permute-start | bytes 393224 | tf_op jit(solution)/shard_map/ppermute | solution.py:19
  17.8 35.2 %all_gather.6 = bf16[1,128,2048]{2,1,0:T(8,128)(2,1)S(1)} all-gather(bf16[1,8,2048]{2,1,0:T(8,128)(2,1)} %param.13), channel_id=1, replica_groups=mesh['row'=32,'col'=16] {'col'}, dimensions={1}, use_global_device_ids=true | all-gather | bytes 557056 | tf_op jit(solution)/shard_map/all_gather | solution.py:51
  54.0 27.7 %all_gather.7 = bf16[1,128,2048]{2,1,0:T(8,128)(2,1)S(1)} all-gather(bf16[1,8,2048]{2,1,0:T(8,128)(2,1)} %param.14), channel_id=1, replica_groups=mesh['row'=32,'col'=16] {'col'}, dimensions={1}, use_global_device_ids=true | all-gather | bytes 557056 | tf_op jit(solution)/shard_map/all_gather | solution.py:52
  88.1 8.0 %collective-permute-start.12 = (bf16[1,1,1,32,2048]{4,3,2,1,0:T(8,128)(2,1)S(1)}, bf16[1,1,1,32,2048]{4,3,2,1,0:T(8,128)(2,1)S(1)}, u32[]{:S(2)}, u32[]{:S(2)}) collective-permute-start(bf16[1,1,1,32,2048]{4,3,2,1,0:T(8,128)(2,1)S(1)} %bitcast.219), channel_id=1, source_target_pairs={{0,16},{16,32},{32,48},{48,64},{64,80},{80,96},{96,112},{112,128},... | collective-permute-start | bytes 393224 | tf_op jit(solution)/shard_map/ppermute | solution.py:19
  96.1 3.7 %collective-permute-start.8 = (bf16[1,1,2,64,2048]{4,3,2,1,0:T(8,128)(2,1)}, bf16[1,1,2,64,2048]{4,3,2,1,0:T(8,128)(2,1)S(1)}, u32[]{:S(2)}, u32[]{:S(2)}) collective-permute-start(bf16[1,1,2,64,2048]{4,3,2,1,0:T(8,128)(2,1)} %param.9), channel_id=1, source_target_pairs={{0,16},{16,32},{32,48},{48,64},{64,80},{80,96},{96,112},{112,128},... | collective-permute-start | bytes 1572872 | tf_op jit(solution)/shard_map/ppermute | solution.py:19
  102.1 8.1 %collective-permute-start.7 = (bf16[1,3,1,32,2048]{4,3,2,1,0:T(8,128)(2,1)S(1)}, bf16[1,3,1,32,2048]{4,3,2,1,0:T(8,128)(2,1)S(1)}, u32[]{:S(2)}, u32[]{:S(2)}) collective-permute-start(bf16[1,3,1,32,2048]{4,3,2,1,0:T(8,128)(2,1)S(1)} %pad_maximum_fusion.3), channel_id=1, source_target_pairs={{1,0},{2,1},{3,2},{4,3},{5,4},{6,5},{7,6},{8,7},{9,8},{10,9},{11,1... | collective-permute-start | bytes 1179656 | tf_op jit(solution)/shard_map/ppermute | solution.py:22
  115.8 8.4 %collective-permute-start.15 = (bf16[1,3,1,32,2048]{4,3,2,1,0:T(8,128)(2,1)}, bf16[1,3,1,32,2048]{4,3,2,1,0:T(8,128)(2,1)}, u32[]{:S(2)}, u32[]{:S(2)}) collective-permute-start(bf16[1,3,1,32,2048]{4,3,2,1,0:T(8,128)(2,1)} %pad_maximum_fusion.2), channel_id=1, source_target_pairs={{1,0},{2,1},{3,2},{4,3},{5,4},{6,5},{7,6},{8,7},{9,8},{10,9},{11,1... | collective-permute-start | bytes 1179656 | tf_op jit(solution)/shard_map/ppermute | solution.py:22
  126.7 1.9 collective-permute-start.14
  131.3 8.4 %collective-permute-start.3 = (bf16[1,3,1,64,2048]{4,3,2,1,0:T(8,128)(2,1)}, bf16[1,3,1,64,2048]{4,3,2,1,0:T(8,128)(2,1)}, u32[]{:S(2)}, u32[]{:S(2)}) collective-permute-start(bf16[1,3,1,64,2048]{4,3,2,1,0:T(8,128)(2,1)} %get-tuple-element.59), channel_id=1, source_target_pairs={{1,0},{2,1},{3,2},{4,3},{5,4},{6,5},{7,6},{8,7},{9,8},{10,9},{11,1... | collective-permute-start | bytes 2359304 | tf_op jit(solution)/shard_map/ppermute | solution.py:22
  139.8 1.9 collective-permute-start.2
  141.7 2.1 pad_maximum_fusion.1
  144.7 3.0 %gather_fusion = bf16[16,16,2048]{2,1,0:T(8,128)(2,1)} fusion(bf16[18,16,2048]{2,1,0:T(8,128)(2,1)} %bitcast.168, s32[1024]{0:T(1024)} %pad_clamp_fusion), kind=kCustom, calls=%fused_computation | custom fusion | bytes 2097216 | tf_op jit(solution)/shard_map/while/body/eval_jaxpr/gather | solution.py:96
  147.7 2.4 %copy.129 = bf16[32,8,16,128]{3,2,1,0:T(8,128)(2,1)} copy(bf16[32,8,16,128]{3,1,2,0:T(8,128)(2,1)} %bitcast.173) | data formatting | bytes 2097152
  150.1 2.7 %fusion.18 = (bf16[1,3,1,64,2048]{4,3,2,1,0:T(8,128)(2,1)}, bf16[1,3,1,64,2048]{4,3,2,1,0:T(8,128)(2,1)}) fusion(bf16[1,3,2,64,2048]{4,3,2,1,0:T(8,128)(2,1)} %constant_dynamic-update-slice_fusion), kind=kLoop, calls=%fused_computation.87 | loop fusion | bytes 3145728 | tf_op jit(solution)/shard_map/slice | solution.py:20
  152.8 8.4 %collective-permute-start.11 = (bf16[1,3,1,64,2048]{4,3,2,1,0:T(8,128)(2,1)}, bf16[1,3,1,64,2048]{4,3,2,1,0:T(8,128)(2,1)}, u32[]{:S(2)}, u32[]{:S(2)}) collective-permute-start(bf16[1,3,1,64,2048]{4,3,2,1,0:T(8,128)(2,1)} %get-tuple-element.57), channel_id=1, source_target_pairs={{1,0},{2,1},{3,2},{4,3},{5,4},{6,5},{7,6},{8,7},{9,8},{10,9},{11,1... | collective-permute-start | bytes 2359304 | tf_op jit(solution)/shard_map/ppermute | solution.py:22
  161.3 1.9 collective-permute-start.10
  163.2 2.3 pad_maximum_fusion
  165.6 3.0 %gather_fusion.1 = bf16[16,16,2048]{2,1,0:T(8,128)(2,1)} fusion(bf16[18,16,2048]{2,1,0:T(8,128)(2,1)} %bitcast.169, s32[1024]{0:T(1024)} %pad_clamp_fusion), kind=kCustom, calls=%fused_computation.1 | custom fusion | bytes 2097216 | tf_op jit(solution)/shard_map/while/body/eval_jaxpr/gather | solution.py:95
  170.0 39.1 %collective-permute-done.2 = bf16[1,3,1,64,2048]{4,3,2,1,0:T(8,128)(2,1)} collective-permute-done((bf16[1,3,1,64,2048]{4,3,2,1,0:T(8,128)(2,1)}, bf16[1,3,1,64,2048]{4,3,2,1,0:T(8,128)(2,1)}, u32[]{:S(2)}, u32[]{:S(2)}) %collective-permute-start.2) | collective-permute-done | bytes 786464 | tf_op jit(solution)/shard_map/ppermute | solution.py:19
  212.9 10.7 %collective-permute-done.10 = bf16[1,3,1,64,2048]{4,3,2,1,0:T(8,128)(2,1)} collective-permute-done((bf16[1,3,1,64,2048]{4,3,2,1,0:T(8,128)(2,1)}, bf16[1,3,1,64,2048]{4,3,2,1,0:T(8,128)(2,1)}, u32[]{:S(2)}, u32[]{:S(2)}) %collective-permute-start.10) | collective-permute-done | bytes 786464 | tf_op jit(solution)/shard_map/ppermute | solution.py:19
  223.6 2.2 maximum_bitcast_fusion
  229.6 2.3 bitcast_reduce_fusion
  236.4 2.2 fusion.4
  (118 shorter events, 44.9 us)
Async XLA Ops:
  0.0 99.7 %copy-start.3 = (bf16[2,16,2048]{2,1,0:T(8,128)(2,1)S(1)}, bf16[2,16,2048]{2,1,0:T(8,128)(2,1)}, u32[]{:S(2)}) copy-start(bf16[2,16,2048]{2,1,0:T(8,128)(2,1)} %param.12) | copy-start | bytes 393220
  0.0 88.1 %copy-start.4 = (bf16[2,16,2048]{2,1,0:T(8,128)(2,1)S(1)}, bf16[2,16,2048]{2,1,0:T(8,128)(2,1)}, u32[]{:S(2)}) copy-start(bf16[2,16,2048]{2,1,0:T(8,128)(2,1)} %param.11) | copy-start | bytes 393220
  0.0 110.9 %collective-permute-start = (bf16[1,1,2,64,2048]{4,3,2,1,0:T(8,128)(2,1)}, bf16[1,1,2,64,2048]{4,3,2,1,0:T(8,128)(2,1)S(1)}, u32[]{:S(2)}, u32[]{:S(2)}) collective-permute-start(bf16[1,1,2,64,2048]{4,3,2,1,0:T(8,128)(2,1)} %param.10), channel_id=1, source_target_pairs={{0,16},{16,32},{32,48},{48,64},{64,80},{80,96},{96,112},{112,128},... | collective-permute-start | bytes 1572872 | tf_op jit(solution)/shard_map/ppermute | solution.py:19
  3.6 112.2 %collective-permute-start.1 = (bf16[1,1,2,64,2048]{4,3,2,1,0:T(8,128)(2,1)}, bf16[1,1,2,64,2048]{4,3,2,1,0:T(8,128)(2,1)}, u32[]{:S(2)}, u32[]{:S(2)}) collective-permute-start(bf16[1,1,2,64,2048]{4,3,2,1,0:T(8,128)(2,1)} %param.10), channel_id=1, source_target_pairs={{16,0},{32,16},{48,32},{64,48},{80,64},{96,80},{112,96},{128,112},... | collective-permute-start | bytes 1572872 | tf_op jit(solution)/shard_map/ppermute | solution.py:22
  4.9 83.1 %collective-permute-start.5 = (bf16[1,1,1,32,2048]{4,3,2,1,0:T(8,128)(2,1)}, bf16[1,1,1,32,2048]{4,3,2,1,0:T(8,128)(2,1)}, u32[]{:S(2)}, u32[]{:S(2)}) collective-permute-start(bf16[1,1,1,32,2048]{4,3,2,1,0:T(8,128)(2,1)} %bitcast.214), channel_id=1, source_target_pairs={{16,0},{32,16},{48,32},{64,48},{80,64},{96,80},{112,96},{128,112},... | collective-permute-start | bytes 393224 | tf_op jit(solution)/shard_map/ppermute | solution.py:22
  6.2 89.8 %collective-permute-start.4 = (bf16[1,1,1,32,2048]{4,3,2,1,0:T(8,128)(2,1)}, bf16[1,1,1,32,2048]{4,3,2,1,0:T(8,128)(2,1)}, u32[]{:S(2)}, u32[]{:S(2)}) collective-permute-start(bf16[1,1,1,32,2048]{4,3,2,1,0:T(8,128)(2,1)} %bitcast.215), channel_id=1, source_target_pairs={{0,16},{16,32},{32,48},{48,64},{64,80},{80,96},{96,112},{112,128},... | collective-permute-start | bytes 393224 | tf_op jit(solution)/shard_map/ppermute | solution.py:19
  12.1 88.7 %collective-permute-start.13 = (bf16[1,1,1,32,2048]{4,3,2,1,0:T(8,128)(2,1)}, bf16[1,1,1,32,2048]{4,3,2,1,0:T(8,128)(2,1)S(1)}, u32[]{:S(2)}, u32[]{:S(2)}) collective-permute-start(bf16[1,1,1,32,2048]{4,3,2,1,0:T(8,128)(2,1)} %bitcast.218), channel_id=1, source_target_pairs={{16,0},{32,16},{48,32},{64,48},{80,64},{96,80},{112,96},{128,112},... | collective-permute-start | bytes 393224 | tf_op jit(solution)/shard_map/ppermute | solution.py:22
  88.1 14.0 %collective-permute-start.12 = (bf16[1,1,1,32,2048]{4,3,2,1,0:T(8,128)(2,1)S(1)}, bf16[1,1,1,32,2048]{4,3,2,1,0:T(8,128)(2,1)S(1)}, u32[]{:S(2)}, u32[]{:S(2)}) collective-permute-start(bf16[1,1,1,32,2048]{4,3,2,1,0:T(8,128)(2,1)S(1)} %bitcast.219), channel_id=1, source_target_pairs={{0,16},{16,32},{32,48},{48,64},{64,80},{80,96},{96,112},{112,128},... | collective-permute-start | bytes 393224 | tf_op jit(solution)/shard_map/ppermute | solution.py:19
  96.1 30.6 %collective-permute-start.8 = (bf16[1,1,2,64,2048]{4,3,2,1,0:T(8,128)(2,1)}, bf16[1,1,2,64,2048]{4,3,2,1,0:T(8,128)(2,1)S(1)}, u32[]{:S(2)}, u32[]{:S(2)}) collective-permute-start(bf16[1,1,2,64,2048]{4,3,2,1,0:T(8,128)(2,1)} %param.9), channel_id=1, source_target_pairs={{0,16},{16,32},{32,48},{48,64},{64,80},{80,96},{96,112},{112,128},... | collective-permute-start | bytes 1572872 | tf_op jit(solution)/shard_map/ppermute | solution.py:19
  100.8 43.1 %collective-permute-start.9 = (bf16[1,1,2,64,2048]{4,3,2,1,0:T(8,128)(2,1)}, bf16[1,1,2,64,2048]{4,3,2,1,0:T(8,128)(2,1)S(1)}, u32[]{:S(2)}, u32[]{:S(2)}) collective-permute-start(bf16[1,1,2,64,2048]{4,3,2,1,0:T(8,128)(2,1)} %param.9), channel_id=1, source_target_pairs={{16,0},{32,16},{48,32},{64,48},{80,64},{96,80},{112,96},{128,112},... | collective-permute-start | bytes 1572872 | tf_op jit(solution)/shard_map/ppermute | solution.py:22
  102.1 13.8 %copy-start.5 = (bf16[1,1,1,32,2048]{4,3,2,1,0:T(8,128)(2,1)}, bf16[1,1,1,32,2048]{4,3,2,1,0:T(8,128)(2,1)S(1)}, u32[]{:S(2)}) copy-start(bf16[1,1,1,32,2048]{4,3,2,1,0:T(8,128)(2,1)S(1)} %collective-permute-done.12) | copy-start | bytes 393220
  102.1 29.2 %collective-permute-start.7 = (bf16[1,3,1,32,2048]{4,3,2,1,0:T(8,128)(2,1)S(1)}, bf16[1,3,1,32,2048]{4,3,2,1,0:T(8,128)(2,1)S(1)}, u32[]{:S(2)}, u32[]{:S(2)}) collective-permute-start(bf16[1,3,1,32,2048]{4,3,2,1,0:T(8,128)(2,1)S(1)} %pad_maximum_fusion.3), channel_id=1, source_target_pairs={{1,0},{2,1},{3,2},{4,3},{5,4},{6,5},{7,6},{8,7},{9,8},{10,9},{11,1... | collective-permute-start | bytes 1179656 | tf_op jit(solution)/shard_map/ppermute | solution.py:22
  110.9 0.8 copy-start.2
  111.7 28.0 %collective-permute-start.6 = (bf16[1,3,1,32,2048]{4,3,2,1,0:T(8,128)(2,1)S(1)}, bf16[1,3,1,32,2048]{4,3,2,1,0:T(8,128)(2,1)S(1)}, u32[]{:S(2)}, u32[]{:S(2)}) collective-permute-start(bf16[1,3,1,32,2048]{4,3,2,1,0:T(8,128)(2,1)S(1)} %pad_maximum_fusion.3), channel_id=1, source_target_pairs={{0,1},{1,2},{2,3},{3,4},{4,5},{5,6},{6,7},{7,8},{8,9},{9,10},{10,1... | collective-permute-start | bytes 1179656 | tf_op jit(solution)/shard_map/ppermute | solution.py:19
  115.8 45.4 %collective-permute-start.15 = (bf16[1,3,1,32,2048]{4,3,2,1,0:T(8,128)(2,1)}, bf16[1,3,1,32,2048]{4,3,2,1,0:T(8,128)(2,1)}, u32[]{:S(2)}, u32[]{:S(2)}) collective-permute-start(bf16[1,3,1,32,2048]{4,3,2,1,0:T(8,128)(2,1)} %pad_maximum_fusion.2), channel_id=1, source_target_pairs={{1,0},{2,1},{3,2},{4,3},{5,4},{6,5},{7,6},{8,7},{9,8},{10,9},{11,1... | collective-permute-start | bytes 1179656 | tf_op jit(solution)/shard_map/ppermute | solution.py:22
  126.7 36.5 %collective-permute-start.14 = (bf16[1,3,1,32,2048]{4,3,2,1,0:T(8,128)(2,1)}, bf16[1,3,1,32,2048]{4,3,2,1,0:T(8,128)(2,1)}, u32[]{:S(2)}, u32[]{:S(2)}) collective-permute-start(bf16[1,3,1,32,2048]{4,3,2,1,0:T(8,128)(2,1)} %pad_maximum_fusion.2), channel_id=1, source_target_pairs={{0,1},{1,2},{2,3},{3,4},{4,5},{5,6},{6,7},{7,8},{8,9},{9,10},{10,1... | collective-permute-start | bytes 1179656 | tf_op jit(solution)/shard_map/ppermute | solution.py:19
  131.3 38.7 %collective-permute-start.3 = (bf16[1,3,1,64,2048]{4,3,2,1,0:T(8,128)(2,1)}, bf16[1,3,1,64,2048]{4,3,2,1,0:T(8,128)(2,1)}, u32[]{:S(2)}, u32[]{:S(2)}) collective-permute-start(bf16[1,3,1,64,2048]{4,3,2,1,0:T(8,128)(2,1)} %get-tuple-element.59), channel_id=1, source_target_pairs={{1,0},{2,1},{3,2},{4,3},{5,4},{6,5},{7,6},{8,7},{9,8},{10,9},{11,1... | collective-permute-start | bytes 2359304 | tf_op jit(solution)/shard_map/ppermute | solution.py:22
  139.8 69.3 %collective-permute-start.2 = (bf16[1,3,1,64,2048]{4,3,2,1,0:T(8,128)(2,1)}, bf16[1,3,1,64,2048]{4,3,2,1,0:T(8,128)(2,1)}, u32[]{:S(2)}, u32[]{:S(2)}) collective-permute-start(bf16[1,3,1,64,2048]{4,3,2,1,0:T(8,128)(2,1)} %get-tuple-element.58), channel_id=1, source_target_pairs={{0,1},{1,2},{2,3},{3,4},{4,5},{5,6},{6,7},{7,8},{8,9},{9,10},{10,1... | collective-permute-start | bytes 2359304 | tf_op jit(solution)/shard_map/ppermute | solution.py:19
  152.8 60.1 %collective-permute-start.11 = (bf16[1,3,1,64,2048]{4,3,2,1,0:T(8,128)(2,1)}, bf16[1,3,1,64,2048]{4,3,2,1,0:T(8,128)(2,1)}, u32[]{:S(2)}, u32[]{:S(2)}) collective-permute-start(bf16[1,3,1,64,2048]{4,3,2,1,0:T(8,128)(2,1)} %get-tuple-element.57), channel_id=1, source_target_pairs={{1,0},{2,1},{3,2},{4,3},{5,4},{6,5},{7,6},{8,7},{9,8},{10,9},{11,1... | collective-permute-start | bytes 2359304 | tf_op jit(solution)/shard_map/ppermute | solution.py:22
  161.3 62.3 %collective-permute-start.10 = (bf16[1,3,1,64,2048]{4,3,2,1,0:T(8,128)(2,1)}, bf16[1,3,1,64,2048]{4,3,2,1,0:T(8,128)(2,1)}, u32[]{:S(2)}, u32[]{:S(2)}) collective-permute-start(bf16[1,3,1,64,2048]{4,3,2,1,0:T(8,128)(2,1)} %get-tuple-element.56), channel_id=1, source_target_pairs={{0,1},{1,2},{2,3},{3,4},{4,5},{5,6},{6,7},{7,8},{8,9},{9,10},{10,1... | collective-permute-start | bytes 2359304 | tf_op jit(solution)/shard_map/ppermute | solution.py:19
  227.7 1.9 copy-start.6
  233.9 2.2 copy-start
  236.4 2.2 copy-start.1
where the time goes:
time: 242 us; the launch traced here: 241 us
  starting transfers between devices  67.3 us (28%)
  blocking collectives  63 us (26%)
  waiting for transfers between devices  49.9 us (21%)
  local copies, waits for them, and re-layouts  38.1 us (16%)
  other arithmetic  16.2 us (7%)
  matrix products  5.78 us (2%)
    ppermute x8, waiting for transfers between devices, extended(): lax.ppermute(lax.slice_in_dim(block, block.shape[dim] - width, None, axis...  49.9 us
    ppermute x8, starting transfers between devices, extended(): lax.ppermute(lax.slice_in_dim(block, 0, width, axis=dim), axis, backward)  38.5 us
    all_gather x1, blocking collectives, body(): lax.all_gather(top_keys, 'col', axis=1, tiled=True)  35.2 us
    ppermute x8, starting transfers between devices, extended(): lax.ppermute(lax.slice_in_dim(block, block.shape[dim] - width, None, axis...  28.8 us
    all_gather x1, blocking collectives, body(): lax.all_gather(top_values, 'col', axis=1, tiled=True)  27.7 us
    unnamed x57, local copies, waits for them, and re-layouts  15.8 us
    concatenate x4, other arithmetic, extended(): block = jnp.concatenate([low, block, high], axis=dim)  6.27 us
  transfers between devices with their start and end apart: 16, of which 2 were waited for; matrix products, arithmetic and copies ran while one was open for 18% of the time, Pallas kernels for 0%

commit v1 on v0

v1 whole, which is shorter than its diff:
```python
import math

import jax
import jax.numpy as jnp
from jax import lax
from jax.experimental import pallas as pl
from jax.experimental.pallas import tpu as pltpu
from jax.sharding import PartitionSpec as P

HEADS = 16
NEG_FILL = -1e30
AXES = ("row", "col")
LANES = 128


def pairs(rows, cols, target):
    out = []
    for row in range(rows):
        for col in range(cols):
            there = target(row, col)
            if 0 <= there[0] < rows and 0 <= there[1] < cols:
                out.append((row * cols + col, there[0] * cols + there[1]))
    return out


def send(block, links):
    return lax.ppermute(block, AXES, links)


def copy_all(copies):
    for copy in copies:
        copy.start()
    for copy in copies:
        copy.wait()


def pack_kernel(side, keys, values, pool_keys, pool_values, top_keys, top_values, near, far, top, sems):
    tokens = keys.shape[1]
    pool = pool_keys.shape[0]
    copies = []
    for out, block in ((far, side[0]), (near, 1 - side[0])):
        place = 0
        for source, count in (
            (keys.at[block], tokens),
            (pool_keys, pool),
            (values.at[block], tokens),
            (pool_values, pool),
        ):
            copies.append((source, out.at[pl.ds(place, count)]))
            place += count
    copies.append((top_keys, top.at[0]))
    copies.append((top_values, top.at[1]))
    copy_all([pltpu.make_async_copy(a, b, sems.at[i]) for i, (a, b) in enumerate(copies)])


def pack(side, keys, values, pool_keys, pool_values, top_keys, top_values):
    tokens, width = keys.shape[1:]
    pool = pool_keys.shape[0]
    message = jax.ShapeDtypeStruct((2 * (tokens + pool), width), keys.dtype)
    share = jax.ShapeDtypeStruct((2,) + top_keys.shape, keys.dtype)
    return pl.pallas_call(
        pack_kernel,
        out_shape=(message, message, share),
        in_specs=[pl.BlockSpec(memory_space=pltpu.SMEM)] + [pl.BlockSpec(memory_space=pl.ANY)] * 6,
        out_specs=[pl.BlockSpec(memory_space=pltpu.VMEM)] * 3,
        scratch_shapes=[pltpu.SemaphoreType.DMA((10,))],
        name="pack",
    )(side, keys, values, pool_keys, pool_values, top_keys, top_values)


def split_in_three(value):
    high = value.astype(jnp.bfloat16)
    rest = value - high.astype(jnp.float32)
    middle = rest.astype(jnp.bfloat16)
    low = (rest - middle.astype(jnp.float32)).astype(jnp.bfloat16)
    return high, middle, low


def attend_kernel(
    q_own, q_up, q_down, keys, values, pool_keys, pool_values, near, far, top_a, top_b, bias,
    out_own, out_up, out_down,
    qs, ks, vs, tks, tvs, sems,
):
    own = keys.shape[0]
    pool = pool_keys.shape[0]
    edge = near.shape[0] // 2
    half_top = top_a.shape[1]
    rows = q_own.shape[0]
    width = q_own.shape[1]
    used = own + edge + pool + edge
    total = ks.shape[0]
    group = rows // 2
    copies = []
    for i, ref in enumerate((q_own, q_up, q_down)):
        copies.append((ref, qs.at[pl.ds(i * rows, rows)]))
    for part, scratch, mine, mine_pool in ((0, ks, keys, pool_keys), (1, vs, values, pool_values)):
        place = 0
        for ref, count in (
            (mine, own),
            (near.at[pl.ds(part * edge, edge)], edge),
            (mine_pool, pool),
            (far.at[pl.ds(part * edge, edge)], edge),
        ):
            copies.append((ref, scratch.at[pl.ds(place, count)]))
            place += count
    for part, scratch in ((0, tks), (1, tvs)):
        copies.append((top_a.at[part], scratch.at[pl.ds(0, half_top)]))
        copies.append((top_b.at[part], scratch.at[pl.ds(half_top, half_top)]))
    started = [pltpu.make_async_copy(a, b, sems.at[i]) for i, (a, b) in enumerate(copies)]
    for copy in started:
        copy.start()
    ks[pl.ds(used, total - used), :] = jnp.zeros((total - used, width), ks.dtype)
    vs[pl.ds(used, total - used), :] = jnp.zeros((total - used, width), vs.dtype)
    for copy in started:
        copy.wait()
    scale = 1.0 / math.sqrt(width // HEADS)
    lane = lax.broadcasted_iota(jnp.int32, (rows, LANES), 1)
    logs = [jnp.zeros((rows, LANES), jnp.float32) for _ in range(3)]
    ones = jnp.ones((total, LANES), jnp.bfloat16)
    ones_top = jnp.ones((2 * half_top, LANES), jnp.bfloat16)
    nt = (((1,), (1,)), ((), ()))
    for head in range(HEADS):
        part = pl.ds(head * LANES, LANES)
        query = qs[:, part]
        scores = lax.dot_general(query, ks[:, part], nt, preferred_element_type=jnp.float32) * scale
        top_scores = (
            lax.dot_general(query[:rows], tks[:, part], nt, preferred_element_type=jnp.float32) * scale
        )
        weights = []
        peaks = []
        for i in range(6):
            piece = scores[i * group : (i + 1) * group] + bias[pl.ds(i, 1), :]
            peak = jnp.max(piece, axis=1, keepdims=True)
            if i < 2:
                peak = jnp.maximum(
                    peak, jnp.max(top_scores[i * group : (i + 1) * group], axis=1, keepdims=True)
                )
            peaks.append(peak)
            weights.append(jnp.exp(piece - peak).astype(jnp.bfloat16))
        value = jnp.concatenate([vs[:, part], ones], axis=1)
        summed = jnp.dot(
            jnp.concatenate(weights, axis=0), value, preferred_element_type=jnp.float32
        )
        top_weights = jnp.exp(top_scores - jnp.concatenate(peaks[:2], axis=0)).astype(jnp.bfloat16)
        top_value = jnp.concatenate([tvs[:, part], ones_top], axis=1)
        top_summed = jnp.dot(top_weights, top_value, preferred_element_type=jnp.float32)
        for i, out in enumerate((out_own, out_up, out_down)):
            piece = summed[i * rows : (i + 1) * rows]
            if i == 0:
                piece = piece + top_summed
            norm = piece[:, LANES:]
            out[:, part] = (piece[:, :LANES] / norm).astype(out.dtype)
            log = jnp.concatenate(peaks[2 * i : 2 * i + 2], axis=0) + jnp.log(norm)
            logs[i] = jnp.where(lane == head, log, logs[i])
    tail = pl.ds(width, LANES)
    out_own[:, tail] = logs[0]
    for log, out in ((logs[1], out_up), (logs[2], out_down)):
        high, middle, low = (x.astype(jnp.float32) for x in split_in_three(log))
        out[:, tail] = (
            high + pltpu.roll(middle, HEADS, 1) + pltpu.roll(low, 2 * HEADS, 1)
        ).astype(out.dtype)


def attend(q_own, q_up, q_down, keys, values, pool_keys, pool_values, near, far, top_a, top_b, bias):
    rows, width = q_own.shape
    total = bias.shape[1]
    top = 2 * top_a.shape[1]
    message = (rows, width + LANES)
    bf16 = jnp.bfloat16
    return pl.pallas_call(
        attend_kernel,
        out_shape=(
            jax.ShapeDtypeStruct(message, jnp.float32),
            jax.ShapeDtypeStruct(message, bf16),
            jax.ShapeDtypeStruct(message, bf16),
        ),
        in_specs=[pl.BlockSpec(memory_space=pl.ANY)] * 11 + [pl.BlockSpec(memory_space=pltpu.VMEM)],
        out_specs=[pl.BlockSpec(memory_space=pltpu.VMEM)] * 3,
        scratch_shapes=[
            pltpu.VMEM((3 * rows, width), bf16),
            pltpu.VMEM((total, width), bf16),
            pltpu.VMEM((total, width), bf16),
            pltpu.VMEM((top, width), bf16),
            pltpu.VMEM((top, width), bf16),
            pltpu.SemaphoreType.DMA((15,)),
        ],
        cost_estimate=pl.CostEstimate(
            flops=4 * 3 * rows * total * width, bytes_accessed=8 << 20, transcendentals=3 * rows * total * HEADS
        ),
        name="attend",
    )(q_own, q_up, q_down, keys, values, pool_keys, pool_values, near, far, top_a, top_b, bias)


def merge_kernel(edges, own, above, below, out):
    rows, width = out.shape
    tail = pl.ds(width, LANES)
    logs = [own[:, tail]]
    for i, ref in enumerate((above, below)):
        coded = ref[:, tail].astype(jnp.float32)
        log = coded + pltpu.roll(coded, LANES - HEADS, 1) + pltpu.roll(coded, LANES - 2 * HEADS, 1)
        logs.append(jnp.where(edges[i] > 0, log, NEG_FILL))
    peak = jnp.maximum(jnp.maximum(logs[0], logs[1]), logs[2])
    shares = [jnp.exp(log - peak) for log in logs]
    norm = shares[0] + shares[1] + shares[2]
    shares = [share / norm for share in shares]
    for head in range(HEADS):
        part = pl.ds(head * LANES, LANES)
        result = own[:, part] * shares[0][:, head : head + 1]
        result = result + above[:, part].astype(jnp.float32) * shares[1][:, head : head + 1]
        result = result + below[:, part].astype(jnp.float32) * shares[2][:, head : head + 1]
        out[:, part] = result.astype(out.dtype)


def merge(edges, own, above, below, width):
    return pl.pallas_call(
        merge_kernel,
        out_shape=jax.ShapeDtypeStruct((own.shape[0], width), jnp.bfloat16),
        in_specs=[pl.BlockSpec(memory_space=pltpu.SMEM)] + [pl.BlockSpec(memory_space=pltpu.VMEM)] * 3,
        out_specs=pl.BlockSpec(memory_space=pltpu.VMEM),
        name="merge",
    )(edges, own, above, below)


def body(queries, keys, values, pool_keys, pool_values, top_keys, top_values, coarse_ids):
    _, _, blocks, tokens, width = queries.shape
    pool_blocks, pool_tokens, _ = pool_keys.shape
    rows = lax.axis_size("row")
    cols = lax.axis_size("col")
    row = lax.axis_index("row")
    col = lax.axis_index("col")
    side = col % 2
    pool = pool_blocks * pool_tokens
    own = blocks * tokens

    up = pairs(rows, cols, lambda r, q: (r - 1, q))
    down = pairs(rows, cols, lambda r, q: (r + 1, q))
    partner = pairs(rows, cols, lambda r, q: (r, q ^ 1))
    across = pairs(rows, cols, lambda r, q: (r, q + 1 if q % 2 else q - 1))
    line = rows // 4
    halves = pairs(rows, cols, lambda r, q: ((3 - r // line) * line + r % line, q ^ 2))
    step_one = pairs(rows, cols, lambda r, q: (r, q ^ 4))
    step_two = pairs(rows, cols, lambda r, q: (r, q ^ 8))

    query = queries.reshape(own, width)
    pk = pool_keys.reshape(pool, width)
    pv = pool_values.reshape(pool, width)
    near, far, top = pack(
        side.reshape(1),
        keys.reshape(blocks, tokens, width),
        values.reshape(blocks, tokens, width),
        pk,
        pv,
        top_keys[0],
        top_values[0],
    )
    far = send(far, across)
    q_up = send(query, down)
    q_down = send(query, up)
    near = send(near, partner)
    for links in (halves, step_one, step_two):
        top = jnp.concatenate([top, send(top, links)], axis=1)
    top_other = send(top, partner)
    ids = coarse_ids.reshape(blocks, -1)
    ids_up = send(ids, down)
    ids_down = send(ids, up)

    other = col + 1 - 2 * side
    beyond = col - 1 + 2 * side
    exists = (beyond >= 0) & (beyond < cols)
    group_block = jnp.tile(jnp.arange(blocks, dtype=jnp.int32), 3)
    all_ids = jnp.concatenate([ids, ids_up, ids_down], axis=0)

    def pool_bias(holder):
        first = (row * cols + holder) * pool_blocks
        block = first + jnp.arange(pool, dtype=jnp.int32) // pool_tokens
        return (all_ids[:, :, None] == block[None, None, :]).any(axis=1)

    def fine(valid):
        return jnp.broadcast_to(valid[:, None], (3 * blocks, tokens))

    full = jnp.ones((3 * blocks, own), bool)
    valid = jnp.concatenate(
        [
            full,
            fine(group_block == 1 - side),
            pool_bias(other),
            pool_bias(col),
            fine((group_block == side) & exists),
            pool_bias(beyond) & exists,
        ],
        axis=1,
    )
    gap = -valid.shape[1] % LANES
    valid = jnp.pad(valid, ((0, 0), (0, gap)))
    bias = jnp.where(valid, 0.0, NEG_FILL).astype(jnp.float32)

    mine, to_up, to_down = attend(
        query, q_up, q_down, keys.reshape(own, width), values.reshape(own, width), pk, pv,
        near, far, top, top_other, bias,
    )
    below = send(to_up, up)
    above = send(to_down, down)
    edges = jnp.stack([row > 0, row < rows - 1]).astype(jnp.int32)
    return merge(edges, mine, above, below, width).reshape(queries.shape)


def solution(mesh):
    placed = (
        P(None, "row", "col", None, None),
        P(None, "row", "col", None, None),
        P(None, "row", "col", None, None),
        P(("row", "col"), None, None),
        P(("row", "col"), None, None),
        P(None, "col", None),
        P(None, "col", None),
        P(None, "row", "col", None),
    )
    return jax.shard_map(
        body,
        mesh=mesh,
        in_specs=placed,
        out_specs=P(None, "row", "col", None, None),
        check_vma=False,
    )
```

time: 242 us -> 138 us (0.57)
  the two profiles are of different devices: /device:TPU:6 before, /device:TPU:124 now
where the time goes in v1:
time: 138 us
  starting transfers between devices  58.8 us (43%)
  waiting for transfers between devices  56.2 us (41%)
  Pallas kernels  16.4 us (12%)
  other arithmetic  3.13 us (2%)
  local copies, waits for them, and re-layouts  3.01 us (2%)
    ppermute x12, starting transfers between devices, send(): return lax.ppermute(block, AXES, links)  58.8 us
    ppermute x12, waiting for transfers between devices, send(): return lax.ppermute(block, AXES, links)  56.2 us
    pallas_call x1, Pallas kernels, attend(): pl.pallas_call(attend_kernel, out_shape=(jax.ShapeDtypeStruct(message, jn...  10.4 us
    pallas_call x1, Pallas kernels, merge(): pl.pallas_call(merge_kernel, out_shape=jax.ShapeDtypeStruct((own.shape[0]...  3.39 us
  transfers between devices with their start and end apart: 12, of which 6 were waited for; matrix products, arithmetic and copies ran while one was open for 3% of the time, Pallas kernels for 2%

profile of v1, /device:TPU:124, one launch (start us, length us, event | category | flops | bytes accessed | tf_op | source)
XLA Modules:
  0.0 137.8 jit_solution(15692365738964145272)
XLA Ops:
  0.0 3.2 %collective-permute-start.9 = (s32[2,8]{1,0:T(2,128)}, s32[2,8]{1,0:T(2,128)S(1)}, u32[]{:S(2)}, u32[]{:S(2)}) collective-permute-start(s32[2,8]{1,0:T(2,128)} %bitcast.27), channel_id=1, source_target_pairs={{16,0},{17,1},{18,2},{19,3},{20,4},{21,5},{22,6},{23,7},{24,8},{25... | collective-permute-start | bytes 200 | tf_op jit(solution)/shard_map/ppermute | solution.py:27
  3.3 4.7 %collective-permute-start.8 = (s32[2,8]{1,0:T(2,128)}, s32[2,8]{1,0:T(2,128)S(1)}, u32[]{:S(2)}, u32[]{:S(2)}) collective-permute-start(s32[2,8]{1,0:T(2,128)} %bitcast.28), channel_id=1, source_target_pairs={{0,16},{1,17},{2,18},{3,19},{4,20},{5,21},{6,22},{7,23},{8,24},{9,... | collective-permute-start | bytes 200 | tf_op jit(solution)/shard_map/ppermute | solution.py:27
  8.0 1.9 %collective-permute-start.1 = (bf16[128,2048]{1,0:T(8,128)(2,1)}, bf16[128,2048]{1,0:T(8,128)(2,1)S(1)}, u32[]{:S(2)}, u32[]{:S(2)}) collective-permute-start(bf16[128,2048]{1,0:T(8,128)(2,1)} %bitcast.18), channel_id=1, source_target_pairs={{16,0},{17,1},{18,2},{19,3},{20,4},{21,5},{22,6},{23,7},{24,8},{25... | collective-permute-start | bytes 1572872 | tf_op jit(solution)/shard_map/ppermute | solution.py:27
  9.9 2.6 %pack.1 = (bf16[192,2048]{1,0:T(8,128)(2,1)}, bf16[192,2048]{1,0:T(8,128)(2,1)}, bf16[2,8,2048]{2,1,0:T(8,128)(2,1)}) custom-call(s32[1]{0:T(128)} %bitcast.7.side, bf16[2,64,2048]{2,1,0:T(8,128)(2,1)} %bitcast.14, bf16[2,64,2048]{2,1,0:T(8,128)(2,1)} %bitcast.16, bf16[32,2048]{1,0:T(8,128)(2,1)} %bitcast.21, bf16[32,2048]{1,0:T(8,128)(2,1)} %bitcast.23, ...), custom_call_target="tpu_custom_call" | custom-call | tf_op jit(solution)/shard_map/pack/pallas_call | solution.py:61
  12.6 10.2 %collective-permute-start.4 = (bf16[2,8,2048]{2,1,0:T(8,128)(2,1)}, bf16[2,8,2048]{2,1,0:T(8,128)(2,1)S(1)}, u32[]{:S(2)}, u32[]{:S(2)}) collective-permute-start(bf16[2,8,2048]{2,1,0:T(8,128)(2,1)} %get-tuple-element.13), channel_id=1, source_target_pairs={{0,386},{1,387},{2,384},{3,385},{4,390},{5,391},{6,388},{7,389},{8... | collective-permute-start | bytes 196616 | tf_op jit(solution)/shard_map/ppermute | solution.py:27
  22.7 1.9 %collective-permute-start.2 = (bf16[192,2048]{1,0:T(8,128)(2,1)}, bf16[192,2048]{1,0:T(8,128)(2,1)S(1)}, u32[]{:S(2)}, u32[]{:S(2)}) collective-permute-start(bf16[192,2048]{1,0:T(8,128)(2,1)} %get-tuple-element.11), channel_id=1, source_target_pairs={{0,1},{1,0},{2,3},{3,2},{4,5},{5,4},{6,7},{7,6},{8,9},{9,8},{10,11... | collective-permute-start | bytes 2359304 | tf_op jit(solution)/shard_map/ppermute | solution.py:27
  25.5 0.9 pad_maximum_fusion.1
  26.4 3.1 %collective-permute-start.5 = (bf16[2,16,2048]{2,1,0:T(8,128)(2,1)S(1)}, bf16[2,16,2048]{2,1,0:T(8,128)(2,1)S(1)}, u32[]{:S(2)}, u32[]{:S(2)}) collective-permute-start(bf16[2,16,2048]{2,1,0:T(8,128)(2,1)S(1)} %pad_maximum_fusion.1), channel_id=1, source_target_pairs={{0,4},{1,5},{2,6},{3,7},{4,0},{5,1},{6,2},{7,3},{8,12},{9,13},{10,... | collective-permute-start | bytes 393224 | tf_op jit(solution)/shard_map/ppermute | solution.py:27
  29.7 4.5 %collective-permute-done.5 = bf16[2,16,2048]{2,1,0:T(8,128)(2,1)S(1)} collective-permute-done((bf16[2,16,2048]{2,1,0:T(8,128)(2,1)S(1)}, bf16[2,16,2048]{2,1,0:T(8,128)(2,1)S(1)}, u32[]{:S(2)}, u32[]{:S(2)}) %collective-permute-start.5) | collective-permute-done | bytes 131104 | tf_op jit(solution)/shard_map/ppermute | solution.py:27
  34.2 0.9 pad_maximum_fusion
  35.0 2.4 %collective-permute-start.6 = (bf16[2,32,2048]{2,1,0:T(8,128)(2,1)S(1)}, bf16[2,32,2048]{2,1,0:T(8,128)(2,1)S(1)}, u32[]{:S(2)}, u32[]{:S(2)}) collective-permute-start(bf16[2,32,2048]{2,1,0:T(8,128)(2,1)S(1)} %pad_maximum_fusion), channel_id=1, source_target_pairs={{0,8},{1,9},{2,10},{3,11},{4,12},{5,13},{6,14},{7,15},{8,0},{9,1},... | collective-permute-start | bytes 786440 | tf_op jit(solution)/shard_map/ppermute | solution.py:27
  37.5 8.8 %collective-permute-done.6 = bf16[2,32,2048]{2,1,0:T(8,128)(2,1)S(1)} collective-permute-done((bf16[2,32,2048]{2,1,0:T(8,128)(2,1)S(1)}, bf16[2,32,2048]{2,1,0:T(8,128)(2,1)S(1)}, u32[]{:S(2)}, u32[]{:S(2)}) %collective-permute-start.6) | collective-permute-done | bytes 262176 | tf_op jit(solution)/shard_map/ppermute | solution.py:27
  46.3 6.3 %collective-permute-start.3 = (bf16[192,2048]{1,0:T(8,128)(2,1)}, bf16[192,2048]{1,0:T(8,128)(2,1)S(1)}, u32[]{:S(2)}, u32[]{:S(2)}) collective-permute-start(bf16[192,2048]{1,0:T(8,128)(2,1)} %get-tuple-element.12), channel_id=1, source_target_pairs={{1,2},{2,1},{3,4},{4,3},{5,6},{6,5},{7,8},{8,7},{9,10},{10,9},{11,... | collective-permute-start | bytes 2359304 | tf_op jit(solution)/shard_map/ppermute | solution.py:27
  52.6 1.9 %collective-permute-start = (bf16[128,2048]{1,0:T(8,128)(2,1)S(1)}, bf16[128,2048]{1,0:T(8,128)(2,1)}, u32[]{:S(2)}, u32[]{:S(2)}) collective-permute-start(bf16[128,2048]{1,0:T(8,128)(2,1)S(1)} %bitcast.20), channel_id=1, source_target_pairs={{0,16},{1,17},{2,18},{3,19},{4,20},{5,21},{6,22},{7,23},{8,24},{9,... | collective-permute-start | bytes 1572872 | tf_op jit(solution)/shard_map/ppermute | solution.py:27
  54.6 4.1 %collective-permute-start.7 = (bf16[2,64,2048]{2,1,0:T(8,128)(2,1)S(1)}, bf16[2,64,2048]{2,1,0:T(8,128)(2,1)}, u32[]{:S(2)}, u32[]{:S(2)}) collective-permute-start(bf16[2,64,2048]{2,1,0:T(8,128)(2,1)S(1)} %constant_dynamic-update-slice_fusion.top_a), channel_id=1, source_target_pairs={{0,1},{1,0},{2,3},{3,2},{4,5},{5,4},{6,7},{7,6},{8,9},{9,8},{10,11... | collective-permute-start | bytes 1572872 | tf_op jit(solution)/shard_map/ppermute | solution.py:27
  59.7 8.4 %collective-permute-done.q_up = bf16[128,2048]{1,0:T(8,128)(2,1)} collective-permute-done((bf16[128,2048]{1,0:T(8,128)(2,1)S(1)}, bf16[128,2048]{1,0:T(8,128)(2,1)}, u32[]{:S(2)}, u32[]{:S(2)}) %collective-permute-start) | collective-permute-done | bytes 524320 | tf_op jit(solution)/shard_map/ppermute | solution.py:27
  68.2 18.8 %collective-permute-done.3.far = bf16[192,2048]{1,0:T(8,128)(2,1)S(1)} collective-permute-done((bf16[192,2048]{1,0:T(8,128)(2,1)}, bf16[192,2048]{1,0:T(8,128)(2,1)S(1)}, u32[]{:S(2)}, u32[]{:S(2)}) %collective-permute-start.3) | collective-permute-done | bytes 786464 | tf_op jit(solution)/shard_map/ppermute | solution.py:27
  87.0 0.9 copy-done.1
  87.9 10.4 %attend.1 = (f32[128,2176]{1,0:T(8,128)}, bf16[128,2176]{1,0:T(8,128)(2,1)}, bf16[128,2176]{1,0:T(8,128)(2,1)}) custom-call(bf16[128,2048]{1,0:T(8,128)(2,1)} %bitcast.19, bf16[128,2048]{1,0:T(8,128)(2,1)} %collective-permute-done.q_up, bf16[128,2048]{1,0:T(8,128)(2,1)} %copy-done.6, bf16[128,2048]{1,0:T(8,128)(2,1)} %bitcast.15, ...), custom_call_target="tpu_custom_call" | custom-call | flops 1207959552 | bytes 8388608 | tf_op jit(solution)/shard_map/attend/pallas_call | solution.py:170
  98.2 17.1 %collective-permute-start.10 = (bf16[128,2176]{1,0:T(8,128)(2,1)}, bf16[128,2176]{1,0:T(8,128)(2,1)S(1)}, u32[]{:S(2)}, u32[]{:S(2)}) collective-permute-start(bf16[128,2176]{1,0:T(8,128)(2,1)} %get-tuple-element.15), channel_id=1, source_target_pairs={{0,16},{1,17},{2,18},{3,19},{4,20},{5,21},{6,22},{7,23},{8,24},{9,... | collective-permute-start | bytes 1671176 | tf_op jit(solution)/shard_map/ppermute | solution.py:27
  115.4 1.9 %collective-permute-start.11 = (bf16[128,2176]{1,0:T(8,128)(2,1)}, bf16[128,2176]{1,0:T(8,128)(2,1)S(1)}, u32[]{:S(2)}, u32[]{:S(2)}) collective-permute-start(bf16[128,2176]{1,0:T(8,128)(2,1)} %get-tuple-element.16), channel_id=1, source_target_pairs={{16,0},{17,1},{18,2},{19,3},{20,4},{21,5},{22,6},{23,7},{24,8},{25... | collective-permute-start | bytes 1671176 | tf_op jit(solution)/shard_map/ppermute | solution.py:27
  117.9 9.5 %collective-permute-done.10.above = bf16[128,2176]{1,0:T(8,128)(2,1)S(1)} collective-permute-done((bf16[128,2176]{1,0:T(8,128)(2,1)}, bf16[128,2176]{1,0:T(8,128)(2,1)S(1)}, u32[]{:S(2)}, u32[]{:S(2)}) %collective-permute-start.10) | collective-permute-done | bytes 557088 | tf_op jit(solution)/shard_map/ppermute | solution.py:27
  127.5 6.1 %collective-permute-done.11.below = bf16[128,2176]{1,0:T(8,128)(2,1)S(1)} collective-permute-done((bf16[128,2176]{1,0:T(8,128)(2,1)}, bf16[128,2176]{1,0:T(8,128)(2,1)S(1)}, u32[]{:S(2)}, u32[]{:S(2)}) %collective-permute-start.11) | collective-permute-done | bytes 557088 | tf_op jit(solution)/shard_map/ppermute | solution.py:27
  134.4 3.4 %merge.1 = bf16[128,2048]{1,0:T(8,128)(2,1)} custom-call(s32[2]{0:T(128)} %add_convert_fusion.edges, f32[128,2176]{1,0:T(8,128)} %get-tuple-element.14.own, bf16[128,2176]{1,0:T(8,128)(2,1)} %copy-done.3, bf16[128,2176]{1,0:T(8,128)(2,1)} %copy-done.4), custom_call_target="tpu_custom_call" | custom-call | tf_op jit(solution)/shard_map/merge/pallas_call | solution.py:215
  (40 shorter events, 3.6 us)
Async XLA Ops:
  0.0 52.6 %collective-permute-start.9 = (s32[2,8]{1,0:T(2,128)}, s32[2,8]{1,0:T(2,128)S(1)}, u32[]{:S(2)}, u32[]{:S(2)}) collective-permute-start(s32[2,8]{1,0:T(2,128)} %bitcast.27), channel_id=1, source_target_pairs={{16,0},{17,1},{18,2},{19,3},{20,4},{21,5},{22,6},{23,7},{24,8},{25... | collective-permute-start | bytes 200 | tf_op jit(solution)/shard_map/ppermute | solution.py:27
  3.3 51.3 %collective-permute-start.8 = (s32[2,8]{1,0:T(2,128)}, s32[2,8]{1,0:T(2,128)S(1)}, u32[]{:S(2)}, u32[]{:S(2)}) collective-permute-start(s32[2,8]{1,0:T(2,128)} %bitcast.28), channel_id=1, source_target_pairs={{0,16},{1,17},{2,18},{3,19},{4,20},{5,21},{6,22},{7,23},{8,24},{9,... | collective-permute-start | bytes 200 | tf_op jit(solution)/shard_map/ppermute | solution.py:27
  8.0 51.8 %collective-permute-start.1 = (bf16[128,2048]{1,0:T(8,128)(2,1)}, bf16[128,2048]{1,0:T(8,128)(2,1)S(1)}, u32[]{:S(2)}, u32[]{:S(2)}) collective-permute-start(bf16[128,2048]{1,0:T(8,128)(2,1)} %bitcast.18), channel_id=1, source_target_pairs={{16,0},{17,1},{18,2},{19,3},{20,4},{21,5},{22,6},{23,7},{24,8},{25... | collective-permute-start | bytes 1572872 | tf_op jit(solution)/shard_map/ppermute | solution.py:27
  12.5 40.1 %copy-start.5 = (bf16[1,1,2,64,2048]{4,3,2,1,0:T(8,128)(2,1)S(1)}, bf16[1,1,2,64,2048]{4,3,2,1,0:T(8,128)(2,1)}, u32[]{:S(2)}) copy-start(bf16[1,1,2,64,2048]{4,3,2,1,0:T(8,128)(2,1)} %param.8) | copy-start | bytes 1572868
  12.5 46.2 %copy-start.7 = (s32[1,1,2,8]{3,2,1,0:T(2,128)S(1)}, s32[1,1,2,8]{3,2,1,0:T(2,128)}, u32[]{:S(2)}) copy-start(s32[1,1,2,8]{3,2,1,0:T(2,128)} %param.15) | copy-start | bytes 196
  12.6 13.0 %collective-permute-start.4 = (bf16[2,8,2048]{2,1,0:T(8,128)(2,1)}, bf16[2,8,2048]{2,1,0:T(8,128)(2,1)S(1)}, u32[]{:S(2)}, u32[]{:S(2)}) collective-permute-start(bf16[2,8,2048]{2,1,0:T(8,128)(2,1)} %get-tuple-element.13), channel_id=1, source_target_pairs={{0,386},{1,387},{2,384},{3,385},{4,390},{5,391},{6,388},{7,389},{8... | collective-permute-start | bytes 196616 | tf_op jit(solution)/shard_map/ppermute | solution.py:27
  22.7 45.4 %collective-permute-start.2 = (bf16[192,2048]{1,0:T(8,128)(2,1)}, bf16[192,2048]{1,0:T(8,128)(2,1)S(1)}, u32[]{:S(2)}, u32[]{:S(2)}) collective-permute-start(bf16[192,2048]{1,0:T(8,128)(2,1)} %get-tuple-element.11), channel_id=1, source_target_pairs={{0,1},{1,0},{2,3},{3,2},{4,5},{5,4},{6,7},{7,6},{8,9},{9,8},{10,11... | collective-permute-start | bytes 2359304 | tf_op jit(solution)/shard_map/ppermute | solution.py:27
  26.4 7.8 %collective-permute-start.5 = (bf16[2,16,2048]{2,1,0:T(8,128)(2,1)S(1)}, bf16[2,16,2048]{2,1,0:T(8,128)(2,1)S(1)}, u32[]{:S(2)}, u32[]{:S(2)}) collective-permute-start(bf16[2,16,2048]{2,1,0:T(8,128)(2,1)S(1)} %pad_maximum_fusion.1), channel_id=1, source_target_pairs={{0,4},{1,5},{2,6},{3,7},{4,0},{5,1},{6,2},{7,3},{8,12},{9,13},{10,... | collective-permute-start | bytes 393224 | tf_op jit(solution)/shard_map/ppermute | solution.py:27
  35.0 11.2 %collective-permute-start.6 = (bf16[2,32,2048]{2,1,0:T(8,128)(2,1)S(1)}, bf16[2,32,2048]{2,1,0:T(8,128)(2,1)S(1)}, u32[]{:S(2)}, u32[]{:S(2)}) collective-permute-start(bf16[2,32,2048]{2,1,0:T(8,128)(2,1)S(1)} %pad_maximum_fusion), channel_id=1, source_target_pairs={{0,8},{1,9},{2,10},{3,11},{4,12},{5,13},{6,14},{7,15},{8,0},{9,1},... | collective-permute-start | bytes 786440 | tf_op jit(solution)/shard_map/ppermute | solution.py:27
  46.3 40.7 %collective-permute-start.3 = (bf16[192,2048]{1,0:T(8,128)(2,1)}, bf16[192,2048]{1,0:T(8,128)(2,1)S(1)}, u32[]{:S(2)}, u32[]{:S(2)}) collective-permute-start(bf16[192,2048]{1,0:T(8,128)(2,1)} %get-tuple-element.12), channel_id=1, source_target_pairs={{1,2},{2,1},{3,4},{4,3},{5,6},{6,5},{7,8},{8,7},{9,10},{10,9},{11,... | collective-permute-start | bytes 2359304 | tf_op jit(solution)/shard_map/ppermute | solution.py:27
  52.6 34.4 %copy-start.2 = (bf16[2,64,2048]{2,1,0:T(8,128)(2,1)}, bf16[2,64,2048]{2,1,0:T(8,128)(2,1)S(1)}, u32[]{:S(2)}) copy-start(bf16[2,64,2048]{2,1,0:T(8,128)(2,1)S(1)} %constant_dynamic-update-slice_fusion.top_a) | copy-start | bytes 1572868
  52.6 15.5 %collective-permute-start = (bf16[128,2048]{1,0:T(8,128)(2,1)S(1)}, bf16[128,2048]{1,0:T(8,128)(2,1)}, u32[]{:S(2)}, u32[]{:S(2)}) collective-permute-start(bf16[128,2048]{1,0:T(8,128)(2,1)S(1)} %bitcast.20), channel_id=1, source_target_pairs={{0,16},{1,17},{2,18},{3,19},{4,20},{5,21},{6,22},{7,23},{8,24},{9,... | collective-permute-start | bytes 1572872 | tf_op jit(solution)/shard_map/ppermute | solution.py:27
  54.6 32.4 %collective-permute-start.7 = (bf16[2,64,2048]{2,1,0:T(8,128)(2,1)S(1)}, bf16[2,64,2048]{2,1,0:T(8,128)(2,1)}, u32[]{:S(2)}, u32[]{:S(2)}) collective-permute-start(bf16[2,64,2048]{2,1,0:T(8,128)(2,1)S(1)} %constant_dynamic-update-slice_fusion.top_a), channel_id=1, source_target_pairs={{0,1},{1,0},{2,3},{3,2},{4,5},{5,4},{6,7},{7,6},{8,9},{9,8},{10,11... | collective-permute-start | bytes 1572872 | tf_op jit(solution)/shard_map/ppermute | solution.py:27
  59.7 27.3 %copy-start.6 = (bf16[128,2048]{1,0:T(8,128)(2,1)}, bf16[128,2048]{1,0:T(8,128)(2,1)S(1)}, u32[]{:S(2)}) copy-start(bf16[128,2048]{1,0:T(8,128)(2,1)S(1)} %collective-permute-done.1.q_down) | copy-start | bytes 1572868
  68.2 18.8 %copy-start = (bf16[192,2048]{1,0:T(8,128)(2,1)}, bf16[192,2048]{1,0:T(8,128)(2,1)S(1)}, u32[]{:S(2)}) copy-start(bf16[192,2048]{1,0:T(8,128)(2,1)S(1)} %collective-permute-done.2.near) | copy-start | bytes 2359300
  87.0 0.9 copy-start.1
  98.2 29.2 %collective-permute-start.10 = (bf16[128,2176]{1,0:T(8,128)(2,1)}, bf16[128,2176]{1,0:T(8,128)(2,1)S(1)}, u32[]{:S(2)}, u32[]{:S(2)}) collective-permute-start(bf16[128,2176]{1,0:T(8,128)(2,1)} %get-tuple-element.15), channel_id=1, source_target_pairs={{0,16},{1,17},{2,18},{3,19},{4,20},{5,21},{6,22},{7,23},{8,24},{9,... | collective-permute-start | bytes 1671176 | tf_op jit(solution)/shard_map/ppermute | solution.py:27
  115.4 18.2 %collective-permute-start.11 = (bf16[128,2176]{1,0:T(8,128)(2,1)}, bf16[128,2176]{1,0:T(8,128)(2,1)S(1)}, u32[]{:S(2)}, u32[]{:S(2)}) collective-permute-start(bf16[128,2176]{1,0:T(8,128)(2,1)} %get-tuple-element.16), channel_id=1, source_target_pairs={{16,0},{17,1},{18,2},{19,3},{20,4},{21,5},{22,6},{23,7},{24,8},{25... | collective-permute-start | bytes 1671176 | tf_op jit(solution)/shard_map/ppermute | solution.py:27
  127.5 6.1 %copy-start.3 = (bf16[128,2176]{1,0:T(8,128)(2,1)}, bf16[128,2176]{1,0:T(8,128)(2,1)S(1)}, u32[]{:S(2)}) copy-start(bf16[128,2176]{1,0:T(8,128)(2,1)S(1)} %collective-permute-done.10.above) | copy-start | bytes 1671172
  133.6 0.8 copy-start.4

commit v2 on v1

v2 whole, which is shorter than its diff:
```python
import math

import jax
import jax.numpy as jnp
from jax import lax
from jax.experimental import pallas as pl
from jax.experimental.pallas import tpu as pltpu
from jax.sharding import PartitionSpec as P


HEADS = 16
NEG_FILL = -1e30
AXES = ("row", "col")
LANES = 128


def pairs(rows, cols, target):
    out = []
    for row in range(rows):
        for col in range(cols):
            there = target(row, col)
            if 0 <= there[0] < rows and 0 <= there[1] < cols:
                out.append((row * cols + col, there[0] * cols + there[1]))
    return out


def send(block, links):
    return lax.ppermute(block, AXES, links)


def pack_kernel(side, query, keys, values, pool_keys, pool_values, top_keys, top_values, near, far, top, first, second, sems):
    tokens = keys.shape[1]
    pool = pool_keys.shape[0]
    copies = []
    for out, block in ((far, side[0]), (near, 1 - side[0])):
        place = 0
        for source, count in (
            (keys.at[block], tokens),
            (pool_keys, pool),
            (values.at[block], tokens),
            (pool_values, pool),
        ):
            copies.append((source, out.at[pl.ds(place, count)]))
            place += count
    copies.append((top_keys, top.at[0]))
    copies.append((top_values, top.at[1]))
    copies.append((query.at[0], first))
    copies.append((query.at[1], second))
    run([pltpu.make_async_copy(a, b, sems.at[i]) for i, (a, b) in enumerate(copies)])


def pack(side, query, keys, values, pool_keys, pool_values, top_keys, top_values):
    tokens, width = keys.shape[1:]
    pool = pool_keys.shape[0]
    message = jax.ShapeDtypeStruct((2 * (tokens + pool), width), keys.dtype)
    share = jax.ShapeDtypeStruct((2,) + top_keys.shape, keys.dtype)
    block = jax.ShapeDtypeStruct((tokens, width), keys.dtype)
    return pl.pallas_call(
        pack_kernel,
        out_shape=(message, message, share, block, block),
        in_specs=[pl.BlockSpec(memory_space=pltpu.SMEM)] + [pl.BlockSpec(memory_space=pltpu.HBM)] * 7,
        out_specs=[pl.BlockSpec(memory_space=pltpu.VMEM)] * 5,
        scratch_shapes=[pltpu.SemaphoreType.DMA((12,))],
        compiler_params=pltpu.CompilerParams(vmem_limit_bytes=6 << 20),
        name="pack",
    )(side, query, keys, values, pool_keys, pool_values, top_keys, top_values)


def split_in_three(value):
    high = value.astype(jnp.bfloat16)
    rest = value - high.astype(jnp.float32)
    middle = rest.astype(jnp.bfloat16)
    low = (rest - middle.astype(jnp.float32)).astype(jnp.bfloat16)
    return high, middle, low


NT = (((1,), (1,)), ((), ()))


def fill(scratch, spans, sems, first):
    copies = []
    place = 0
    for ref in spans:
        count = ref.shape[0]
        copies.append(pltpu.make_async_copy(ref, scratch.at[pl.ds(place, count)], sems.at[first + len(copies)]))
        place += count
    return copies


def halves_of(ref):
    edge = ref.shape[0] // 2
    return ref.at[pl.ds(0, edge)], ref.at[pl.ds(edge, edge)]


def run(copies):
    for copy in copies:
        copy.start()
    for copy in copies:
        copy.wait()


def weigh(scores, bias, group, before=None):
    peaks, weights = [], []
    for i in range(scores.shape[0] // group):
        piece = scores[i * group : (i + 1) * group] + bias[pl.ds(i, 1), :]
        peak = jnp.max(piece, axis=1, keepdims=True)
        if before is not None:
            peak = jnp.maximum(before[i], peak)
        peaks.append(peak)
        weights.append(jnp.exp(piece - peak).astype(jnp.bfloat16))
    return peaks, jnp.concatenate(weights, axis=0)


def near_kernel(
    ends, q_up, q_down, bound, passed, keys, values, pool_keys, pool_values, near, bias,
    qs, sums, tops, norms, ks, vs, sems,
):
    rows, width = q_up.shape
    group = rows // 2
    near_keys, near_values = halves_of(near)
    copies = (
        fill(qs, (*halves_of(q_up), *halves_of(q_down)), sems, 0)
        + fill(ks, (keys, near_keys, pool_keys), sems, 4)
        + fill(vs, (values, near_values, pool_values), sems, 7)
    )
    for i in range(2):
        apart = fill(qs.at[pl.ds(i * rows, rows)], (bound, passed), sems, 2 * i)

        @pl.when(ends[i] > 0)
        def _():
            for copy in apart:
                copy.start()

        @pl.when(ends[i] == 0)
        def _():
            for copy in copies[2 * i : 2 * i + 2]:
                copy.start()

    for copy in copies[4:]:
        copy.start()
    for copy in copies:
        copy.wait()
    scale = 1.0 / math.sqrt(width // HEADS)
    ones = jnp.ones((ks.shape[0], LANES), jnp.bfloat16)
    for head in range(HEADS):
        part = pl.ds(head * LANES, LANES)
        scores = lax.dot_general(qs[:, part], ks[:, part], NT, preferred_element_type=jnp.float32) * scale
        peaks, weights = weigh(scores, bias, group)
        value = jnp.concatenate([vs[:, part], ones], axis=1)
        summed = jnp.dot(weights, value, preferred_element_type=jnp.float32)
        sums[:, part] = summed[:, :LANES]
        norms[:, part] = summed[:, LANES:]
        for i, peak in enumerate(peaks):
            tops[pl.ds(i * group, group), part] = jnp.broadcast_to(peak, (group, LANES))


def near_attention(ends, q_up, q_down, bound, passed, keys, values, pool_keys, pool_values, near, bias):
    rows, width = q_up.shape
    total = bias.shape[1]
    bf16, f32 = jnp.bfloat16, jnp.float32
    held, sent = pltpu.HBM, pl.ANY
    places = (pltpu.SMEM, sent, sent, sent, sent, held, held, held, held, sent, pltpu.VMEM)
    return pl.pallas_call(
        near_kernel,
        out_shape=[jax.ShapeDtypeStruct((2 * rows, width), kind) for kind in (bf16, f32, f32, f32)],
        in_specs=[pl.BlockSpec(memory_space=place) for place in places],
        out_specs=[pl.BlockSpec(memory_space=pltpu.VMEM)] * 4,
        scratch_shapes=[
            pltpu.VMEM((total, width), bf16),
            pltpu.VMEM((total, width), bf16),
            pltpu.SemaphoreType.DMA((10,)),
        ],
        compiler_params=pltpu.CompilerParams(vmem_limit_bytes=16 << 20),
        cost_estimate=pl.CostEstimate(
            flops=4 * 2 * rows * total * width, bytes_accessed=4 << 20, transcendentals=2 * rows * total * HEADS
        ),
        name="near_attention",
    )(ends, q_up, q_down, bound, passed, keys, values, pool_keys, pool_values, near, bias)


def far_kernel(qs, sums, tops, norms, far, bias, out_up, out_down, ks, vs):
    edge = far.shape[0] // 2
    rows = out_up.shape[0]
    width = qs.shape[1]
    group = rows // 2
    scale = 1.0 / math.sqrt(width // HEADS)
    for part, scratch in ((0, ks), (1, vs)):
        scratch[pl.ds(0, edge), :] = far[pl.ds(part * edge, edge), :]
        scratch[pl.ds(edge, LANES - edge), :] = jnp.zeros((LANES - edge, width), scratch.dtype)
    lane = lax.broadcasted_iota(jnp.int32, (group, LANES), 1)
    zero = jnp.zeros((group, LANES), jnp.float32)
    kept_peak, kept_norm = [zero] * 4, [zero + 1.0] * 4
    ones = jnp.ones((LANES, LANES), jnp.bfloat16)
    outs = (out_up, out_down)
    spans = [pl.ds(i * group, group) for i in range(4)]
    for head in range(HEADS):
        part = pl.ds(head * LANES, LANES)
        scores = lax.dot_general(qs[:, part], ks[:, part], NT, preferred_element_type=jnp.float32) * scale
        before = [tops[span, part] for span in spans]
        peaks, weights = weigh(scores, bias, group, before)
        value = jnp.concatenate([vs[:, part], ones], axis=1)
        summed = jnp.dot(weights, value, preferred_element_type=jnp.float32)
        for i, span in enumerate(spans):
            factor = jnp.exp(before[i] - peaks[i])
            piece = summed[i * group : (i + 1) * group]
            norm = norms[span, part] * factor + piece[:, LANES:]
            result = (sums[span, part] * factor + piece[:, :LANES]) / norm
            outs[i // 2][spans[i % 2], part] = result.astype(jnp.bfloat16)
            kept_peak[i] = jnp.where(lane == head, peaks[i], kept_peak[i])
            kept_norm[i] = jnp.where(lane == head, norm, kept_norm[i])
    for i in range(4):
        high, middle, low = split_in_three(kept_peak[i] + jnp.log(kept_norm[i]))
        middle = pltpu.roll(middle.astype(jnp.float32), HEADS, 1)
        low = pltpu.roll(low.astype(jnp.float32), 2 * HEADS, 1)
        outs[i // 2][spans[i % 2], pl.ds(width, LANES)] = (high.astype(jnp.float32) + middle + low).astype(jnp.bfloat16)


def far_attention(qs, sums, tops, norms, far, bias):
    rows, width = qs.shape[0] // 2, qs.shape[1]
    message = jax.ShapeDtypeStruct((rows, width + LANES), jnp.bfloat16)
    return pl.pallas_call(
        far_kernel,
        out_shape=(message, message),
        in_specs=[pl.BlockSpec(memory_space=pltpu.VMEM)] * 6,
        out_specs=[pl.BlockSpec(memory_space=pltpu.VMEM)] * 2,
        scratch_shapes=[pltpu.VMEM((LANES, width), jnp.bfloat16)] * 2,
        compiler_params=pltpu.CompilerParams(vmem_limit_bytes=16 << 20),
        cost_estimate=pl.CostEstimate(
            flops=4 * 2 * rows * LANES * width, bytes_accessed=4 << 20, transcendentals=2 * rows * LANES * HEADS
        ),
        name="far_attention",
    )(qs, sums, tops, norms, far, bias)


def own_kernel(query, keys, values, pool_keys, pool_values, near, far, top_a, top_b, bias, out, logs, qs, ks, vs, sems):
    rows, width = query.shape
    group = rows // 2
    gap = ks.shape[0] - keys.shape[0] - near.shape[0] // 2 - pool_keys.shape[0] - far.shape[0] // 2 - 2 * top_a.shape[1]
    copies = [pltpu.make_async_copy(query, qs, sems.at[0])]
    for part, scratch, mine, pool in ((0, ks, keys, pool_keys), (1, vs, values, pool_values)):
        spans = (top_a.at[part], top_b.at[part], mine, halves_of(near)[part], pool, halves_of(far)[part])
        copies += fill(scratch, spans, sems, 1 + 6 * part)
    for copy in copies:
        copy.start()
    for scratch in (ks, vs):
        scratch[pl.ds(ks.shape[0] - gap, gap), :] = jnp.zeros((gap, width), scratch.dtype)
    for copy in copies:
        copy.wait()
    scale = 1.0 / math.sqrt(width // HEADS)
    ones = jnp.ones((ks.shape[0], LANES), jnp.bfloat16)
    for head in range(HEADS):
        part = pl.ds(head * LANES, LANES)
        scores = lax.dot_general(qs[:, part], ks[:, part], NT, preferred_element_type=jnp.float32) * scale
        peaks, weights = weigh(scores, bias, group)
        value = jnp.concatenate([vs[:, part], ones], axis=1)
        summed = jnp.dot(weights, value, preferred_element_type=jnp.float32)
        norm = summed[:, LANES:]
        out[:, part] = summed[:, :LANES] / norm
        for i, peak in enumerate(peaks):
            span = pl.ds(i * group, group)
            logs[span, part] = peak + jnp.log(norm[i * group : (i + 1) * group])


def own_attention(query, keys, values, pool_keys, pool_values, near, far, top_a, top_b, bias):
    rows, width = query.shape
    total = bias.shape[1]
    bf16, f32 = jnp.bfloat16, jnp.float32
    held, sent = pltpu.HBM, pl.ANY
    places = (held, held, held, held, held, sent, sent, sent, sent, pltpu.VMEM)
    return pl.pallas_call(
        own_kernel,
        out_shape=[jax.ShapeDtypeStruct((rows, width), f32)] * 2,
        in_specs=[pl.BlockSpec(memory_space=place) for place in places],
        out_specs=[pl.BlockSpec(memory_space=pltpu.VMEM)] * 2,
        scratch_shapes=[
            pltpu.VMEM((rows, width), bf16),
            pltpu.VMEM((total, width), bf16),
            pltpu.VMEM((total, width), bf16),
            pltpu.SemaphoreType.DMA((13,)),
        ],
        compiler_params=pltpu.CompilerParams(vmem_limit_bytes=16 << 20),
        cost_estimate=pl.CostEstimate(
            flops=4 * rows * total * width, bytes_accessed=4 << 20, transcendentals=rows * total * HEADS
        ),
        name="own_attention",
    )(query, keys, values, pool_keys, pool_values, near, far, top_a, top_b, bias)


def merge_kernel(edges, own, own_logs, above, below, out):
    _, width = out.shape
    tail = pl.ds(width, LANES)
    logs = []
    for i, ref in enumerate((above, below)):
        coded = ref[:, tail].astype(jnp.float32)
        log = coded + pltpu.roll(coded, LANES - HEADS, 1) + pltpu.roll(coded, LANES - 2 * HEADS, 1)
        logs.append(jnp.where(edges[i] > 0, log, NEG_FILL))
    for head in range(HEADS):
        part = pl.ds(head * LANES, LANES)
        own_log = own_logs[:, part]
        up_log, down_log = (jnp.broadcast_to(log[:, head : head + 1], own_log.shape) for log in logs)
        peak = jnp.maximum(jnp.maximum(own_log, up_log), down_log)
        shares = [jnp.exp(log - peak) for log in (own_log, up_log, down_log)]
        result = own[:, part] * shares[0]
        result = result + above[:, part].astype(jnp.float32) * shares[1]
        result = result + below[:, part].astype(jnp.float32) * shares[2]
        out[:, part] = (result / (shares[0] + shares[1] + shares[2])).astype(out.dtype)


def merge(edges, own, own_logs, above, below):
    return pl.pallas_call(
        merge_kernel,
        out_shape=jax.ShapeDtypeStruct(own.shape, jnp.bfloat16),
        in_specs=[pl.BlockSpec(memory_space=pltpu.SMEM)] + [pl.BlockSpec(memory_space=pltpu.VMEM)] * 4,
        out_specs=pl.BlockSpec(memory_space=pltpu.VMEM),
        compiler_params=pltpu.CompilerParams(vmem_limit_bytes=8 << 20),
        name="merge",
    )(edges, own, own_logs, above, below)


def body(queries, keys, values, pool_keys, pool_values, top_keys, top_values, coarse_ids):
    _, _, blocks, tokens, width = queries.shape
    pool_blocks, pool_tokens, _ = pool_keys.shape
    rows = lax.axis_size("row")
    cols = lax.axis_size("col")
    row = lax.axis_index("row")
    col = lax.axis_index("col")
    side = col % 2
    pool = pool_blocks * pool_tokens
    own = blocks * tokens

    up = pairs(rows, cols, lambda r, q: (r - 1, q))
    down = pairs(rows, cols, lambda r, q: (r + 1, q))
    partner = pairs(rows, cols, lambda r, q: (r, q ^ 1))
    across = pairs(rows, cols, lambda r, q: (r, q + 1 if q % 2 else q - 1))
    line = rows // 4
    nowhere = (-1, -1)
    at_start = lambda r: r % line == 0
    at_end = lambda r: r % line == line - 1
    up_inside = pairs(rows, cols, lambda r, q: nowhere if at_start(r) else (r - 1, q))
    down_inside = pairs(rows, cols, lambda r, q: nowhere if at_end(r) else (r + 1, q))
    between = pairs(rows, cols, lambda r, q: (r + 1, q) if at_end(r) else (r - 1, q) if at_start(r) else nowhere)
    along_z = pairs(rows, cols, lambda r, q: (r + line, q) if at_end(r) else (r - line, q) if at_start(r) else nowhere)
    round_y = pairs(
        rows,
        cols,
        lambda r, q: (r - line + 1, q)
        if at_end(r) and r >= line
        else (r + line - 1, q)
        if at_start(r) and r < rows - line
        else nowhere,
    )
    halves = pairs(rows, cols, lambda r, q: ((3 - r // line) * line + r % line, q ^ 2))
    step_one = pairs(rows, cols, lambda r, q: (r, q ^ 4))
    step_two = pairs(rows, cols, lambda r, q: (r, q ^ 8))

    def stay(array, *shape):
        return pltpu.with_memory_space_constraint(array.reshape(shape), pltpu.HBM)

    query = queries.reshape(own, width)
    pk = stay(pool_keys, pool, width)
    pv = stay(pool_values, pool, width)
    near, far, top, first, second = pack(
        side.reshape(1),
        stay(queries, blocks, tokens, width),
        stay(keys, blocks, tokens, width),
        stay(values, blocks, tokens, width),
        pk,
        pv,
        stay(top_keys, *top_keys.shape[1:]),
        stay(top_values, *top_values.shape[1:]),
    )
    far = send(far, across)
    q_up = send(query, down_inside)
    q_down = send(query, up_inside)
    bound = send(first, between)
    passed = send(send(second, along_z), round_y)
    ends = jnp.stack([at_start(row), at_end(row)]).astype(jnp.int32)
    near = send(near, partner)
    for links in (step_one, step_two, halves):
        top = jnp.concatenate([top, send(top, links)], axis=1)
    top_other = send(top, partner)
    ids = coarse_ids.reshape(blocks, -1)
    ids_up = send(ids, down)
    ids_down = send(ids, up)

    other = col + 1 - 2 * side
    beyond = col - 1 + 2 * side
    exists = (beyond >= 0) & (beyond < cols)
    block_of = jnp.arange(blocks, dtype=jnp.int32)

    def bias_of(listed, count):
        def pool_valid(holder):
            first = (row * cols + holder) * pool_blocks
            block = first + jnp.arange(pool, dtype=jnp.int32) // pool_tokens
            return (listed[:, :, None] == block[None, None, :]).any(axis=1)

        def fine(valid):
            return jnp.broadcast_to(jnp.tile(valid, count)[:, None], (count * blocks, tokens))

        near_parts = [jnp.ones((count * blocks, own), bool), fine(block_of == 1 - side), pool_valid(other), pool_valid(col)]
        far_parts = [fine((block_of == side) & exists), pool_valid(beyond) & exists]
        far_parts.append(jnp.zeros((count * blocks, -(tokens + pool) % LANES), bool))
        as_bias = lambda parts: jnp.where(jnp.concatenate(parts, axis=1), 0.0, NEG_FILL).astype(jnp.float32)
        return as_bias(near_parts), as_bias(far_parts)

    near_bias, far_bias = bias_of(jnp.concatenate([ids_up, ids_down], axis=0), 2)
    own_bias = jnp.concatenate([jnp.zeros((blocks, 2 * top_other.shape[1]), jnp.float32), *bias_of(ids, 1)], axis=1)

    kept_keys, kept_values = stay(keys, own, width), stay(values, own, width)
    near_parts = near_attention(ends, q_up, q_down, bound, passed, kept_keys, kept_values, pk, pv, near, near_bias)
    to_up, to_down = far_attention(*near_parts, far, far_bias)
    below = send(to_up, up)
    above = send(to_down, down)
    mine = own_attention(
        stay(queries, own, width), kept_keys, kept_values, pk, pv, near, far, top, top_other, own_bias
    )
    edges = jnp.stack([row > 0, row < rows - 1]).astype(jnp.int32)
    return merge(edges, *mine, above, below).reshape(queries.shape)


def solution(mesh):
    placed = (
        P(None, "row", "col", None, None),
        P(None, "row", "col", None, None),
        P(None, "row", "col", None, None),
        P(("row", "col"), None, None),
        P(("row", "col"), None, None),
        P(None, "col", None),
        P(None, "col", None),
        P(None, "row", "col", None),
    )

    return jax.shard_map(
        body,
        mesh=mesh,
        in_specs=placed,
        out_specs=P(None, "row", "col", None, None),
        check_vma=False,
    )
```

time: 138 us -> 124 us (0.90)
  the two profiles are of different devices: /device:TPU:124 before, /device:TPU:62 now
where the time goes in v2:
time: 124 us; the launch traced here: 123 us
  waiting for transfers between devices  54.4 us (44%)
  starting transfers between devices  48.3 us (39%)
  Pallas kernels  14 us (11%)
  other arithmetic  3.21 us (3%)
  local copies, waits for them, and re-layouts  2.97 us (2%)
    ppermute x15, waiting for transfers between devices, send(): return lax.ppermute(block, AXES, links)  54.4 us
    ppermute x15, starting transfers between devices, send(): return lax.ppermute(block, AXES, links)  48.3 us
    pallas_call x1, Pallas kernels, near_attention(): pl.pallas_call(near_kernel, out_shape=[jax.ShapeDtypeStruct((2 * rows, wi...  3.59 us
    pallas_call x1, Pallas kernels, own_attention(): pl.pallas_call(own_kernel, out_shape=[jax.ShapeDtypeStruct((rows, width),...  3.58 us
    pallas_call x1, Pallas kernels, far_attention(): pl.pallas_call(far_kernel, out_shape=(message, message), in_specs=[pl.Blo...  2.82 us
    broadcast_in_dim x6, local copies, waits for them, and re-layouts, fine(): jnp.broadcast_to(jnp.tile(valid, count)[:, None], (count * blocks, tokens))  2.79 us
  transfers between devices with their start and end apart: 15, of which 5 were waited for; matrix products, arithmetic and copies ran while one was open for 5% of the time, Pallas kernels for 9%

profile of v2, /device:TPU:62, one launch (start us, length us, event | category | flops | bytes accessed | tf_op | source)
XLA Modules:
  0.0 123.3 jit_solution(14496759476244188267)
XLA Ops:
  0.0 3.5 %collective-permute-start.11 = (s32[2,8]{1,0:T(2,128)}, s32[2,8]{1,0:T(2,128)}, u32[]{:S(2)}, u32[]{:S(2)}) collective-permute-start(s32[2,8]{1,0:T(2,128)} %bitcast.35), channel_id=1, source_target_pairs={{0,16},{1,17},{2,18},{3,19},{4,20},{5,21},{6,22},{7,23},{8,24},{9,... | collective-permute-start | bytes 200 | tf_op jit(solution)/shard_map/ppermute | solution.py:28
  3.5 2.4 %collective-permute-start.12 = (s32[2,8]{1,0:T(2,128)}, s32[2,8]{1,0:T(2,128)}, u32[]{:S(2)}, u32[]{:S(2)}) collective-permute-start(s32[2,8]{1,0:T(2,128)} %bitcast.36), channel_id=1, source_target_pairs={{16,0},{17,1},{18,2},{19,3},{20,4},{21,5},{22,6},{23,7},{24,8},{25... | collective-permute-start | bytes 200 | tf_op jit(solution)/shard_map/ppermute | solution.py:28
  5.9 1.7 %pack.1 = (bf16[192,2048]{1,0:T(8,128)(2,1)S(1)}, bf16[192,2048]{1,0:T(8,128)(2,1)S(1)}, bf16[2,8,2048]{2,1,0:T(8,128)(2,1)S(1)}, bf16[64,2048]{1,0:T(8,128)(2,1)S(1)}, bf16[64,2048]{1,0:T(8,128)(2,1)S(1)}) custom-call(s32[1]{0:T(128)} %bitcast.7.side, bf16[2,64,2048]{2,1,0:T(8,128)(2,1)} %bitcast.23, bf16[2,64,2048]{2,1,0:T(8,128)(2,1)} %bitcast.17, ...), custom_call_target="tpu_custom_call" | custom-call | tf_op jit(solution)/shard_map/pack/pallas_call | solution.py:58
  7.5 1.9 %collective-permute-start = (bf16[192,2048]{1,0:T(8,128)(2,1)S(1)}, bf16[192,2048]{1,0:T(8,128)(2,1)S(1)}, u32[]{:S(2)}, u32[]{:S(2)}) collective-permute-start(bf16[192,2048]{1,0:T(8,128)(2,1)S(1)} %get-tuple-element.18), channel_id=1, source_target_pairs={{0,1},{1,0},{2,3},{3,2},{4,5},{5,4},{6,7},{7,6},{8,9},{9,8},{10,11... | collective-permute-start | bytes 2359304 | tf_op jit(solution)/shard_map/ppermute | solution.py:28
  9.5 5.0 %collective-permute-start.9 = (bf16[64,2048]{1,0:T(8,128)(2,1)S(1)}, bf16[64,2048]{1,0:T(8,128)(2,1)}, u32[]{:S(2)}, u32[]{:S(2)}) collective-permute-start(bf16[64,2048]{1,0:T(8,128)(2,1)S(1)} %get-tuple-element.24), channel_id=1, source_target_pairs={{112,240},{113,241},{114,242},{115,243},{116,244},{117,245},{118,2... | collective-permute-start | bytes 786440 | tf_op jit(solution)/shard_map/ppermute | solution.py:28
  14.5 2.7 %collective-permute-start.2 = (bf16[2,8,2048]{2,1,0:T(8,128)(2,1)S(1)}, bf16[2,8,2048]{2,1,0:T(8,128)(2,1)S(1)}, u32[]{:S(2)}, u32[]{:S(2)}) collective-permute-start(bf16[2,8,2048]{2,1,0:T(8,128)(2,1)S(1)} %get-tuple-element.20), channel_id=1, source_target_pairs={{0,4},{1,5},{2,6},{3,7},{4,0},{5,1},{6,2},{7,3},{8,12},{9,13},{10,... | collective-permute-start | bytes 196616 | tf_op jit(solution)/shard_map/ppermute | solution.py:28
  18.6 1.3 %compare_reduce_fusion.5 = (pred[2,32]{1,0:T(4,128)(4,1)S(1)}, pred[2,32]{1,0:T(4,128)(4,1)}, pred[2,32]{1,0:T(4,128)(4,1)S(1)}) fusion(s32[32]{0:T(128)S(1)} %fusion, s32[2,8]{1,0:T(2,128)} %bitcast.37, s32[32]{0:T(128)S(1)} %get-tuple-element.38, s32[32]{0:T(128)S(1)} %get-tuple-element.37), kind=kLoop, calls=%fused_computation.11 | loop fusion | flops 2880 | bytes 640 | tf_op jit(solution)/shard_map/reduce_or | solution.py:395
  20.7 2.5 %collective-permute-start.8 = (bf16[64,2048]{1,0:T(8,128)(2,1)S(1)}, bf16[64,2048]{1,0:T(8,128)(2,1)S(1)}, u32[]{:S(2)}, u32[]{:S(2)}) collective-permute-start(bf16[64,2048]{1,0:T(8,128)(2,1)S(1)} %get-tuple-element.23), channel_id=1, source_target_pairs={{112,128},{113,129},{114,130},{115,131},{116,132},{117,133},{118,1... | collective-permute-start | bytes 786440 | tf_op jit(solution)/shard_map/ppermute | solution.py:28
  23.3 10.2 %collective-permute-start.1 = (bf16[192,2048]{1,0:T(8,128)(2,1)S(1)}, bf16[192,2048]{1,0:T(8,128)(2,1)S(1)}, u32[]{:S(2)}, u32[]{:S(2)}) collective-permute-start(bf16[192,2048]{1,0:T(8,128)(2,1)S(1)} %get-tuple-element.19), channel_id=1, source_target_pairs={{1,2},{2,1},{3,4},{4,3},{5,6},{6,5},{7,8},{8,7},{9,10},{10,9},{11,... | collective-permute-start | bytes 2359304 | tf_op jit(solution)/shard_map/ppermute | solution.py:28
  35.0 3.3 %collective-permute-start.3 = (bf16[2,16,2048]{2,1,0:T(8,128)(2,1)S(1)}, bf16[2,16,2048]{2,1,0:T(8,128)(2,1)S(1)}, u32[]{:S(2)}, u32[]{:S(2)}) collective-permute-start(bf16[2,16,2048]{2,1,0:T(8,128)(2,1)S(1)} %pad_maximum_fusion.1), channel_id=1, source_target_pairs={{0,8},{1,9},{2,10},{3,11},{4,12},{5,13},{6,14},{7,15},{8,0},{9,1},... | collective-permute-start | bytes 393224 | tf_op jit(solution)/shard_map/ppermute | solution.py:28
  38.4 5.4 %collective-permute-done.3 = bf16[2,16,2048]{2,1,0:T(8,128)(2,1)S(1)} collective-permute-done((bf16[2,16,2048]{2,1,0:T(8,128)(2,1)S(1)}, bf16[2,16,2048]{2,1,0:T(8,128)(2,1)S(1)}, u32[]{:S(2)}, u32[]{:S(2)}) %collective-permute-start.3) | collective-permute-done | bytes 131104 | tf_op jit(solution)/shard_map/ppermute | solution.py:28
  43.8 1.9 %collective-permute-start.4 = (bf16[2,32,2048]{2,1,0:T(8,128)(2,1)S(1)}, bf16[2,32,2048]{2,1,0:T(8,128)(2,1)S(1)}, u32[]{:S(2)}, u32[]{:S(2)}) collective-permute-start(bf16[2,32,2048]{2,1,0:T(8,128)(2,1)S(1)} %pad_maximum_fusion), channel_id=1, source_target_pairs={{0,386},{1,387},{2,384},{3,385},{4,390},{5,391},{6,388},{7,389},{8... | collective-permute-start | bytes 786440 | tf_op jit(solution)/shard_map/ppermute | solution.py:28
  47.8 4.6 %collective-permute-start.7 = (bf16[128,2048]{1,0:T(8,128)(2,1)}, bf16[128,2048]{1,0:T(8,128)(2,1)S(1)}, u32[]{:S(2)}, u32[]{:S(2)}) collective-permute-start(bf16[128,2048]{1,0:T(8,128)(2,1)} %bitcast.25), channel_id=1, source_target_pairs={{16,0},{17,1},{18,2},{19,3},{20,4},{21,5},{22,6},{23,7},{24,8},{25... | collective-permute-start | bytes 1572872 | tf_op jit(solution)/shard_map/ppermute | solution.py:28
  52.4 27.6 %collective-permute-done.4 = bf16[2,32,2048]{2,1,0:T(8,128)(2,1)S(1)} collective-permute-done((bf16[2,32,2048]{2,1,0:T(8,128)(2,1)S(1)}, bf16[2,32,2048]{2,1,0:T(8,128)(2,1)S(1)}, u32[]{:S(2)}, u32[]{:S(2)}) %collective-permute-start.4) | collective-permute-done | bytes 262176 | tf_op jit(solution)/shard_map/ppermute | solution.py:28
  81.4 10.2 %collective-permute-done.10.passed = bf16[64,2048]{1,0:T(8,128)(2,1)S(1)} collective-permute-done((bf16[64,2048]{1,0:T(8,128)(2,1)}, bf16[64,2048]{1,0:T(8,128)(2,1)S(1)}, u32[]{:S(2)}, u32[]{:S(2)}) %collective-permute-start.10) | collective-permute-done | bytes 262176 | tf_op jit(solution)/shard_map/ppermute | solution.py:28
  91.6 1.9 %collective-permute-start.5 = (bf16[2,64,2048]{2,1,0:T(8,128)(2,1)S(1)}, bf16[2,64,2048]{2,1,0:T(8,128)(2,1)S(1)}, u32[]{:S(2)}, u32[]{:S(2)}) collective-permute-start(bf16[2,64,2048]{2,1,0:T(8,128)(2,1)S(1)} %constant_dynamic-update-slice_fusion.top_a), channel_id=1, source_target_pairs={{0,1},{1,0},{2,3},{3,2},{4,5},{5,4},{6,7},{7,6},{8,9},{9,8},{10,11... | collective-permute-start | bytes 1572872 | tf_op jit(solution)/shard_map/ppermute | solution.py:28
  93.6 3.6 %near_attention.1 = (bf16[256,2048]{1,0:T(8,128)(2,1)S(1)}, f32[256,2048]{1,0:T(8,128)S(1)}, f32[256,2048]{1,0:T(8,128)S(1)}, f32[256,2048]{1,0:T(8,128)S(1)}) custom-call(s32[2]{0:T(128)S(1)} %add_convert_fusion.1.ends, bf16[128,2048]{1,0:T(8,128)(2,1)S(1)} %collective-permute-done.6.q_up, bf16[128,2048]{1,0:T(8,128)(2,1)S(1)} %collective-permute-done.7.q_down, ...), custom_call_target="tpu_custom_call" | custom-call | flops 536870912 | bytes 4194304 | tf_op jit(solution)/shard_map/near_attention/pallas_call | solution.py:163
  97.2 2.8 %far_attention.1 = (bf16[128,2176]{1,0:T(8,128)(2,1)S(1)}, bf16[128,2176]{1,0:T(8,128)(2,1)S(1)}) custom-call(bf16[256,2048]{1,0:T(8,128)(2,1)S(1)} %get-tuple-element.25.qs, f32[256,2048]{1,0:T(8,128)S(1)} %get-tuple-element.26.sums, f32[256,2048]{1,0:T(8,128)S(1)} %get-tuple-element.27.tops, f32[256,2048]{1,0:T(8,128)S(1)} %get-tuple-element.28.norms, ...), custom_call_target="tpu_custom_call" | custom-call | flops 268435456 | bytes 4194304 | tf_op jit(solution)/shard_map/far_attention/pallas_call | solution.py:221
  100.0 1.9 %collective-permute-start.13 = (bf16[128,2176]{1,0:T(8,128)(2,1)S(1)}, bf16[128,2176]{1,0:T(8,128)(2,1)S(1)}, u32[]{:S(2)}, u32[]{:S(2)}) collective-permute-start(bf16[128,2176]{1,0:T(8,128)(2,1)S(1)} %get-tuple-element.29), channel_id=1, source_target_pairs={{0,16},{1,17},{2,18},{3,19},{4,20},{5,21},{6,22},{7,23},{8,24},{9,... | collective-permute-start | bytes 1671176 | tf_op jit(solution)/shard_map/ppermute | solution.py:28
  102.0 3.9 %collective-permute-start.14 = (bf16[128,2176]{1,0:T(8,128)(2,1)S(1)}, bf16[128,2176]{1,0:T(8,128)(2,1)S(1)}, u32[]{:S(2)}, u32[]{:S(2)}) collective-permute-start(bf16[128,2176]{1,0:T(8,128)(2,1)S(1)} %get-tuple-element.30), channel_id=1, source_target_pairs={{16,0},{17,1},{18,2},{19,3},{20,4},{21,5},{22,6},{23,7},{24,8},{25... | collective-permute-start | bytes 1671176 | tf_op jit(solution)/shard_map/ppermute | solution.py:28
  106.2 3.6 %own_attention.1 = (f32[128,2048]{1,0:T(8,128)S(1)}, f32[128,2048]{1,0:T(8,128)S(1)}) custom-call(bf16[128,2048]{1,0:T(8,128)(2,1)} %bitcast.26, bf16[128,2048]{1,0:T(8,128)(2,1)} %bitcast.19, bf16[128,2048]{1,0:T(8,128)(2,1)} %bitcast.22, bf16[32,2048]{1,0:T(8,128)(2,1)} %bitcast.29, bf16[32,2048]{1,0:T(8,128)(2,1)} %bitcast.32, ...), custom_call_target="tpu_custom_call" | custom-call | flops 536870912 | bytes 4194304 | tf_op jit(solution)/shard_map/own_attention/pallas_call | solution.py:270
  109.8 7.1 %collective-permute-done.13.above = bf16[128,2176]{1,0:T(8,128)(2,1)S(1)} collective-permute-done((bf16[128,2176]{1,0:T(8,128)(2,1)S(1)}, bf16[128,2176]{1,0:T(8,128)(2,1)S(1)}, u32[]{:S(2)}, u32[]{:S(2)}) %collective-permute-start.13) | collective-permute-done | bytes 557088 | tf_op jit(solution)/shard_map/ppermute | solution.py:28
  117.0 4.0 %collective-permute-done.14.below = bf16[128,2176]{1,0:T(8,128)(2,1)S(1)} collective-permute-done((bf16[128,2176]{1,0:T(8,128)(2,1)S(1)}, bf16[128,2176]{1,0:T(8,128)(2,1)S(1)}, u32[]{:S(2)}, u32[]{:S(2)}) %collective-permute-start.14) | collective-permute-done | bytes 557088 | tf_op jit(solution)/shard_map/ppermute | solution.py:28
  121.0 2.4 %merge.1 = bf16[128,2048]{1,0:T(8,128)(2,1)} custom-call(s32[2]{0:T(128)S(1)} %add_convert_fusion.edges, f32[128,2048]{1,0:T(8,128)S(1)} %get-tuple-element.21.own, f32[128,2048]{1,0:T(8,128)S(1)} %get-tuple-element.22.own_logs, bf16[128,2176]{1,0:T(8,128)(2,1)S(1)} %collective-permute-done.13.above, bf16[128,2176]{1,0:T(8,128)(2,1)S(1)} %collective-permute-done.14.below), custom_call_target="tpu_custom_call" | custom-call | tf_op jit(solution)/shard_map/merge/pallas_call | solution.py:310
  (58 shorter events, 7.5 us)
Async XLA Ops:
  0.0 20.7 %collective-permute-start.11 = (s32[2,8]{1,0:T(2,128)}, s32[2,8]{1,0:T(2,128)}, u32[]{:S(2)}, u32[]{:S(2)}) collective-permute-start(s32[2,8]{1,0:T(2,128)} %bitcast.35), channel_id=1, source_target_pairs={{0,16},{1,17},{2,18},{3,19},{4,20},{5,21},{6,22},{7,23},{8,24},{9,... | collective-permute-start | bytes 200 | tf_op jit(solution)/shard_map/ppermute | solution.py:28
  3.5 19.8 %collective-permute-start.12 = (s32[2,8]{1,0:T(2,128)}, s32[2,8]{1,0:T(2,128)}, u32[]{:S(2)}, u32[]{:S(2)}) collective-permute-start(s32[2,8]{1,0:T(2,128)} %bitcast.36), channel_id=1, source_target_pairs={{16,0},{17,1},{18,2},{19,3},{20,4},{21,5},{22,6},{23,7},{24,8},{25... | collective-permute-start | bytes 200 | tf_op jit(solution)/shard_map/ppermute | solution.py:28
  7.5 86.0 %collective-permute-start = (bf16[192,2048]{1,0:T(8,128)(2,1)S(1)}, bf16[192,2048]{1,0:T(8,128)(2,1)S(1)}, u32[]{:S(2)}, u32[]{:S(2)}) collective-permute-start(bf16[192,2048]{1,0:T(8,128)(2,1)S(1)} %get-tuple-element.18), channel_id=1, source_target_pairs={{0,1},{1,0},{2,3},{3,2},{4,5},{5,4},{6,7},{7,6},{8,9},{9,8},{10,11... | collective-permute-start | bytes 2359304 | tf_op jit(solution)/shard_map/ppermute | solution.py:28
  9.5 37.1 %collective-permute-start.9 = (bf16[64,2048]{1,0:T(8,128)(2,1)S(1)}, bf16[64,2048]{1,0:T(8,128)(2,1)}, u32[]{:S(2)}, u32[]{:S(2)}) collective-permute-start(bf16[64,2048]{1,0:T(8,128)(2,1)S(1)} %get-tuple-element.24), channel_id=1, source_target_pairs={{112,240},{113,241},{114,242},{115,243},{116,244},{117,245},{118,2... | collective-permute-start | bytes 786440 | tf_op jit(solution)/shard_map/ppermute | solution.py:28
  14.5 20.6 %collective-permute-start.2 = (bf16[2,8,2048]{2,1,0:T(8,128)(2,1)S(1)}, bf16[2,8,2048]{2,1,0:T(8,128)(2,1)S(1)}, u32[]{:S(2)}, u32[]{:S(2)}) collective-permute-start(bf16[2,8,2048]{2,1,0:T(8,128)(2,1)S(1)} %get-tuple-element.20), channel_id=1, source_target_pairs={{0,4},{1,5},{2,6},{3,7},{4,0},{5,1},{6,2},{7,3},{8,12},{9,13},{10,... | collective-permute-start | bytes 196616 | tf_op jit(solution)/shard_map/ppermute | solution.py:28
  17.3 0.6 copy-start.4
  17.9 0.7 copy-start.2
  20.7 27.1 %collective-permute-start.8 = (bf16[64,2048]{1,0:T(8,128)(2,1)S(1)}, bf16[64,2048]{1,0:T(8,128)(2,1)S(1)}, u32[]{:S(2)}, u32[]{:S(2)}) collective-permute-start(bf16[64,2048]{1,0:T(8,128)(2,1)S(1)} %get-tuple-element.23), channel_id=1, source_target_pairs={{112,128},{113,129},{114,130},{115,131},{116,132},{117,133},{118,1... | collective-permute-start | bytes 786440 | tf_op jit(solution)/shard_map/ppermute | solution.py:28
  23.3 73.9 %collective-permute-start.1 = (bf16[192,2048]{1,0:T(8,128)(2,1)S(1)}, bf16[192,2048]{1,0:T(8,128)(2,1)S(1)}, u32[]{:S(2)}, u32[]{:S(2)}) collective-permute-start(bf16[192,2048]{1,0:T(8,128)(2,1)S(1)} %get-tuple-element.19), channel_id=1, source_target_pairs={{1,2},{2,1},{3,4},{4,3},{5,6},{6,5},{7,8},{8,7},{9,10},{10,9},{11,... | collective-permute-start | bytes 2359304 | tf_op jit(solution)/shard_map/ppermute | solution.py:28
  35.0 8.7 %collective-permute-start.3 = (bf16[2,16,2048]{2,1,0:T(8,128)(2,1)S(1)}, bf16[2,16,2048]{2,1,0:T(8,128)(2,1)S(1)}, u32[]{:S(2)}, u32[]{:S(2)}) collective-permute-start(bf16[2,16,2048]{2,1,0:T(8,128)(2,1)S(1)} %pad_maximum_fusion.1), channel_id=1, source_target_pairs={{0,8},{1,9},{2,10},{3,11},{4,12},{5,13},{6,14},{7,15},{8,0},{9,1},... | collective-permute-start | bytes 393224 | tf_op jit(solution)/shard_map/ppermute | solution.py:28
  43.8 36.3 %collective-permute-start.4 = (bf16[2,32,2048]{2,1,0:T(8,128)(2,1)S(1)}, bf16[2,32,2048]{2,1,0:T(8,128)(2,1)S(1)}, u32[]{:S(2)}, u32[]{:S(2)}) collective-permute-start(bf16[2,32,2048]{2,1,0:T(8,128)(2,1)S(1)} %pad_maximum_fusion), channel_id=1, source_target_pairs={{0,386},{1,387},{2,384},{3,385},{4,390},{5,391},{6,388},{7,389},{8... | collective-permute-start | bytes 786440 | tf_op jit(solution)/shard_map/ppermute | solution.py:28
  46.5 47.0 %collective-permute-start.6 = (bf16[128,2048]{1,0:T(8,128)(2,1)}, bf16[128,2048]{1,0:T(8,128)(2,1)S(1)}, u32[]{:S(2)}, u32[]{:S(2)}) collective-permute-start(bf16[128,2048]{1,0:T(8,128)(2,1)} %bitcast.24), channel_id=1, source_target_pairs={{0,16},{1,17},{2,18},{3,19},{4,20},{5,21},{6,22},{7,23},{8,24},{9,... | collective-permute-start | bytes 1572872 | tf_op jit(solution)/shard_map/ppermute | solution.py:28
  47.8 45.7 %collective-permute-start.7 = (bf16[128,2048]{1,0:T(8,128)(2,1)}, bf16[128,2048]{1,0:T(8,128)(2,1)S(1)}, u32[]{:S(2)}, u32[]{:S(2)}) collective-permute-start(bf16[128,2048]{1,0:T(8,128)(2,1)} %bitcast.25), channel_id=1, source_target_pairs={{16,0},{17,1},{18,2},{19,3},{20,4},{21,5},{22,6},{23,7},{24,8},{25... | collective-permute-start | bytes 1572872 | tf_op jit(solution)/shard_map/ppermute | solution.py:28
  80.1 11.5 %collective-permute-start.10 = (bf16[64,2048]{1,0:T(8,128)(2,1)}, bf16[64,2048]{1,0:T(8,128)(2,1)S(1)}, u32[]{:S(2)}, u32[]{:S(2)}) collective-permute-start(bf16[64,2048]{1,0:T(8,128)(2,1)} %collective-permute-done.9), channel_id=1, source_target_pairs={{0,112},{1,113},{2,114},{3,115},{4,116},{5,117},{6,118},{7,119},{8... | collective-permute-start | bytes 786440 | tf_op jit(solution)/shard_map/ppermute | solution.py:28
  91.6 14.6 %collective-permute-start.5 = (bf16[2,64,2048]{2,1,0:T(8,128)(2,1)S(1)}, bf16[2,64,2048]{2,1,0:T(8,128)(2,1)S(1)}, u32[]{:S(2)}, u32[]{:S(2)}) collective-permute-start(bf16[2,64,2048]{2,1,0:T(8,128)(2,1)S(1)} %constant_dynamic-update-slice_fusion.top_a), channel_id=1, source_target_pairs={{0,1},{1,0},{2,3},{3,2},{4,5},{5,4},{6,7},{7,6},{8,9},{9,8},{10,11... | collective-permute-start | bytes 1572872 | tf_op jit(solution)/shard_map/ppermute | solution.py:28
  97.2 8.7 %copy-start.3 = (pred[2]{0:T(512)(128)(4,1)S(1)}, pred[2]{0:T(512)(128)(4,1)}, u32[]{:S(2)}) copy-start(pred[2]{0:T(512)(128)(4,1)} %copy-done.2) | copy-start | bytes 10
  97.2 8.8 %copy-start.1 = (pred[2,32]{1,0:T(4,128)(4,1)S(1)}, pred[2,32]{1,0:T(4,128)(4,1)}, u32[]{:S(2)}) copy-start(pred[2,32]{1,0:T(4,128)(4,1)} %broadcast_and_fusion.1) | copy-start | bytes 196
  97.2 8.9 %copy-start.5 = (pred[2]{0:T(512)(128)(4,1)S(1)}, pred[2]{0:T(512)(128)(4,1)}, u32[]{:S(2)}) copy-start(pred[2]{0:T(512)(128)(4,1)} %copy-done.4) | copy-start | bytes 10
  97.2 8.9 %copy-start = (pred[2,32]{1,0:T(4,128)(4,1)S(1)}, pred[2,32]{1,0:T(4,128)(4,1)}, u32[]{:S(2)}) copy-start(pred[2,32]{1,0:T(4,128)(4,1)} %get-tuple-element.35) | copy-start | bytes 196
  100.0 16.9 %collective-permute-start.13 = (bf16[128,2176]{1,0:T(8,128)(2,1)S(1)}, bf16[128,2176]{1,0:T(8,128)(2,1)S(1)}, u32[]{:S(2)}, u32[]{:S(2)}) collective-permute-start(bf16[128,2176]{1,0:T(8,128)(2,1)S(1)} %get-tuple-element.29), channel_id=1, source_target_pairs={{0,16},{1,17},{2,18},{3,19},{4,20},{5,21},{6,22},{7,23},{8,24},{9,... | collective-permute-start | bytes 1671176 | tf_op jit(solution)/shard_map/ppermute | solution.py:28
  102.0 19.0 %collective-permute-start.14 = (bf16[128,2176]{1,0:T(8,128)(2,1)S(1)}, bf16[128,2176]{1,0:T(8,128)(2,1)S(1)}, u32[]{:S(2)}, u32[]{:S(2)}) collective-permute-start(bf16[128,2176]{1,0:T(8,128)(2,1)S(1)} %get-tuple-element.30), channel_id=1, source_target_pairs={{16,0},{17,1},{18,2},{19,3},{20,4},{21,5},{22,6},{23,7},{24,8},{25... | collective-permute-start | bytes 1671176 | tf_op jit(solution)/shard_map/ppermute | solution.py:28

commit v3 on v2

v3 whole, which is shorter than its diff:
```python
import functools
import math

import jax
import jax.numpy as jnp
from jax import lax
from jax.experimental import pallas as pl
from jax.experimental.pallas import tpu as pltpu
from jax.sharding import PartitionSpec as P


HEADS = 16
NEG_FILL = -1e30
AXES = ("row", "col")
LANES = 128
TILE = 8
BASE = 256


def pairs(rows, cols, target):
    out = []
    for row in range(rows):
        for col in range(cols):
            there = target(row, col)
            if 0 <= there[0] < rows and 0 <= there[1] < cols:
                out.append((row * cols + col, there[0] * cols + there[1]))
    return out


def send(block, links):
    return lax.ppermute(block, AXES, links)


def into(out, sources):
    copies, place = [], 0
    for ref in sources:
        copies.append((ref, out.at[pl.ds(place, ref.shape[0])]))
        place += ref.shape[0]
    return copies


def carry_out(copies, sems):
    run([pltpu.make_async_copy(a, b, sems.at[i]) for i, (a, b) in enumerate(copies)])


def pack_far_kernel(position, query, keys, values, pool_keys, pool_values, far, second, sems):
    block = lax.rem(position[1], 2)
    copies = into(far, (keys.at[block], pool_keys, values.at[block], pool_values))
    carry_out(copies + [(query.at[1], second)], sems)


def pack_near_kernel(
    position, ids, query, keys, values, pool_keys, pool_values, top_keys, top_values, near, top, message, bound, sems
):
    block = 1 - lax.rem(position[1], 2)
    blocks, _, _ = query.shape
    copies = into(near, (keys.at[block], pool_keys, values.at[block], pool_values))
    copies += [(top_keys, top.at[0]), (top_values, top.at[1])]
    copies += into(message, [query.at[i] for i in range(blocks)])
    copies += into(bound, [query.at[0]])
    started = [pltpu.make_async_copy(a, b, sems.at[i]) for i, (a, b) in enumerate(copies)]
    for copy in started:
        copy.start()
    count = ids.shape[1]
    line = lax.broadcasted_iota(jnp.int32, (TILE, LANES), 0)
    lane = lax.broadcasted_iota(jnp.int32, (TILE, LANES), 1)
    digits = jnp.zeros((TILE, LANES), jnp.int32)
    for i in range(blocks):
        for j in range(count):
            number = ids[i, j]
            digits = jnp.where((line == i) & (lane == j), number // BASE, digits)
            digits = jnp.where((line == i) & (lane == count + j), number % BASE, digits)
    digits = digits.astype(jnp.float32).astype(message.dtype)
    for out in (message, bound):
        tail = pl.ds(out.shape[0] - TILE, TILE)
        out[tail, :] = jnp.zeros((TILE, out.shape[1]), out.dtype)
        out[tail, pl.ds(0, LANES)] = digits
    for copy in started:
        copy.wait()


def join_kernel(first, second, out, sems):
    size = first.shape[1]
    pieces = []
    for i in range(2):
        pieces.append((first.at[i], out.at[i, pl.ds(0, size)]))
        pieces.append((second.at[i], out.at[i, pl.ds(size, size)]))
    carry_out(pieces, sems)


def join(first, second):
    shape = (2, 2 * first.shape[1], first.shape[2])
    return pl.pallas_call(
        join_kernel,
        out_shape=jax.ShapeDtypeStruct(shape, first.dtype),
        in_specs=[pl.BlockSpec(memory_space=pl.ANY)] * 2,
        out_specs=pl.BlockSpec(memory_space=pltpu.VMEM),
        scratch_shapes=[pltpu.SemaphoreType.DMA((4,))],
        compiler_params=pltpu.CompilerParams(vmem_limit_bytes=1 << 20),
        name="join",
    )(first, second)


def packed(kernel, outs, scalars, arrays, copies):
    dtype = arrays[0].dtype
    places = [pltpu.SMEM] * len(scalars) + [pltpu.HBM] * len(arrays)
    return pl.pallas_call(
        kernel,
        out_shape=[jax.ShapeDtypeStruct(shape, dtype) for shape in outs],
        in_specs=[pl.BlockSpec(memory_space=place) for place in places],
        out_specs=[pl.BlockSpec(memory_space=pltpu.VMEM)] * len(outs),
        scratch_shapes=[pltpu.SemaphoreType.DMA((copies,))],
        compiler_params=pltpu.CompilerParams(vmem_limit_bytes=4 << 20),
    )(*scalars, *arrays)


def split_in_three(value):
    high = value.astype(jnp.bfloat16)
    rest = value - high.astype(jnp.float32)
    middle = rest.astype(jnp.bfloat16)
    low = (rest - middle.astype(jnp.float32)).astype(jnp.bfloat16)
    return high, middle, low


NT = (((1,), (1,)), ((), ()))


def fill(scratch, spans, sems, first):
    copies = []
    place = 0
    for ref in spans:
        count = ref.shape[0]
        copies.append(pltpu.make_async_copy(ref, scratch.at[pl.ds(place, count)], sems.at[first + len(copies)]))
        place += count
    return copies


def halves_of(ref):
    edge = ref.shape[0] // 2
    return ref.at[pl.ds(0, edge)], ref.at[pl.ds(edge, edge)]


def run(copies):
    for copy in copies:
        copy.start()
    for copy in copies:
        copy.wait()


class Spot:
    def __init__(self, position, cols, blocks):
        row, col = position[0], position[1]
        self.side = lax.rem(col, 2)
        other = col + 1 - 2 * self.side
        beyond = col - 1 + 2 * self.side
        self.exists = jnp.where((beyond >= 0) & (beyond < cols), 1, 0)
        self.own, self.other, self.beyond = ((row * cols + holder) * blocks for holder in (col, other, beyond))
        self.blocks = blocks


def numbers_of(digits, count):
    digits = digits.astype(jnp.float32)
    lane = lax.broadcasted_iota(jnp.int32, digits.shape, 1)
    number = digits * BASE + pltpu.roll(digits, LANES - count, 1)
    return jnp.where(lane < count, number, -1.0).astype(jnp.int32)


def bias_of(numbers, spot, width, near, tokens, pool):
    lane = lax.broadcasted_iota(jnp.int32, (TILE, width), 1)
    line = lax.broadcasted_iota(jnp.int32, (TILE, width), 0)
    if near:
        start = 2 * tokens
        mine = jnp.where(line == 1 - spot.side, 1, 0)
        listed = jnp.where(lane < start, 1, 0)
        holders = (spot.other, spot.own)
    else:
        start = 0
        mine = jnp.where(line == spot.side, spot.exists, 0)
        listed = jnp.zeros((TILE, width), jnp.int32)
        holders = (spot.beyond,)
    listed = jnp.where((lane >= start) & (lane < start + tokens), mine, listed)
    start += tokens
    size = pool // spot.blocks
    for holder in holders:
        for i in range(spot.blocks):
            hit = jnp.max(jnp.where(numbers == holder + i, 1.0, 0.0), axis=1, keepdims=True)
            hit = jnp.broadcast_to(hit, (TILE, width)).astype(jnp.int32)
            if not near:
                hit = hit * spot.exists
            listed = jnp.where((lane >= start) & (lane < start + size), hit, listed)
            start += size
    return jnp.where(listed > 0, 0.0, NEG_FILL)


def weigh(scores, bias, group, before=None):
    peaks, weights = [], []
    for i in range(scores.shape[0] // group):
        piece = scores[i * group : (i + 1) * group] + bias[pl.ds(i, 1), :]
        peak = jnp.max(piece, axis=1, keepdims=True)
        if before is not None:
            peak = jnp.maximum(before[i], peak)
        peaks.append(peak)
        weights.append(jnp.exp(piece - peak).astype(jnp.bfloat16))
    return peaks, jnp.concatenate(weights, axis=0)


def near_kernel(
    cols, pool_blocks, count, line, position, q_up, q_down, bound, passed, keys, values, pool_keys, pool_values, near,
    qs, sums, tops, norms, numbers, ks, vs, tails, bias, sems,
):
    rows, width = qs.shape[0] // 2, qs.shape[1]
    group = rows // 2
    in_line = lax.rem(position[0], line)
    at_end = (in_line == 0, in_line == line - 1)
    near_keys, near_values = halves_of(near)
    blocks = [ref.at[pl.ds(i * group, group)] for ref in (q_up, q_down) for i in range(2)]
    copies = (
        fill(qs, blocks, sems, 0)
        + fill(ks, (keys, near_keys, pool_keys), sems, 4)
        + fill(vs, (values, near_values, pool_values), sems, 7)
    )
    for i in range(2):
        apart = fill(qs.at[pl.ds(i * rows, rows)], (bound.at[pl.ds(0, group)], passed), sems, 2 * i)
        corner = pl.ds(0, LANES)
        tail = tails.at[pl.ds(i * TILE, TILE)]
        source = (q_up, q_down)[i].at[pl.ds(rows, TILE), corner]
        copies.append(pltpu.make_async_copy(source, tail, sems.at[10 + i]))
        apart.append(pltpu.make_async_copy(bound.at[pl.ds(group, TILE), corner], tail, sems.at[10 + i]))

        @pl.when(at_end[i])
        def _():
            for copy in apart:
                copy.start()

        @pl.when(jnp.logical_not(at_end[i]))
        def _():
            for copy in (*copies[2 * i : 2 * i + 2], copies[10 + i]):
                copy.start()

    for copy in copies[4:10]:
        copy.start()
    for copy in copies:
        copy.wait()
    spot = Spot(position, cols, pool_blocks)
    for i in range(2):
        listed = numbers_of(tails[pl.ds(i * TILE, TILE), :], count)
        numbers[pl.ds(i * TILE, TILE), :] = listed
        bias[pl.ds(2 * i, 2), :] = bias_of(listed, spot, ks.shape[0], True, group, pool_keys.shape[0])[:2]
    scale = 1.0 / math.sqrt(width // HEADS)
    ones = jnp.ones((ks.shape[0], LANES), jnp.bfloat16)
    for head in range(HEADS):
        part = pl.ds(head * LANES, LANES)
        scores = lax.dot_general(qs[:, part], ks[:, part], NT, preferred_element_type=jnp.float32) * scale
        peaks, weights = weigh(scores, bias, group)
        value = jnp.concatenate([vs[:, part], ones], axis=1)
        summed = jnp.dot(weights, value, preferred_element_type=jnp.float32)
        sums[:, part] = summed[:, :LANES]
        norms[:, part] = summed[:, LANES:]
        for i, peak in enumerate(peaks):
            tops[pl.ds(i * group, group), part] = jnp.broadcast_to(peak, (group, LANES))


def near_attention(shape, position, q_up, q_down, bound, passed, keys, values, pool_keys, pool_values, near):
    rows, width = keys.shape
    total = rows + near.shape[0] // 2 + pool_keys.shape[0]
    bf16, f32 = jnp.bfloat16, jnp.float32
    held, sent = pltpu.HBM, pl.ANY
    places = (pltpu.SMEM, sent, sent, sent, sent, held, held, held, held, sent)
    return pl.pallas_call(
        functools.partial(near_kernel, *shape),
        out_shape=[jax.ShapeDtypeStruct((2 * rows, width), kind) for kind in (bf16, f32, f32, f32)]
        + [jax.ShapeDtypeStruct((2 * TILE, LANES), jnp.int32)],
        in_specs=[pl.BlockSpec(memory_space=place) for place in places],
        out_specs=[pl.BlockSpec(memory_space=pltpu.VMEM)] * 5,
        scratch_shapes=[
            pltpu.VMEM((total, width), bf16),
            pltpu.VMEM((total, width), bf16),
            pltpu.VMEM((2 * TILE, LANES), bf16),
            pltpu.VMEM((TILE, total), f32),
            pltpu.SemaphoreType.DMA((12,)),
        ],
        compiler_params=pltpu.CompilerParams(vmem_limit_bytes=11 << 20),
        cost_estimate=pl.CostEstimate(
            flops=4 * 2 * rows * total * width, bytes_accessed=4 << 20, transcendentals=2 * rows * total * HEADS
        ),
        name="near_attention",
    )(position, q_up, q_down, bound, passed, keys, values, pool_keys, pool_values, near)


def far_kernel(cols, pool_blocks, count, position, qs, sums, tops, norms, numbers, far, out_up, out_down, ks, vs, bias):
    edge = far.shape[0] // 2
    spot = Spot(position, cols, pool_blocks)
    half = out_up.shape[0] // 2
    for i in range(2):
        listed = numbers[pl.ds(i * TILE, TILE), :]
        bias[pl.ds(2 * i, 2), :] = bias_of(listed, spot, LANES, False, half, edge - half)[:2]
    rows = out_up.shape[0]
    width = qs.shape[1]
    group = rows // 2
    scale = 1.0 / math.sqrt(width // HEADS)
    for part, scratch in ((0, ks), (1, vs)):
        scratch[pl.ds(0, edge), :] = far[pl.ds(part * edge, edge), :]
        scratch[pl.ds(edge, LANES - edge), :] = jnp.zeros((LANES - edge, width), scratch.dtype)
    lane = lax.broadcasted_iota(jnp.int32, (group, LANES), 1)
    zero = jnp.zeros((group, LANES), jnp.float32)
    kept_peak, kept_norm = [zero] * 4, [zero + 1.0] * 4
    ones = jnp.ones((LANES, LANES), jnp.bfloat16)
    outs = (out_up, out_down)
    spans = [pl.ds(i * group, group) for i in range(4)]
    for head in range(HEADS):
        part = pl.ds(head * LANES, LANES)
        scores = lax.dot_general(qs[:, part], ks[:, part], NT, preferred_element_type=jnp.float32) * scale
        before = [tops[span, part] for span in spans]
        peaks, weights = weigh(scores, bias, group, before)
        value = jnp.concatenate([vs[:, part], ones], axis=1)
        summed = jnp.dot(weights, value, preferred_element_type=jnp.float32)
        for i, span in enumerate(spans):
            factor = jnp.exp(before[i] - peaks[i])
            piece = summed[i * group : (i + 1) * group]
            norm = norms[span, part] * factor + piece[:, LANES:]
            result = (sums[span, part] * factor + piece[:, :LANES]) / norm
            outs[i // 2][spans[i % 2], part] = result.astype(jnp.bfloat16)
            kept_peak[i] = jnp.where(lane == head, peaks[i], kept_peak[i])
            kept_norm[i] = jnp.where(lane == head, norm, kept_norm[i])
    for i in range(4):
        high, middle, low = split_in_three(kept_peak[i] + jnp.log(kept_norm[i]))
        middle = pltpu.roll(middle.astype(jnp.float32), HEADS, 1)
        low = pltpu.roll(low.astype(jnp.float32), 2 * HEADS, 1)
        outs[i // 2][spans[i % 2], pl.ds(width, LANES)] = (high.astype(jnp.float32) + middle + low).astype(jnp.bfloat16)


def far_attention(shape, position, qs, sums, tops, norms, numbers, far):
    rows, width = qs.shape[0] // 2, qs.shape[1]
    message = jax.ShapeDtypeStruct((rows, width + LANES), jnp.bfloat16)
    return pl.pallas_call(
        functools.partial(far_kernel, *shape),
        out_shape=(message, message),
        in_specs=[pl.BlockSpec(memory_space=pltpu.SMEM)] + [pl.BlockSpec(memory_space=pltpu.VMEM)] * 6,
        out_specs=[pl.BlockSpec(memory_space=pltpu.VMEM)] * 2,
        scratch_shapes=[pltpu.VMEM((LANES, width), jnp.bfloat16)] * 2 + [pltpu.VMEM((TILE, LANES), jnp.float32)],
        compiler_params=pltpu.CompilerParams(vmem_limit_bytes=3 << 20),
        cost_estimate=pl.CostEstimate(
            flops=4 * 2 * rows * LANES * width, bytes_accessed=4 << 20, transcendentals=2 * rows * LANES * HEADS
        ),
        name="far_attention",
    )(position, qs, sums, tops, norms, numbers, far)


def own_kernel(
    cols, pool_blocks, count, position, message, keys, values, pool_keys, pool_values, near, far, top_a, top_b,
    out, logs, qs, ks, vs, tail, bias, sems,
):
    rows, width = qs.shape
    group = rows // 2
    gap = ks.shape[0] - keys.shape[0] - near.shape[0] // 2 - pool_keys.shape[0] - far.shape[0] // 2 - 2 * top_a.shape[1]
    corner = message.at[pl.ds(rows, TILE), pl.ds(0, LANES)]
    copies = [
        pltpu.make_async_copy(message.at[pl.ds(0, rows)], qs, sems.at[0]),
        pltpu.make_async_copy(corner, tail, sems.at[13]),
    ]
    for part, scratch, mine, pool in ((0, ks, keys, pool_keys), (1, vs, values, pool_values)):
        spans = (top_a.at[part], top_b.at[part], mine, halves_of(near)[part], pool, halves_of(far)[part])
        copies += fill(scratch, spans, sems, 1 + 6 * part)
    for copy in copies:
        copy.start()
    for scratch in (ks, vs):
        scratch[pl.ds(ks.shape[0] - gap, gap), :] = jnp.zeros((gap, width), scratch.dtype)
    for copy in copies:
        copy.wait()
    spot = Spot(position, cols, pool_blocks)
    listed = numbers_of(tail[...], count)
    top, pool = 2 * top_a.shape[1], pool_keys.shape[0]
    chip = keys.shape[0] + near.shape[0] // 2 + pool
    bias[:, pl.ds(0, top)] = jnp.zeros((TILE, top), jnp.float32)
    bias[:, pl.ds(top, chip)] = bias_of(listed, spot, chip, True, group, pool)
    bias[:, pl.ds(top + chip, LANES)] = bias_of(listed, spot, LANES, False, group, pool)
    scale = 1.0 / math.sqrt(width // HEADS)
    ones = jnp.ones((ks.shape[0], LANES), jnp.bfloat16)
    for head in range(HEADS):
        part = pl.ds(head * LANES, LANES)
        scores = lax.dot_general(qs[:, part], ks[:, part], NT, preferred_element_type=jnp.float32) * scale
        peaks, weights = weigh(scores, bias, group)
        value = jnp.concatenate([vs[:, part], ones], axis=1)
        summed = jnp.dot(weights, value, preferred_element_type=jnp.float32)
        norm = summed[:, LANES:]
        out[:, part] = summed[:, :LANES] / norm
        for i, peak in enumerate(peaks):
            span = pl.ds(i * group, group)
            logs[span, part] = peak + jnp.log(norm[i * group : (i + 1) * group])


def own_attention(shape, position, message, keys, values, pool_keys, pool_values, near, far, top_a, top_b):
    rows, width = keys.shape
    total = 2 * top_a.shape[1] + rows + near.shape[0] // 2 + pool_keys.shape[0] + LANES
    bf16, f32 = jnp.bfloat16, jnp.float32
    held, sent = pltpu.HBM, pl.ANY
    places = (pltpu.SMEM, sent, held, held, held, held, sent, sent, sent, sent)
    return pl.pallas_call(
        functools.partial(own_kernel, *shape),
        out_shape=[jax.ShapeDtypeStruct((rows, width), f32)] * 2,
        in_specs=[pl.BlockSpec(memory_space=place) for place in places],
        out_specs=[pl.BlockSpec(memory_space=pltpu.VMEM)] * 2,
        scratch_shapes=[
            pltpu.VMEM((rows, width), bf16),
            pltpu.VMEM((total, width), bf16),
            pltpu.VMEM((total, width), bf16),
            pltpu.VMEM((TILE, LANES), bf16),
            pltpu.VMEM((TILE, total), f32),
            pltpu.SemaphoreType.DMA((14,)),
        ],
        compiler_params=pltpu.CompilerParams(vmem_limit_bytes=8 << 20),
        cost_estimate=pl.CostEstimate(
            flops=4 * rows * total * width, bytes_accessed=4 << 20, transcendentals=rows * total * HEADS
        ),
        name="own_attention",
    )(position, message, keys, values, pool_keys, pool_values, near, far, top_a, top_b)


def merge_kernel(last, position, own, own_logs, above, below, out):
    _, width = out.shape
    tail = pl.ds(width, LANES)
    logs = []
    for i, ref in enumerate((above, below)):
        coded = ref[:, tail].astype(jnp.float32)
        log = coded + pltpu.roll(coded, LANES - HEADS, 1) + pltpu.roll(coded, LANES - 2 * HEADS, 1)
        logs.append(jnp.where(position[0] == last * i, NEG_FILL, log))
    for head in range(HEADS):
        part = pl.ds(head * LANES, LANES)
        own_log = own_logs[:, part]
        up_log, down_log = (jnp.broadcast_to(log[:, head : head + 1], own_log.shape) for log in logs)
        peak = jnp.maximum(jnp.maximum(own_log, up_log), down_log)
        shares = [jnp.exp(log - peak) for log in (own_log, up_log, down_log)]
        result = own[:, part] * shares[0]
        result = result + above[:, part].astype(jnp.float32) * shares[1]
        result = result + below[:, part].astype(jnp.float32) * shares[2]
        out[:, part] = (result / (shares[0] + shares[1] + shares[2])).astype(out.dtype)


def merge(rows_in_all, position, own, own_logs, above, below):
    return pl.pallas_call(
        functools.partial(merge_kernel, rows_in_all - 1),
        out_shape=jax.ShapeDtypeStruct(own.shape, jnp.bfloat16),
        in_specs=[pl.BlockSpec(memory_space=pltpu.SMEM)] + [pl.BlockSpec(memory_space=pltpu.VMEM)] * 4,
        out_specs=pl.BlockSpec(memory_space=pltpu.VMEM),
        compiler_params=pltpu.CompilerParams(vmem_limit_bytes=4 << 20),
        name="merge",
    )(position, own, own_logs, above, below)


def body(queries, keys, values, pool_keys, pool_values, top_keys, top_values, coarse_ids):
    _, _, blocks, tokens, width = queries.shape
    pool_blocks, pool_tokens, _ = pool_keys.shape
    rows = lax.axis_size("row")
    cols = lax.axis_size("col")
    row = lax.axis_index("row")
    col = lax.axis_index("col")
    position = jnp.stack([row, col]).astype(jnp.int32)
    pool = pool_blocks * pool_tokens
    own = blocks * tokens

    up = pairs(rows, cols, lambda r, q: (r - 1, q))
    down = pairs(rows, cols, lambda r, q: (r + 1, q))
    partner = pairs(rows, cols, lambda r, q: (r, q ^ 1))
    across = pairs(rows, cols, lambda r, q: (r, q + 1 if q % 2 else q - 1))
    line = rows // 4
    nowhere = (-1, -1)
    at_start = lambda r: r % line == 0
    at_end = lambda r: r % line == line - 1
    up_inside = pairs(rows, cols, lambda r, q: nowhere if at_start(r) else (r - 1, q))
    down_inside = pairs(rows, cols, lambda r, q: nowhere if at_end(r) else (r + 1, q))
    between = pairs(rows, cols, lambda r, q: (r + 1, q) if at_end(r) else (r - 1, q) if at_start(r) else nowhere)
    along_z = pairs(rows, cols, lambda r, q: (r + line, q) if at_end(r) else (r - line, q) if at_start(r) else nowhere)
    round_y = pairs(
        rows,
        cols,
        lambda r, q: (r - line + 1, q)
        if at_end(r) and r >= line
        else (r + line - 1, q)
        if at_start(r) and r < rows - line
        else nowhere,
    )
    halves = pairs(rows, cols, lambda r, q: ((3 - r // line) * line + r % line, q ^ 2))
    step_one = pairs(rows, cols, lambda r, q: (r, q ^ 4))
    step_two = pairs(rows, cols, lambda r, q: (r, q ^ 8))

    def stay(array, *shape):
        return pltpu.with_memory_space_constraint(array.reshape(shape), pltpu.HBM)

    pk = stay(pool_keys, pool, width)
    pv = stay(pool_values, pool, width)
    sources = (
        stay(queries, blocks, tokens, width),
        stay(keys, blocks, tokens, width),
        stay(values, blocks, tokens, width),
        pk,
        pv,
    )
    shares = (stay(top_keys, *top_keys.shape[1:]), stay(top_values, *top_values.shape[1:]))
    ids = coarse_ids.reshape(blocks, -1)
    edge = (2 * (tokens + pool), width)
    far, second = packed(pack_far_kernel, [edge, (tokens, width)], [position], sources, 5)
    passed = send(second, along_z)
    far = send(far, across)
    near, top, message, bound = packed(
        pack_near_kernel,
        [edge, (2,) + top_keys.shape[1:], (own + TILE, width), (tokens + TILE, width)],
        [position, ids],
        sources + shares,
        9,
    )
    bound = send(bound, between)
    q_down = send(message, up_inside)
    q_up = send(message, down_inside)
    near = send(near, partner)
    passed = send(passed, round_y)
    for links in (step_one, step_two, halves):
        top = join(top, send(top, links))
    top_other = send(top, partner)

    shape = (cols, pool_blocks, ids.shape[1])
    kept_keys, kept_values = stay(keys, own, width), stay(values, own, width)
    near_parts = near_attention(
        shape + (line,), position, q_up, q_down, bound, passed, kept_keys, kept_values, pk, pv, near
    )
    to_up, to_down = far_attention(shape, position, *near_parts, far)
    below = send(to_up, up)
    above = send(to_down, down)
    mine = own_attention(shape, position, message, kept_keys, kept_values, pk, pv, near, far, top, top_other)
    return merge(rows, position, *mine, above, below).reshape(queries.shape)


def solution(mesh):
    placed = (
        P(None, "row", "col", None, None),
        P(None, "row", "col", None, None),
        P(None, "row", "col", None, None),
        P(("row", "col"), None, None),
        P(("row", "col"), None, None),
        P(None, "col", None),
        P(None, "col", None),
        P(None, "row", "col", None),
    )

    return jax.shard_map(
        body,
        mesh=mesh,
        in_specs=placed,
        out_specs=P(None, "row", "col", None, None),
        check_vma=False,
    )
```

time: 124 us -> 115 us (0.927)
  the two profiles are of different devices: /device:TPU:62 before, /device:TPU:56 now
where the time goes in v3:
time: 115 us
  waiting for transfers between devices  54.8 us (48%)
  starting transfers between devices  40.6 us (35%)
  Pallas kernels  18.6 us (16%)
    ppermute x13, waiting for transfers between devices, send(): return lax.ppermute(block, AXES, links)  54.8 us
    ppermute x13, starting transfers between devices, send(): return lax.ppermute(block, AXES, links)  40.6 us
    pallas_call x1, Pallas kernels, own_attention(): pl.pallas_call(functools.partial(own_kernel, *shape), out_shape=[jax.Shap...  4.16 us
    pallas_call x2, Pallas kernels, packed(): pl.pallas_call(kernel, out_shape=[jax.ShapeDtypeStruct(shape, dtype) for...  3.84 us
    pallas_call x1, Pallas kernels, near_attention(): pl.pallas_call(functools.partial(near_kernel, *shape), out_shape=[jax.Sha...  3.6 us
    pallas_call x1, Pallas kernels, far_attention(): pl.pallas_call(functools.partial(far_kernel, *shape), out_shape=(message,...  3.34 us
    pallas_call x1, Pallas kernels, merge(): pl.pallas_call(functools.partial(merge_kernel, rows_in_all - 1), out_shap...  2.35 us
  transfers between devices with their start and end apart: 13, of which 6 were waited for; matrix products, arithmetic and copies ran while one was open for 0% of the time, Pallas kernels for 12%

profile of v3, /device:TPU:56, one launch (start us, length us, event | category | flops | bytes accessed | tf_op | source)
XLA Modules:
  0.0 115.0 jit_solution(4435031003571622338)
XLA Ops:
  0.8 2.0 %shard_map.82 = (bf16[192,2048]{1,0:T(8,128)(2,1)S(1)}, bf16[2,8,2048]{2,1,0:T(8,128)(2,1)S(1)}, bf16[136,2048]{1,0:T(8,128)(2,1)S(1)}, bf16[72,2048]{1,0:T(8,128)(2,1)S(1)}) custom-call(s32[2]{0:T(128)S(1)} %pad_add_fusion.position, s32[2,8]{1,0:T(2,128)S(1)} %bitcast.13, bf16[2,64,2048]{2,1,0:T(8,128)(2,1)} %bitcast.22, bf16[2,64,2048]{2,1,0:T(8,128)(2,1)} %bitcast.14, ...), custom_call_target="tpu_custom_call" | custom-call | tf_op jit(solution)/shard_map/pallas_call | solution.py:107
  2.8 3.5 %collective-permute-start.8 = (bf16[72,2048]{1,0:T(8,128)(2,1)S(1)}, bf16[72,2048]{1,0:T(8,128)(2,1)S(1)}, u32[]{:S(2)}, u32[]{:S(2)}) collective-permute-start(bf16[72,2048]{1,0:T(8,128)(2,1)S(1)} %get-tuple-element.26), channel_id=1, source_target_pairs={{112,128},{113,129},{114,130},{115,131},{116,132},{117,133},{118,1... | collective-permute-start | bytes 884744 | tf_op jit(solution)/shard_map/ppermute | solution.py:31
  6.3 1.8 %shard_map.83 = (bf16[192,2048]{1,0:T(8,128)(2,1)S(1)}, bf16[64,2048]{1,0:T(8,128)(2,1)S(1)}) custom-call(s32[2]{0:T(128)S(1)} %pad_add_fusion.position, bf16[2,64,2048]{2,1,0:T(8,128)(2,1)} %bitcast.23, bf16[2,64,2048]{2,1,0:T(8,128)(2,1)} %bitcast.15, bf16[2,64,2048]{2,1,0:T(8,128)(2,1)} %bitcast.19, bf16[32,2048]{1,0:T(8,128)(2,1)} %bitcast.25, ...), custom_call_target="tpu_custom_call" | custom-call | tf_op jit(solution)/shard_map/pallas_call | solution.py:107
  8.1 4.3 %collective-permute-start.9 = (bf16[64,2048]{1,0:T(8,128)(2,1)S(1)}, bf16[64,2048]{1,0:T(8,128)(2,1)S(1)}, u32[]{:S(2)}, u32[]{:S(2)}) collective-permute-start(bf16[64,2048]{1,0:T(8,128)(2,1)S(1)} %get-tuple-element.27), channel_id=1, source_target_pairs={{112,240},{113,241},{114,242},{115,243},{116,244},{117,245},{118,2... | collective-permute-start | bytes 786440 | tf_op jit(solution)/shard_map/ppermute | solution.py:31
  12.4 1.9 %collective-permute-start = (bf16[192,2048]{1,0:T(8,128)(2,1)S(1)}, bf16[192,2048]{1,0:T(8,128)(2,1)S(1)}, u32[]{:S(2)}, u32[]{:S(2)}) collective-permute-start(bf16[192,2048]{1,0:T(8,128)(2,1)S(1)} %get-tuple-element.21), channel_id=1, source_target_pairs={{0,1},{1,0},{2,3},{3,2},{4,5},{5,4},{6,7},{7,6},{8,9},{9,8},{10,11... | collective-permute-start | bytes 2359304 | tf_op jit(solution)/shard_map/ppermute | solution.py:31
  14.3 3.4 %collective-permute-start.2 = (bf16[2,8,2048]{2,1,0:T(8,128)(2,1)S(1)}, bf16[2,8,2048]{2,1,0:T(8,128)(2,1)S(1)}, u32[]{:S(2)}, u32[]{:S(2)}) collective-permute-start(bf16[2,8,2048]{2,1,0:T(8,128)(2,1)S(1)} %get-tuple-element.23.first), channel_id=1, source_target_pairs={{0,4},{1,5},{2,6},{3,7},{4,0},{5,1},{6,2},{7,3},{8,12},{9,13},{10,... | collective-permute-start | bytes 196616 | tf_op jit(solution)/shard_map/ppermute | solution.py:31
  18.5 2.3 %collective-permute-done.2.second = bf16[2,8,2048]{2,1,0:T(8,128)(2,1)S(1)} collective-permute-done((bf16[2,8,2048]{2,1,0:T(8,128)(2,1)S(1)}, bf16[2,8,2048]{2,1,0:T(8,128)(2,1)S(1)}, u32[]{:S(2)}, u32[]{:S(2)}) %collective-permute-start.2) | collective-permute-done | bytes 65568 | tf_op jit(solution)/shard_map/ppermute | solution.py:31
  20.9 10.0 %collective-permute-start.3 = (bf16[2,16,2048]{2,1,0:T(8,128)(2,1)S(1)}, bf16[2,16,2048]{2,1,0:T(8,128)(2,1)S(1)}, u32[]{:S(2)}, u32[]{:S(2)}) collective-permute-start(bf16[2,16,2048]{2,1,0:T(8,128)(2,1)S(1)} %join.3.first), channel_id=1, source_target_pairs={{0,8},{1,9},{2,10},{3,11},{4,12},{5,13},{6,14},{7,15},{8,0},{9,1},... | collective-permute-start | bytes 393224 | tf_op jit(solution)/shard_map/ppermute | solution.py:31
  30.9 5.5 %collective-permute-done.3.second = bf16[2,16,2048]{2,1,0:T(8,128)(2,1)S(1)} collective-permute-done((bf16[2,16,2048]{2,1,0:T(8,128)(2,1)S(1)}, bf16[2,16,2048]{2,1,0:T(8,128)(2,1)S(1)}, u32[]{:S(2)}, u32[]{:S(2)}) %collective-permute-start.3) | collective-permute-done | bytes 131104 | tf_op jit(solution)/shard_map/ppermute | solution.py:31
  36.4 1.3 %collective-permute-start.6 = (bf16[136,2048]{1,0:T(8,128)(2,1)S(1)}, bf16[136,2048]{1,0:T(8,128)(2,1)S(1)}, u32[]{:S(2)}, u32[]{:S(2)}) collective-permute-start(bf16[136,2048]{1,0:T(8,128)(2,1)S(1)} %get-tuple-element.20.message), channel_id=1, source_target_pairs={{0,16},{1,17},{2,18},{3,19},{4,20},{5,21},{6,22},{7,23},{8,24},{9,... | collective-permute-start | bytes 1671176 | tf_op jit(solution)/shard_map/ppermute | solution.py:31
  37.7 4.6 %collective-permute-start.7 = (bf16[136,2048]{1,0:T(8,128)(2,1)S(1)}, bf16[136,2048]{1,0:T(8,128)(2,1)S(1)}, u32[]{:S(2)}, u32[]{:S(2)}) collective-permute-start(bf16[136,2048]{1,0:T(8,128)(2,1)S(1)} %get-tuple-element.20.message), channel_id=1, source_target_pairs={{16,0},{17,1},{18,2},{19,3},{20,4},{21,5},{22,6},{23,7},{24,8},{25... | collective-permute-start | bytes 1671176 | tf_op jit(solution)/shard_map/ppermute | solution.py:31
  42.7 1.9 %collective-permute-start.4 = (bf16[2,32,2048]{2,1,0:T(8,128)(2,1)S(1)}, bf16[2,32,2048]{2,1,0:T(8,128)(2,1)S(1)}, u32[]{:S(2)}, u32[]{:S(2)}) collective-permute-start(bf16[2,32,2048]{2,1,0:T(8,128)(2,1)S(1)} %join.4.first), channel_id=1, source_target_pairs={{0,386},{1,387},{2,384},{3,385},{4,390},{5,391},{6,388},{7,389},{8... | collective-permute-start | bytes 786440 | tf_op jit(solution)/shard_map/ppermute | solution.py:31
  44.6 26.8 %collective-permute-done.4.second = bf16[2,32,2048]{2,1,0:T(8,128)(2,1)S(1)} collective-permute-done((bf16[2,32,2048]{2,1,0:T(8,128)(2,1)S(1)}, bf16[2,32,2048]{2,1,0:T(8,128)(2,1)S(1)}, u32[]{:S(2)}, u32[]{:S(2)}) %collective-permute-start.4) | collective-permute-done | bytes 262176 | tf_op jit(solution)/shard_map/ppermute | solution.py:31
  71.4 1.3 %collective-permute-start.10 = (bf16[64,2048]{1,0:T(8,128)(2,1)S(1)}, bf16[64,2048]{1,0:T(8,128)(2,1)S(1)}, u32[]{:S(2)}, u32[]{:S(2)}) collective-permute-start(bf16[64,2048]{1,0:T(8,128)(2,1)S(1)} %collective-permute-done.9), channel_id=1, source_target_pairs={{0,112},{1,113},{2,114},{3,115},{4,116},{5,117},{6,118},{7,119},{8... | collective-permute-start | bytes 786440 | tf_op jit(solution)/shard_map/ppermute | solution.py:31
  73.4 9.3 %collective-permute-done.10.passed = bf16[64,2048]{1,0:T(8,128)(2,1)S(1)} collective-permute-done((bf16[64,2048]{1,0:T(8,128)(2,1)S(1)}, bf16[64,2048]{1,0:T(8,128)(2,1)S(1)}, u32[]{:S(2)}, u32[]{:S(2)}) %collective-permute-start.10) | collective-permute-done | bytes 262176 | tf_op jit(solution)/shard_map/ppermute | solution.py:31
  82.7 1.9 %collective-permute-start.5 = (bf16[2,64,2048]{2,1,0:T(8,128)(2,1)S(1)}, bf16[2,64,2048]{2,1,0:T(8,128)(2,1)S(1)}, u32[]{:S(2)}, u32[]{:S(2)}) collective-permute-start(bf16[2,64,2048]{2,1,0:T(8,128)(2,1)S(1)} %join.5.top_a), channel_id=1, source_target_pairs={{0,1},{1,0},{2,3},{3,2},{4,5},{5,4},{6,7},{7,6},{8,9},{9,8},{10,11... | collective-permute-start | bytes 1572872 | tf_op jit(solution)/shard_map/ppermute | solution.py:31
  84.7 3.6 %near_attention.1 = (bf16[256,2048]{1,0:T(8,128)(2,1)S(1)}, f32[256,2048]{1,0:T(8,128)S(1)}, f32[256,2048]{1,0:T(8,128)S(1)}, f32[256,2048]{1,0:T(8,128)S(1)}, s32[16,128]{1,0:T(8,128)S(1)}) custom-call(s32[2]{0:T(128)S(1)} %pad_add_fusion.position, bf16[136,2048]{1,0:T(8,128)(2,1)S(1)} %collective-permute-done.6.q_up, ...), custom_call_target="tpu_custom_call" | custom-call | flops 536870912 | bytes 4194304 | tf_op jit(solution)/shard_map/near_attention/pallas_call | solution.py:269
  88.3 3.3 %far_attention.1 = (bf16[128,2176]{1,0:T(8,128)(2,1)S(1)}, bf16[128,2176]{1,0:T(8,128)(2,1)S(1)}) custom-call(s32[2]{0:T(128)S(1)} %pad_add_fusion.position, bf16[256,2048]{1,0:T(8,128)(2,1)S(1)} %get-tuple-element.28.qs, f32[256,2048]{1,0:T(8,128)S(1)} %get-tuple-element.29.sums, f32[256,2048]{1,0:T(8,128)S(1)} %get-tuple-element.30.tops, ...), custom_call_target="tpu_custom_call" | custom-call | flops 268435456 | bytes 4194304 | tf_op jit(solution)/shard_map/far_attention/pallas_call | solution.py:335
  91.6 1.9 %collective-permute-start.11 = (bf16[128,2176]{1,0:T(8,128)(2,1)S(1)}, bf16[128,2176]{1,0:T(8,128)(2,1)S(1)}, u32[]{:S(2)}, u32[]{:S(2)}) collective-permute-start(bf16[128,2176]{1,0:T(8,128)(2,1)S(1)} %get-tuple-element.33), channel_id=1, source_target_pairs={{0,16},{1,17},{2,18},{3,19},{4,20},{5,21},{6,22},{7,23},{8,24},{9,... | collective-permute-start | bytes 1671176 | tf_op jit(solution)/shard_map/ppermute | solution.py:31
  93.6 3.9 %collective-permute-start.12 = (bf16[128,2176]{1,0:T(8,128)(2,1)S(1)}, bf16[128,2176]{1,0:T(8,128)(2,1)S(1)}, u32[]{:S(2)}, u32[]{:S(2)}) collective-permute-start(bf16[128,2176]{1,0:T(8,128)(2,1)S(1)} %get-tuple-element.34), channel_id=1, source_target_pairs={{16,0},{17,1},{18,2},{19,3},{20,4},{21,5},{22,6},{23,7},{24,8},{25... | collective-permute-start | bytes 1671176 | tf_op jit(solution)/shard_map/ppermute | solution.py:31
  97.5 4.2 %own_attention.1 = (f32[128,2048]{1,0:T(8,128)S(1)}, f32[128,2048]{1,0:T(8,128)S(1)}) custom-call(s32[2]{0:T(128)S(1)} %pad_add_fusion.position, bf16[136,2048]{1,0:T(8,128)(2,1)S(1)} %get-tuple-element.20.message, bf16[128,2048]{1,0:T(8,128)(2,1)} %bitcast.17, bf16[128,2048]{1,0:T(8,128)(2,1)} %bitcast.21, bf16[32,2048]{1,0:T(8,128)(2,1)} %bitcast.27, ...), custom_call_target="tpu_custom_call" | custom-call | flops 536870912 | bytes 4194304 | tf_op jit(solution)/shard_map/own_attention/pallas_call | solution.py:398
  101.7 6.9 %collective-permute-done.11.above = bf16[128,2176]{1,0:T(8,128)(2,1)S(1)} collective-permute-done((bf16[128,2176]{1,0:T(8,128)(2,1)S(1)}, bf16[128,2176]{1,0:T(8,128)(2,1)S(1)}, u32[]{:S(2)}, u32[]{:S(2)}) %collective-permute-start.11) | collective-permute-done | bytes 557088 | tf_op jit(solution)/shard_map/ppermute | solution.py:31
  108.6 4.0 %collective-permute-done.12.below = bf16[128,2176]{1,0:T(8,128)(2,1)S(1)} collective-permute-done((bf16[128,2176]{1,0:T(8,128)(2,1)S(1)}, bf16[128,2176]{1,0:T(8,128)(2,1)S(1)}, u32[]{:S(2)}, u32[]{:S(2)}) %collective-permute-start.12) | collective-permute-done | bytes 557088 | tf_op jit(solution)/shard_map/ppermute | solution.py:31
  112.6 2.4 %merge.1 = bf16[128,2048]{1,0:T(8,128)(2,1)} custom-call(s32[2]{0:T(128)S(1)} %pad_add_fusion.position, f32[128,2048]{1,0:T(8,128)S(1)} %get-tuple-element.24.own, f32[128,2048]{1,0:T(8,128)S(1)} %get-tuple-element.25.own_logs, bf16[128,2176]{1,0:T(8,128)(2,1)S(1)} %collective-permute-done.11.above, bf16[128,2176]{1,0:T(8,128)(2,1)S(1)} %collective-permute-done.12.below), custom_call_target="tpu_custom_call" | custom-call | tf_op jit(solution)/shard_map/merge/pallas_call | solution.py:440
  (14 shorter events, 2.8 us)
Async XLA Ops:
  0.1 0.7 copy-start
  2.8 39.9 %collective-permute-start.8 = (bf16[72,2048]{1,0:T(8,128)(2,1)S(1)}, bf16[72,2048]{1,0:T(8,128)(2,1)S(1)}, u32[]{:S(2)}, u32[]{:S(2)}) collective-permute-start(bf16[72,2048]{1,0:T(8,128)(2,1)S(1)} %get-tuple-element.26), channel_id=1, source_target_pairs={{112,128},{113,129},{114,130},{115,131},{116,132},{117,133},{118,1... | collective-permute-start | bytes 884744 | tf_op jit(solution)/shard_map/ppermute | solution.py:31
  8.1 29.6 %collective-permute-start.9 = (bf16[64,2048]{1,0:T(8,128)(2,1)S(1)}, bf16[64,2048]{1,0:T(8,128)(2,1)S(1)}, u32[]{:S(2)}, u32[]{:S(2)}) collective-permute-start(bf16[64,2048]{1,0:T(8,128)(2,1)S(1)} %get-tuple-element.27), channel_id=1, source_target_pairs={{112,240},{113,241},{114,242},{115,243},{116,244},{117,245},{118,2... | collective-permute-start | bytes 786440 | tf_op jit(solution)/shard_map/ppermute | solution.py:31
  12.4 72.3 %collective-permute-start = (bf16[192,2048]{1,0:T(8,128)(2,1)S(1)}, bf16[192,2048]{1,0:T(8,128)(2,1)S(1)}, u32[]{:S(2)}, u32[]{:S(2)}) collective-permute-start(bf16[192,2048]{1,0:T(8,128)(2,1)S(1)} %get-tuple-element.21), channel_id=1, source_target_pairs={{0,1},{1,0},{2,3},{3,2},{4,5},{5,4},{6,7},{7,6},{8,9},{9,8},{10,11... | collective-permute-start | bytes 2359304 | tf_op jit(solution)/shard_map/ppermute | solution.py:31
  14.3 6.4 %collective-permute-start.2 = (bf16[2,8,2048]{2,1,0:T(8,128)(2,1)S(1)}, bf16[2,8,2048]{2,1,0:T(8,128)(2,1)S(1)}, u32[]{:S(2)}, u32[]{:S(2)}) collective-permute-start(bf16[2,8,2048]{2,1,0:T(8,128)(2,1)S(1)} %get-tuple-element.23.first), channel_id=1, source_target_pairs={{0,4},{1,5},{2,6},{3,7},{4,0},{5,1},{6,2},{7,3},{8,12},{9,13},{10,... | collective-permute-start | bytes 196616 | tf_op jit(solution)/shard_map/ppermute | solution.py:31
  17.7 70.6 %collective-permute-start.1 = (bf16[192,2048]{1,0:T(8,128)(2,1)S(1)}, bf16[192,2048]{1,0:T(8,128)(2,1)S(1)}, u32[]{:S(2)}, u32[]{:S(2)}) collective-permute-start(bf16[192,2048]{1,0:T(8,128)(2,1)S(1)} %get-tuple-element.22), channel_id=1, source_target_pairs={{1,2},{2,1},{3,4},{4,3},{5,6},{6,5},{7,8},{8,7},{9,10},{10,9},{11,... | collective-permute-start | bytes 2359304 | tf_op jit(solution)/shard_map/ppermute | solution.py:31
  20.9 15.5 %collective-permute-start.3 = (bf16[2,16,2048]{2,1,0:T(8,128)(2,1)S(1)}, bf16[2,16,2048]{2,1,0:T(8,128)(2,1)S(1)}, u32[]{:S(2)}, u32[]{:S(2)}) collective-permute-start(bf16[2,16,2048]{2,1,0:T(8,128)(2,1)S(1)} %join.3.first), channel_id=1, source_target_pairs={{0,8},{1,9},{2,10},{3,11},{4,12},{5,13},{6,14},{7,15},{8,0},{9,1},... | collective-permute-start | bytes 393224 | tf_op jit(solution)/shard_map/ppermute | solution.py:31
  36.4 48.2 %collective-permute-start.6 = (bf16[136,2048]{1,0:T(8,128)(2,1)S(1)}, bf16[136,2048]{1,0:T(8,128)(2,1)S(1)}, u32[]{:S(2)}, u32[]{:S(2)}) collective-permute-start(bf16[136,2048]{1,0:T(8,128)(2,1)S(1)} %get-tuple-element.20.message), channel_id=1, source_target_pairs={{0,16},{1,17},{2,18},{3,19},{4,20},{5,21},{6,22},{7,23},{8,24},{9,... | collective-permute-start | bytes 1671176 | tf_op jit(solution)/shard_map/ppermute | solution.py:31
  37.7 47.0 %collective-permute-start.7 = (bf16[136,2048]{1,0:T(8,128)(2,1)S(1)}, bf16[136,2048]{1,0:T(8,128)(2,1)S(1)}, u32[]{:S(2)}, u32[]{:S(2)}) collective-permute-start(bf16[136,2048]{1,0:T(8,128)(2,1)S(1)} %get-tuple-element.20.message), channel_id=1, source_target_pairs={{16,0},{17,1},{18,2},{19,3},{20,4},{21,5},{22,6},{23,7},{24,8},{25... | collective-permute-start | bytes 1671176 | tf_op jit(solution)/shard_map/ppermute | solution.py:31
  42.7 28.7 %collective-permute-start.4 = (bf16[2,32,2048]{2,1,0:T(8,128)(2,1)S(1)}, bf16[2,32,2048]{2,1,0:T(8,128)(2,1)S(1)}, u32[]{:S(2)}, u32[]{:S(2)}) collective-permute-start(bf16[2,32,2048]{2,1,0:T(8,128)(2,1)S(1)} %join.4.first), channel_id=1, source_target_pairs={{0,386},{1,387},{2,384},{3,385},{4,390},{5,391},{6,388},{7,389},{8... | collective-permute-start | bytes 786440 | tf_op jit(solution)/shard_map/ppermute | solution.py:31
  71.4 11.3 %collective-permute-start.10 = (bf16[64,2048]{1,0:T(8,128)(2,1)S(1)}, bf16[64,2048]{1,0:T(8,128)(2,1)S(1)}, u32[]{:S(2)}, u32[]{:S(2)}) collective-permute-start(bf16[64,2048]{1,0:T(8,128)(2,1)S(1)} %collective-permute-done.9), channel_id=1, source_target_pairs={{0,112},{1,113},{2,114},{3,115},{4,116},{5,117},{6,118},{7,119},{8... | collective-permute-start | bytes 786440 | tf_op jit(solution)/shard_map/ppermute | solution.py:31
  82.7 14.8 %collective-permute-start.5 = (bf16[2,64,2048]{2,1,0:T(8,128)(2,1)S(1)}, bf16[2,64,2048]{2,1,0:T(8,128)(2,1)S(1)}, u32[]{:S(2)}, u32[]{:S(2)}) collective-permute-start(bf16[2,64,2048]{2,1,0:T(8,128)(2,1)S(1)} %join.5.top_a), channel_id=1, source_target_pairs={{0,1},{1,0},{2,3},{3,2},{4,5},{5,4},{6,7},{7,6},{8,9},{9,8},{10,11... | collective-permute-start | bytes 1572872 | tf_op jit(solution)/shard_map/ppermute | solution.py:31
  91.6 16.9 %collective-permute-start.11 = (bf16[128,2176]{1,0:T(8,128)(2,1)S(1)}, bf16[128,2176]{1,0:T(8,128)(2,1)S(1)}, u32[]{:S(2)}, u32[]{:S(2)}) collective-permute-start(bf16[128,2176]{1,0:T(8,128)(2,1)S(1)} %get-tuple-element.33), channel_id=1, source_target_pairs={{0,16},{1,17},{2,18},{3,19},{4,20},{5,21},{6,22},{7,23},{8,24},{9,... | collective-permute-start | bytes 1671176 | tf_op jit(solution)/shard_map/ppermute | solution.py:31
  93.6 19.0 %collective-permute-start.12 = (bf16[128,2176]{1,0:T(8,128)(2,1)S(1)}, bf16[128,2176]{1,0:T(8,128)(2,1)S(1)}, u32[]{:S(2)}, u32[]{:S(2)}) collective-permute-start(bf16[128,2176]{1,0:T(8,128)(2,1)S(1)} %get-tuple-element.34), channel_id=1, source_target_pairs={{16,0},{17,1},{18,2},{19,3},{20,4},{21,5},{22,6},{23,7},{24,8},{25... | collective-permute-start | bytes 1671176 | tf_op jit(solution)/shard_map/ppermute | solution.py:31

commit v4 on v3

--- a/solution.py
+++ b/solution.py
@@ -206,7 +206,7 @@
 
 def near_kernel(
     cols, pool_blocks, count, line, position, q_up, q_down, bound, passed, keys, values, pool_keys, pool_values, near,
-    qs, sums, tops, norms, numbers, ks, vs, tails, bias, sems,
+    qs, sums, tops, norms, far_bias, ks, vs, tails, bias, sems,
 ):
     rows, width = qs.shape[0] // 2, qs.shape[1]
     group = rows // 2
@@ -244,8 +244,8 @@
     spot = Spot(position, cols, pool_blocks)
     for i in range(2):
         listed = numbers_of(tails[pl.ds(i * TILE, TILE), :], count)
-        numbers[pl.ds(i * TILE, TILE), :] = listed
         bias[pl.ds(2 * i, 2), :] = bias_of(listed, spot, ks.shape[0], True, group, pool_keys.shape[0])[:2]
+        far_bias[pl.ds(2 * i, 2), :] = bias_of(listed, spot, LANES, False, group, pool_keys.shape[0])[:2]
     scale = 1.0 / math.sqrt(width // HEADS)
     ones = jnp.ones((ks.shape[0], LANES), jnp.bfloat16)
     for head in range(HEADS):
@@ -269,7 +269,7 @@
     return pl.pallas_call(
         functools.partial(near_kernel, *shape),
         out_shape=[jax.ShapeDtypeStruct((2 * rows, width), kind) for kind in (bf16, f32, f32, f32)]
-        + [jax.ShapeDtypeStruct((2 * TILE, LANES), jnp.int32)],
+        + [jax.ShapeDtypeStruct((TILE, LANES), f32)],
         in_specs=[pl.BlockSpec(memory_space=place) for place in places],
         out_specs=[pl.BlockSpec(memory_space=pltpu.VMEM)] * 5,
         scratch_shapes=[
@@ -287,13 +287,8 @@
     )(position, q_up, q_down, bound, passed, keys, values, pool_keys, pool_values, near)
 
 
-def far_kernel(cols, pool_blocks, count, position, qs, sums, tops, norms, numbers, far, out_up, out_down, ks, vs, bias):
+def far_kernel(qs, sums, tops, norms, bias, far, out_up, out_down, ks, vs):
     edge = far.shape[0] // 2
-    spot = Spot(position, cols, pool_blocks)
-    half = out_up.shape[0] // 2
-    for i in range(2):
-        listed = numbers[pl.ds(i * TILE, TILE), :]
-        bias[pl.ds(2 * i, 2), :] = bias_of(listed, spot, LANES, False, half, edge - half)[:2]
     rows = out_up.shape[0]
     width = qs.shape[1]
     group = rows // 2
@@ -329,21 +324,21 @@
         outs[i // 2][spans[i % 2], pl.ds(width, LANES)] = (high.astype(jnp.float32) + middle + low).astype(jnp.bfloat16)
 
 
-def far_attention(shape, position, qs, sums, tops, norms, numbers, far):
+def far_attention(qs, sums, tops, norms, bias, far):
     rows, width = qs.shape[0] // 2, qs.shape[1]
     message = jax.ShapeDtypeStruct((rows, width + LANES), jnp.bfloat16)
     return pl.pallas_call(
-        functools.partial(far_kernel, *shape),
+        far_kernel,
         out_shape=(message, message),
-        in_specs=[pl.BlockSpec(memory_space=pltpu.SMEM)] + [pl.BlockSpec(memory_space=pltpu.VMEM)] * 6,
+        in_specs=[pl.BlockSpec(memory_space=pltpu.VMEM)] * 6,
         out_specs=[pl.BlockSpec(memory_space=pltpu.VMEM)] * 2,
-        scratch_shapes=[pltpu.VMEM((LANES, width), jnp.bfloat16)] * 2 + [pltpu.VMEM((TILE, LANES), jnp.float32)],
+        scratch_shapes=[pltpu.VMEM((LANES, width), jnp.bfloat16)] * 2,
         compiler_params=pltpu.CompilerParams(vmem_limit_bytes=3 << 20),
         cost_estimate=pl.CostEstimate(
             flops=4 * 2 * rows * LANES * width, bytes_accessed=4 << 20, transcendentals=2 * rows * LANES * HEADS
         ),
         name="far_attention",
-    )(position, qs, sums, tops, norms, numbers, far)
+    )(qs, sums, tops, norms, bias, far)
 
 
 def own_kernel(
@@ -522,7 +517,7 @@
     near_parts = near_attention(
         shape + (line,), position, q_up, q_down, bound, passed, kept_keys, kept_values, pk, pv, near
     )
-    to_up, to_down = far_attention(shape, position, *near_parts, far)
+    to_up, to_down = far_attention(*near_parts, far)
     below = send(to_up, up)
     above = send(to_down, down)
     mine = own_attention(shape, position, message, kept_keys, kept_values, pk, pv, near, far, top, top_other)

time: 115 us -> 115 us (level)
  no operation moved by 1% of the time
where the time goes in v4:
time: 115 us; the launch traced here: 114 us
  waiting for transfers between devices  54.8 us (48%)
  starting transfers between devices  40.6 us (35%)
  Pallas kernels  18.1 us (16%)
    ppermute x13, waiting for transfers between devices, send(): return lax.ppermute(block, AXES, links)  54.8 us
    ppermute x13, starting transfers between devices, send(): return lax.ppermute(block, AXES, links)  40.6 us
    pallas_call x1, Pallas kernels, own_attention(): pl.pallas_call(functools.partial(own_kernel, *shape), out_shape=[jax.Shap...  4.16 us
    pallas_call x2, Pallas kernels, packed(): pl.pallas_call(kernel, out_shape=[jax.ShapeDtypeStruct(shape, dtype) for...  3.84 us
    pallas_call x1, Pallas kernels, near_attention(): pl.pallas_call(functools.partial(near_kernel, *shape), out_shape=[jax.Sha...  3.61 us
    pallas_call x1, Pallas kernels, far_attention(): pl.pallas_call(far_kernel, out_shape=(message, message), in_specs=[pl.Blo...  2.82 us
    pallas_call x1, Pallas kernels, merge(): pl.pallas_call(functools.partial(merge_kernel, rows_in_all - 1), out_shap...  2.35 us
  transfers between devices with their start and end apart: 13, of which 6 were waited for; matrix products, arithmetic and copies ran while one was open for 0% of the time, Pallas kernels for 12%

profile of v4, /device:TPU:56, one launch (start us, length us, event | category | flops | bytes accessed | tf_op | source)
XLA Modules:
  0.0 114.4 jit_solution(5176393140693415025)
XLA Ops:
  0.8 2.0 %shard_map.82 = (bf16[192,2048]{1,0:T(8,128)(2,1)S(1)}, bf16[2,8,2048]{2,1,0:T(8,128)(2,1)S(1)}, bf16[136,2048]{1,0:T(8,128)(2,1)S(1)}, bf16[72,2048]{1,0:T(8,128)(2,1)S(1)}) custom-call(s32[2]{0:T(128)S(1)} %pad_add_fusion.position, s32[2,8]{1,0:T(2,128)S(1)} %bitcast.13, bf16[2,64,2048]{2,1,0:T(8,128)(2,1)} %bitcast.22, bf16[2,64,2048]{2,1,0:T(8,128)(2,1)} %bitcast.14, ...), custom_call_target="tpu_custom_call" | custom-call | tf_op jit(solution)/shard_map/pallas_call | solution.py:107
  2.8 3.5 %collective-permute-start.8 = (bf16[72,2048]{1,0:T(8,128)(2,1)S(1)}, bf16[72,2048]{1,0:T(8,128)(2,1)S(1)}, u32[]{:S(2)}, u32[]{:S(2)}) collective-permute-start(bf16[72,2048]{1,0:T(8,128)(2,1)S(1)} %get-tuple-element.26), channel_id=1, source_target_pairs={{112,128},{113,129},{114,130},{115,131},{116,132},{117,133},{118,1... | collective-permute-start | bytes 884744 | tf_op jit(solution)/shard_map/ppermute | solution.py:31
  6.3 1.8 %shard_map.83 = (bf16[192,2048]{1,0:T(8,128)(2,1)S(1)}, bf16[64,2048]{1,0:T(8,128)(2,1)S(1)}) custom-call(s32[2]{0:T(128)S(1)} %pad_add_fusion.position, bf16[2,64,2048]{2,1,0:T(8,128)(2,1)} %bitcast.23, bf16[2,64,2048]{2,1,0:T(8,128)(2,1)} %bitcast.15, bf16[2,64,2048]{2,1,0:T(8,128)(2,1)} %bitcast.19, bf16[32,2048]{1,0:T(8,128)(2,1)} %bitcast.25, ...), custom_call_target="tpu_custom_call" | custom-call | tf_op jit(solution)/shard_map/pallas_call | solution.py:107
  8.1 4.3 %collective-permute-start.9 = (bf16[64,2048]{1,0:T(8,128)(2,1)S(1)}, bf16[64,2048]{1,0:T(8,128)(2,1)S(1)}, u32[]{:S(2)}, u32[]{:S(2)}) collective-permute-start(bf16[64,2048]{1,0:T(8,128)(2,1)S(1)} %get-tuple-element.27), channel_id=1, source_target_pairs={{112,240},{113,241},{114,242},{115,243},{116,244},{117,245},{118,2... | collective-permute-start | bytes 786440 | tf_op jit(solution)/shard_map/ppermute | solution.py:31
  12.4 1.9 %collective-permute-start = (bf16[192,2048]{1,0:T(8,128)(2,1)S(1)}, bf16[192,2048]{1,0:T(8,128)(2,1)S(1)}, u32[]{:S(2)}, u32[]{:S(2)}) collective-permute-start(bf16[192,2048]{1,0:T(8,128)(2,1)S(1)} %get-tuple-element.21), channel_id=1, source_target_pairs={{0,1},{1,0},{2,3},{3,2},{4,5},{5,4},{6,7},{7,6},{8,9},{9,8},{10,11... | collective-permute-start | bytes 2359304 | tf_op jit(solution)/shard_map/ppermute | solution.py:31
  14.3 3.4 %collective-permute-start.2 = (bf16[2,8,2048]{2,1,0:T(8,128)(2,1)S(1)}, bf16[2,8,2048]{2,1,0:T(8,128)(2,1)S(1)}, u32[]{:S(2)}, u32[]{:S(2)}) collective-permute-start(bf16[2,8,2048]{2,1,0:T(8,128)(2,1)S(1)} %get-tuple-element.23.first), channel_id=1, source_target_pairs={{0,4},{1,5},{2,6},{3,7},{4,0},{5,1},{6,2},{7,3},{8,12},{9,13},{10,... | collective-permute-start | bytes 196616 | tf_op jit(solution)/shard_map/ppermute | solution.py:31
  18.5 2.3 %collective-permute-done.2.second = bf16[2,8,2048]{2,1,0:T(8,128)(2,1)S(1)} collective-permute-done((bf16[2,8,2048]{2,1,0:T(8,128)(2,1)S(1)}, bf16[2,8,2048]{2,1,0:T(8,128)(2,1)S(1)}, u32[]{:S(2)}, u32[]{:S(2)}) %collective-permute-start.2) | collective-permute-done | bytes 65568 | tf_op jit(solution)/shard_map/ppermute | solution.py:31
  20.9 10.0 %collective-permute-start.3 = (bf16[2,16,2048]{2,1,0:T(8,128)(2,1)S(1)}, bf16[2,16,2048]{2,1,0:T(8,128)(2,1)S(1)}, u32[]{:S(2)}, u32[]{:S(2)}) collective-permute-start(bf16[2,16,2048]{2,1,0:T(8,128)(2,1)S(1)} %join.3.first), channel_id=1, source_target_pairs={{0,8},{1,9},{2,10},{3,11},{4,12},{5,13},{6,14},{7,15},{8,0},{9,1},... | collective-permute-start | bytes 393224 | tf_op jit(solution)/shard_map/ppermute | solution.py:31
  30.9 5.5 %collective-permute-done.3.second = bf16[2,16,2048]{2,1,0:T(8,128)(2,1)S(1)} collective-permute-done((bf16[2,16,2048]{2,1,0:T(8,128)(2,1)S(1)}, bf16[2,16,2048]{2,1,0:T(8,128)(2,1)S(1)}, u32[]{:S(2)}, u32[]{:S(2)}) %collective-permute-start.3) | collective-permute-done | bytes 131104 | tf_op jit(solution)/shard_map/ppermute | solution.py:31
  36.4 1.3 %collective-permute-start.6 = (bf16[136,2048]{1,0:T(8,128)(2,1)S(1)}, bf16[136,2048]{1,0:T(8,128)(2,1)S(1)}, u32[]{:S(2)}, u32[]{:S(2)}) collective-permute-start(bf16[136,2048]{1,0:T(8,128)(2,1)S(1)} %get-tuple-element.20.message), channel_id=1, source_target_pairs={{0,16},{1,17},{2,18},{3,19},{4,20},{5,21},{6,22},{7,23},{8,24},{9,... | collective-permute-start | bytes 1671176 | tf_op jit(solution)/shard_map/ppermute | solution.py:31
  37.7 4.6 %collective-permute-start.7 = (bf16[136,2048]{1,0:T(8,128)(2,1)S(1)}, bf16[136,2048]{1,0:T(8,128)(2,1)S(1)}, u32[]{:S(2)}, u32[]{:S(2)}) collective-permute-start(bf16[136,2048]{1,0:T(8,128)(2,1)S(1)} %get-tuple-element.20.message), channel_id=1, source_target_pairs={{16,0},{17,1},{18,2},{19,3},{20,4},{21,5},{22,6},{23,7},{24,8},{25... | collective-permute-start | bytes 1671176 | tf_op jit(solution)/shard_map/ppermute | solution.py:31
  42.7 1.9 %collective-permute-start.4 = (bf16[2,32,2048]{2,1,0:T(8,128)(2,1)S(1)}, bf16[2,32,2048]{2,1,0:T(8,128)(2,1)S(1)}, u32[]{:S(2)}, u32[]{:S(2)}) collective-permute-start(bf16[2,32,2048]{2,1,0:T(8,128)(2,1)S(1)} %join.4.first), channel_id=1, source_target_pairs={{0,386},{1,387},{2,384},{3,385},{4,390},{5,391},{6,388},{7,389},{8... | collective-permute-start | bytes 786440 | tf_op jit(solution)/shard_map/ppermute | solution.py:31
  44.6 26.8 %collective-permute-done.4.second = bf16[2,32,2048]{2,1,0:T(8,128)(2,1)S(1)} collective-permute-done((bf16[2,32,2048]{2,1,0:T(8,128)(2,1)S(1)}, bf16[2,32,2048]{2,1,0:T(8,128)(2,1)S(1)}, u32[]{:S(2)}, u32[]{:S(2)}) %collective-permute-start.4) | collective-permute-done | bytes 262176 | tf_op jit(solution)/shard_map/ppermute | solution.py:31
  71.4 1.3 %collective-permute-start.10 = (bf16[64,2048]{1,0:T(8,128)(2,1)S(1)}, bf16[64,2048]{1,0:T(8,128)(2,1)S(1)}, u32[]{:S(2)}, u32[]{:S(2)}) collective-permute-start(bf16[64,2048]{1,0:T(8,128)(2,1)S(1)} %collective-permute-done.9), channel_id=1, source_target_pairs={{0,112},{1,113},{2,114},{3,115},{4,116},{5,117},{6,118},{7,119},{8... | collective-permute-start | bytes 786440 | tf_op jit(solution)/shard_map/ppermute | solution.py:31
  73.4 9.3 %collective-permute-done.10.passed = bf16[64,2048]{1,0:T(8,128)(2,1)S(1)} collective-permute-done((bf16[64,2048]{1,0:T(8,128)(2,1)S(1)}, bf16[64,2048]{1,0:T(8,128)(2,1)S(1)}, u32[]{:S(2)}, u32[]{:S(2)}) %collective-permute-start.10) | collective-permute-done | bytes 262176 | tf_op jit(solution)/shard_map/ppermute | solution.py:31
  82.7 1.9 %collective-permute-start.5 = (bf16[2,64,2048]{2,1,0:T(8,128)(2,1)S(1)}, bf16[2,64,2048]{2,1,0:T(8,128)(2,1)S(1)}, u32[]{:S(2)}, u32[]{:S(2)}) collective-permute-start(bf16[2,64,2048]{2,1,0:T(8,128)(2,1)S(1)} %join.5.top_a), channel_id=1, source_target_pairs={{0,1},{1,0},{2,3},{3,2},{4,5},{5,4},{6,7},{7,6},{8,9},{9,8},{10,11... | collective-permute-start | bytes 1572872 | tf_op jit(solution)/shard_map/ppermute | solution.py:31
  84.7 3.6 %near_attention.1 = (bf16[256,2048]{1,0:T(8,128)(2,1)S(1)}, f32[256,2048]{1,0:T(8,128)S(1)}, f32[256,2048]{1,0:T(8,128)S(1)}, f32[256,2048]{1,0:T(8,128)S(1)}, f32[8,128]{1,0:T(8,128)S(1)}) custom-call(s32[2]{0:T(128)S(1)} %pad_add_fusion.position, bf16[136,2048]{1,0:T(8,128)(2,1)S(1)} %collective-permute-done.6.q_up, ...), custom_call_target="tpu_custom_call" | custom-call | flops 536870912 | bytes 4194304 | tf_op jit(solution)/shard_map/near_attention/pallas_call | solution.py:269
  88.3 2.8 %far_attention.1 = (bf16[128,2176]{1,0:T(8,128)(2,1)S(1)}, bf16[128,2176]{1,0:T(8,128)(2,1)S(1)}) custom-call(bf16[256,2048]{1,0:T(8,128)(2,1)S(1)} %get-tuple-element.28.qs, f32[256,2048]{1,0:T(8,128)S(1)} %get-tuple-element.29.sums, f32[256,2048]{1,0:T(8,128)S(1)} %get-tuple-element.30.tops, f32[256,2048]{1,0:T(8,128)S(1)} %get-tuple-element.31.norms, ...), custom_call_target="tpu_custom_call" | custom-call | flops 268435456 | bytes 4194304 | tf_op jit(solution)/shard_map/far_attention/pallas_call | solution.py:330
  91.1 1.9 %collective-permute-start.11 = (bf16[128,2176]{1,0:T(8,128)(2,1)S(1)}, bf16[128,2176]{1,0:T(8,128)(2,1)S(1)}, u32[]{:S(2)}, u32[]{:S(2)}) collective-permute-start(bf16[128,2176]{1,0:T(8,128)(2,1)S(1)} %get-tuple-element.33), channel_id=1, source_target_pairs={{0,16},{1,17},{2,18},{3,19},{4,20},{5,21},{6,22},{7,23},{8,24},{9,... | collective-permute-start | bytes 1671176 | tf_op jit(solution)/shard_map/ppermute | solution.py:31
  93.1 3.9 %collective-permute-start.12 = (bf16[128,2176]{1,0:T(8,128)(2,1)S(1)}, bf16[128,2176]{1,0:T(8,128)(2,1)S(1)}, u32[]{:S(2)}, u32[]{:S(2)}) collective-permute-start(bf16[128,2176]{1,0:T(8,128)(2,1)S(1)} %get-tuple-element.34), channel_id=1, source_target_pairs={{16,0},{17,1},{18,2},{19,3},{20,4},{21,5},{22,6},{23,7},{24,8},{25... | collective-permute-start | bytes 1671176 | tf_op jit(solution)/shard_map/ppermute | solution.py:31
  97.0 4.2 %own_attention.1 = (f32[128,2048]{1,0:T(8,128)S(1)}, f32[128,2048]{1,0:T(8,128)S(1)}) custom-call(s32[2]{0:T(128)S(1)} %pad_add_fusion.position, bf16[136,2048]{1,0:T(8,128)(2,1)S(1)} %get-tuple-element.20.message, bf16[128,2048]{1,0:T(8,128)(2,1)} %bitcast.17, bf16[128,2048]{1,0:T(8,128)(2,1)} %bitcast.21, bf16[32,2048]{1,0:T(8,128)(2,1)} %bitcast.27, ...), custom_call_target="tpu_custom_call" | custom-call | flops 536870912 | bytes 4194304 | tf_op jit(solution)/shard_map/own_attention/pallas_call | solution.py:393
  101.2 6.9 %collective-permute-done.11.above = bf16[128,2176]{1,0:T(8,128)(2,1)S(1)} collective-permute-done((bf16[128,2176]{1,0:T(8,128)(2,1)S(1)}, bf16[128,2176]{1,0:T(8,128)(2,1)S(1)}, u32[]{:S(2)}, u32[]{:S(2)}) %collective-permute-start.11) | collective-permute-done | bytes 557088 | tf_op jit(solution)/shard_map/ppermute | solution.py:31
  108.0 4.0 %collective-permute-done.12.below = bf16[128,2176]{1,0:T(8,128)(2,1)S(1)} collective-permute-done((bf16[128,2176]{1,0:T(8,128)(2,1)S(1)}, bf16[128,2176]{1,0:T(8,128)(2,1)S(1)}, u32[]{:S(2)}, u32[]{:S(2)}) %collective-permute-start.12) | collective-permute-done | bytes 557088 | tf_op jit(solution)/shard_map/ppermute | solution.py:31
  112.1 2.4 %merge.1 = bf16[128,2048]{1,0:T(8,128)(2,1)} custom-call(s32[2]{0:T(128)S(1)} %pad_add_fusion.position, f32[128,2048]{1,0:T(8,128)S(1)} %get-tuple-element.24.own, f32[128,2048]{1,0:T(8,128)S(1)} %get-tuple-element.25.own_logs, bf16[128,2176]{1,0:T(8,128)(2,1)S(1)} %collective-permute-done.11.above, bf16[128,2176]{1,0:T(8,128)(2,1)S(1)} %collective-permute-done.12.below), custom_call_target="tpu_custom_call" | custom-call | tf_op jit(solution)/shard_map/merge/pallas_call | solution.py:435
  (14 shorter events, 2.8 us)
Async XLA Ops:
  0.1 0.7 copy-start
  2.8 39.9 %collective-permute-start.8 = (bf16[72,2048]{1,0:T(8,128)(2,1)S(1)}, bf16[72,2048]{1,0:T(8,128)(2,1)S(1)}, u32[]{:S(2)}, u32[]{:S(2)}) collective-permute-start(bf16[72,2048]{1,0:T(8,128)(2,1)S(1)} %get-tuple-element.26), channel_id=1, source_target_pairs={{112,128},{113,129},{114,130},{115,131},{116,132},{117,133},{118,1... | collective-permute-start | bytes 884744 | tf_op jit(solution)/shard_map/ppermute | solution.py:31
  8.1 29.6 %collective-permute-start.9 = (bf16[64,2048]{1,0:T(8,128)(2,1)S(1)}, bf16[64,2048]{1,0:T(8,128)(2,1)S(1)}, u32[]{:S(2)}, u32[]{:S(2)}) collective-permute-start(bf16[64,2048]{1,0:T(8,128)(2,1)S(1)} %get-tuple-element.27), channel_id=1, source_target_pairs={{112,240},{113,241},{114,242},{115,243},{116,244},{117,245},{118,2... | collective-permute-start | bytes 786440 | tf_op jit(solution)/shard_map/ppermute | solution.py:31
  12.4 72.3 %collective-permute-start = (bf16[192,2048]{1,0:T(8,128)(2,1)S(1)}, bf16[192,2048]{1,0:T(8,128)(2,1)S(1)}, u32[]{:S(2)}, u32[]{:S(2)}) collective-permute-start(bf16[192,2048]{1,0:T(8,128)(2,1)S(1)} %get-tuple-element.21), channel_id=1, source_target_pairs={{0,1},{1,0},{2,3},{3,2},{4,5},{5,4},{6,7},{7,6},{8,9},{9,8},{10,11... | collective-permute-start | bytes 2359304 | tf_op jit(solution)/shard_map/ppermute | solution.py:31
  14.3 6.4 %collective-permute-start.2 = (bf16[2,8,2048]{2,1,0:T(8,128)(2,1)S(1)}, bf16[2,8,2048]{2,1,0:T(8,128)(2,1)S(1)}, u32[]{:S(2)}, u32[]{:S(2)}) collective-permute-start(bf16[2,8,2048]{2,1,0:T(8,128)(2,1)S(1)} %get-tuple-element.23.first), channel_id=1, source_target_pairs={{0,4},{1,5},{2,6},{3,7},{4,0},{5,1},{6,2},{7,3},{8,12},{9,13},{10,... | collective-permute-start | bytes 196616 | tf_op jit(solution)/shard_map/ppermute | solution.py:31
  17.7 70.6 %collective-permute-start.1 = (bf16[192,2048]{1,0:T(8,128)(2,1)S(1)}, bf16[192,2048]{1,0:T(8,128)(2,1)S(1)}, u32[]{:S(2)}, u32[]{:S(2)}) collective-permute-start(bf16[192,2048]{1,0:T(8,128)(2,1)S(1)} %get-tuple-element.22), channel_id=1, source_target_pairs={{1,2},{2,1},{3,4},{4,3},{5,6},{6,5},{7,8},{8,7},{9,10},{10,9},{11,... | collective-permute-start | bytes 2359304 | tf_op jit(solution)/shard_map/ppermute | solution.py:31
  20.9 15.5 %collective-permute-start.3 = (bf16[2,16,2048]{2,1,0:T(8,128)(2,1)S(1)}, bf16[2,16,2048]{2,1,0:T(8,128)(2,1)S(1)}, u32[]{:S(2)}, u32[]{:S(2)}) collective-permute-start(bf16[2,16,2048]{2,1,0:T(8,128)(2,1)S(1)} %join.3.first), channel_id=1, source_target_pairs={{0,8},{1,9},{2,10},{3,11},{4,12},{5,13},{6,14},{7,15},{8,0},{9,1},... | collective-permute-start | bytes 393224 | tf_op jit(solution)/shard_map/ppermute | solution.py:31
  36.4 48.2 %collective-permute-start.6 = (bf16[136,2048]{1,0:T(8,128)(2,1)S(1)}, bf16[136,2048]{1,0:T(8,128)(2,1)S(1)}, u32[]{:S(2)}, u32[]{:S(2)}) collective-permute-start(bf16[136,2048]{1,0:T(8,128)(2,1)S(1)} %get-tuple-element.20.message), channel_id=1, source_target_pairs={{0,16},{1,17},{2,18},{3,19},{4,20},{5,21},{6,22},{7,23},{8,24},{9,... | collective-permute-start | bytes 1671176 | tf_op jit(solution)/shard_map/ppermute | solution.py:31
  37.7 47.0 %collective-permute-start.7 = (bf16[136,2048]{1,0:T(8,128)(2,1)S(1)}, bf16[136,2048]{1,0:T(8,128)(2,1)S(1)}, u32[]{:S(2)}, u32[]{:S(2)}) collective-permute-start(bf16[136,2048]{1,0:T(8,128)(2,1)S(1)} %get-tuple-element.20.message), channel_id=1, source_target_pairs={{16,0},{17,1},{18,2},{19,3},{20,4},{21,5},{22,6},{23,7},{24,8},{25... | collective-permute-start | bytes 1671176 | tf_op jit(solution)/shard_map/ppermute | solution.py:31
  42.7 28.7 %collective-permute-start.4 = (bf16[2,32,2048]{2,1,0:T(8,128)(2,1)S(1)}, bf16[2,32,2048]{2,1,0:T(8,128)(2,1)S(1)}, u32[]{:S(2)}, u32[]{:S(2)}) collective-permute-start(bf16[2,32,2048]{2,1,0:T(8,128)(2,1)S(1)} %join.4.first), channel_id=1, source_target_pairs={{0,386},{1,387},{2,384},{3,385},{4,390},{5,391},{6,388},{7,389},{8... | collective-permute-start | bytes 786440 | tf_op jit(solution)/shard_map/ppermute | solution.py:31
  71.4 11.3 %collective-permute-start.10 = (bf16[64,2048]{1,0:T(8,128)(2,1)S(1)}, bf16[64,2048]{1,0:T(8,128)(2,1)S(1)}, u32[]{:S(2)}, u32[]{:S(2)}) collective-permute-start(bf16[64,2048]{1,0:T(8,128)(2,1)S(1)} %collective-permute-done.9), channel_id=1, source_target_pairs={{0,112},{1,113},{2,114},{3,115},{4,116},{5,117},{6,118},{7,119},{8... | collective-permute-start | bytes 786440 | tf_op jit(solution)/shard_map/ppermute | solution.py:31
  82.7 14.3 %collective-permute-start.5 = (bf16[2,64,2048]{2,1,0:T(8,128)(2,1)S(1)}, bf16[2,64,2048]{2,1,0:T(8,128)(2,1)S(1)}, u32[]{:S(2)}, u32[]{:S(2)}) collective-permute-start(bf16[2,64,2048]{2,1,0:T(8,128)(2,1)S(1)} %join.5.top_a), channel_id=1, source_target_pairs={{0,1},{1,0},{2,3},{3,2},{4,5},{5,4},{6,7},{7,6},{8,9},{9,8},{10,11... | collective-permute-start | bytes 1572872 | tf_op jit(solution)/shard_map/ppermute | solution.py:31
  91.1 16.9 %collective-permute-start.11 = (bf16[128,2176]{1,0:T(8,128)(2,1)S(1)}, bf16[128,2176]{1,0:T(8,128)(2,1)S(1)}, u32[]{:S(2)}, u32[]{:S(2)}) collective-permute-start(bf16[128,2176]{1,0:T(8,128)(2,1)S(1)} %get-tuple-element.33), channel_id=1, source_target_pairs={{0,16},{1,17},{2,18},{3,19},{4,20},{5,21},{6,22},{7,23},{8,24},{9,... | collective-permute-start | bytes 1671176 | tf_op jit(solution)/shard_map/ppermute | solution.py:31
  93.1 19.0 %collective-permute-start.12 = (bf16[128,2176]{1,0:T(8,128)(2,1)S(1)}, bf16[128,2176]{1,0:T(8,128)(2,1)S(1)}, u32[]{:S(2)}, u32[]{:S(2)}) collective-permute-start(bf16[128,2176]{1,0:T(8,128)(2,1)S(1)} %get-tuple-element.34), channel_id=1, source_target_pairs={{16,0},{17,1},{18,2},{19,3},{20,4},{21,5},{22,6},{23,7},{24,8},{25... | collective-permute-start | bytes 1671176 | tf_op jit(solution)/shard_map/ppermute | solution.py:31

commit v5 on v4

--- a/solution.py
+++ b/solution.py
@@ -13,6 +13,7 @@
 NEG_FILL = -1e30
 AXES = ("row", "col")
 LANES = 128
+LOG2E = math.log2(math.e)
 TILE = 8
 BASE = 256
 
@@ -192,7 +193,7 @@
     return jnp.where(listed > 0, 0.0, NEG_FILL)
 
 
-def weigh(scores, bias, group, before=None):
+def weigh(scores, bias, group, rate, before=None):
     peaks, weights = [], []
     for i in range(scores.shape[0] // group):
         piece = scores[i * group : (i + 1) * group] + bias[pl.ds(i, 1), :]
@@ -200,7 +201,7 @@
         if before is not None:
             peak = jnp.maximum(before[i], peak)
         peaks.append(peak)
-        weights.append(jnp.exp(piece - peak).astype(jnp.bfloat16))
+        weights.append(jnp.exp2((piece - peak) * rate).astype(jnp.bfloat16))
     return peaks, jnp.concatenate(weights, axis=0)
 
 
@@ -250,8 +251,8 @@
     ones = jnp.ones((ks.shape[0], LANES), jnp.bfloat16)
     for head in range(HEADS):
         part = pl.ds(head * LANES, LANES)
-        scores = lax.dot_general(qs[:, part], ks[:, part], NT, preferred_element_type=jnp.float32) * scale
-        peaks, weights = weigh(scores, bias, group)
+        scores = lax.dot_general(qs[:, part], ks[:, part], NT, preferred_element_type=jnp.float32)
+        peaks, weights = weigh(scores, bias, group, scale * LOG2E)
         value = jnp.concatenate([vs[:, part], ones], axis=1)
         summed = jnp.dot(weights, value, preferred_element_type=jnp.float32)
         sums[:, part] = summed[:, :LANES]
@@ -304,13 +305,13 @@
     spans = [pl.ds(i * group, group) for i in range(4)]
     for head in range(HEADS):
         part = pl.ds(head * LANES, LANES)
-        scores = lax.dot_general(qs[:, part], ks[:, part], NT, preferred_element_type=jnp.float32) * scale
+        scores = lax.dot_general(qs[:, part], ks[:, part], NT, preferred_element_type=jnp.float32)
         before = [tops[span, part] for span in spans]
-        peaks, weights = weigh(scores, bias, group, before)
+        peaks, weights = weigh(scores, bias, group, scale * LOG2E, before)
         value = jnp.concatenate([vs[:, part], ones], axis=1)
         summed = jnp.dot(weights, value, preferred_element_type=jnp.float32)
         for i, span in enumerate(spans):
-            factor = jnp.exp(before[i] - peaks[i])
+            factor = jnp.exp2((before[i] - peaks[i]) * (scale * LOG2E))
             piece = summed[i * group : (i + 1) * group]
             norm = norms[span, part] * factor + piece[:, LANES:]
             result = (sums[span, part] * factor + piece[:, :LANES]) / norm
@@ -318,7 +319,7 @@
             kept_peak[i] = jnp.where(lane == head, peaks[i], kept_peak[i])
             kept_norm[i] = jnp.where(lane == head, norm, kept_norm[i])
     for i in range(4):
-        high, middle, low = split_in_three(kept_peak[i] + jnp.log(kept_norm[i]))
+        high, middle, low = split_in_three(kept_peak[i] * scale + jnp.log(kept_norm[i]))
         middle = pltpu.roll(middle.astype(jnp.float32), HEADS, 1)
         low = pltpu.roll(low.astype(jnp.float32), 2 * HEADS, 1)
         outs[i // 2][spans[i % 2], pl.ds(width, LANES)] = (high.astype(jnp.float32) + middle + low).astype(jnp.bfloat16)
@@ -373,15 +374,15 @@
     ones = jnp.ones((ks.shape[0], LANES), jnp.bfloat16)
     for head in range(HEADS):
         part = pl.ds(head * LANES, LANES)
-        scores = lax.dot_general(qs[:, part], ks[:, part], NT, preferred_element_type=jnp.float32) * scale
-        peaks, weights = weigh(scores, bias, group)
+        scores = lax.dot_general(qs[:, part], ks[:, part], NT, preferred_element_type=jnp.float32)
+        peaks, weights = weigh(scores, bias, group, scale * LOG2E)
         value = jnp.concatenate([vs[:, part], ones], axis=1)
         summed = jnp.dot(weights, value, preferred_element_type=jnp.float32)
         norm = summed[:, LANES:]
         out[:, part] = summed[:, :LANES] / norm
         for i, peak in enumerate(peaks):
             span = pl.ds(i * group, group)
-            logs[span, part] = peak + jnp.log(norm[i * group : (i + 1) * group])
+            logs[span, part] = peak * scale + jnp.log(norm[i * group : (i + 1) * group])
 
 
 def own_attention(shape, position, message, keys, values, pool_keys, pool_values, near, far, top_a, top_b):

time: 115 us -> 115 us (level)
  no operation moved by 1% of the time
where the time goes in v5:
time: 115 us; the launch traced here: 114 us
  waiting for transfers between devices  55 us (48%)
  starting transfers between devices  40.6 us (35%)
  Pallas kernels  17.9 us (16%)
    ppermute x13, waiting for transfers between devices, send(): return lax.ppermute(block, AXES, links)  55 us
    ppermute x13, starting transfers between devices, send(): return lax.ppermute(block, AXES, links)  40.6 us
    pallas_call x1, Pallas kernels, own_attention(): pl.pallas_call(functools.partial(own_kernel, *shape), out_shape=[jax.Shap...  4.03 us
    pallas_call x2, Pallas kernels, packed(): pl.pallas_call(kernel, out_shape=[jax.ShapeDtypeStruct(shape, dtype) for...  3.84 us
    pallas_call x1, Pallas kernels, near_attention(): pl.pallas_call(functools.partial(near_kernel, *shape), out_shape=[jax.Sha...  3.6 us
    pallas_call x1, Pallas kernels, far_attention(): pl.pallas_call(far_kernel, out_shape=(message, message), in_specs=[pl.Blo...  2.81 us
    pallas_call x1, Pallas kernels, merge(): pl.pallas_call(functools.partial(merge_kernel, rows_in_all - 1), out_shap...  2.35 us
  transfers between devices with their start and end apart: 13, of which 6 were waited for; matrix products, arithmetic and copies ran while one was open for 0% of the time, Pallas kernels for 12%

profile of v5, /device:TPU:56, one launch (start us, length us, event | category | flops | bytes accessed | tf_op | source)
XLA Modules:
  0.0 114.4 jit_solution(5695380379588687516)
XLA Ops:
  0.8 2.0 %shard_map.82 = (bf16[192,2048]{1,0:T(8,128)(2,1)S(1)}, bf16[2,8,2048]{2,1,0:T(8,128)(2,1)S(1)}, bf16[136,2048]{1,0:T(8,128)(2,1)S(1)}, bf16[72,2048]{1,0:T(8,128)(2,1)S(1)}) custom-call(s32[2]{0:T(128)S(1)} %pad_add_fusion.position, s32[2,8]{1,0:T(2,128)S(1)} %bitcast.13, bf16[2,64,2048]{2,1,0:T(8,128)(2,1)} %bitcast.22, bf16[2,64,2048]{2,1,0:T(8,128)(2,1)} %bitcast.14, ...), custom_call_target="tpu_custom_call" | custom-call | tf_op jit(solution)/shard_map/pallas_call | solution.py:108
  2.8 3.5 %collective-permute-start.8 = (bf16[72,2048]{1,0:T(8,128)(2,1)S(1)}, bf16[72,2048]{1,0:T(8,128)(2,1)S(1)}, u32[]{:S(2)}, u32[]{:S(2)}) collective-permute-start(bf16[72,2048]{1,0:T(8,128)(2,1)S(1)} %get-tuple-element.26), channel_id=1, source_target_pairs={{112,128},{113,129},{114,130},{115,131},{116,132},{117,133},{118,1... | collective-permute-start | bytes 884744 | tf_op jit(solution)/shard_map/ppermute | solution.py:32
  6.3 1.8 %shard_map.83 = (bf16[192,2048]{1,0:T(8,128)(2,1)S(1)}, bf16[64,2048]{1,0:T(8,128)(2,1)S(1)}) custom-call(s32[2]{0:T(128)S(1)} %pad_add_fusion.position, bf16[2,64,2048]{2,1,0:T(8,128)(2,1)} %bitcast.23, bf16[2,64,2048]{2,1,0:T(8,128)(2,1)} %bitcast.15, bf16[2,64,2048]{2,1,0:T(8,128)(2,1)} %bitcast.19, bf16[32,2048]{1,0:T(8,128)(2,1)} %bitcast.25, ...), custom_call_target="tpu_custom_call" | custom-call | tf_op jit(solution)/shard_map/pallas_call | solution.py:108
  8.1 4.3 %collective-permute-start.9 = (bf16[64,2048]{1,0:T(8,128)(2,1)S(1)}, bf16[64,2048]{1,0:T(8,128)(2,1)S(1)}, u32[]{:S(2)}, u32[]{:S(2)}) collective-permute-start(bf16[64,2048]{1,0:T(8,128)(2,1)S(1)} %get-tuple-element.27), channel_id=1, source_target_pairs={{112,240},{113,241},{114,242},{115,243},{116,244},{117,245},{118,2... | collective-permute-start | bytes 786440 | tf_op jit(solution)/shard_map/ppermute | solution.py:32
  12.4 1.9 %collective-permute-start = (bf16[192,2048]{1,0:T(8,128)(2,1)S(1)}, bf16[192,2048]{1,0:T(8,128)(2,1)S(1)}, u32[]{:S(2)}, u32[]{:S(2)}) collective-permute-start(bf16[192,2048]{1,0:T(8,128)(2,1)S(1)} %get-tuple-element.21), channel_id=1, source_target_pairs={{0,1},{1,0},{2,3},{3,2},{4,5},{5,4},{6,7},{7,6},{8,9},{9,8},{10,11... | collective-permute-start | bytes 2359304 | tf_op jit(solution)/shard_map/ppermute | solution.py:32
  14.3 3.4 %collective-permute-start.2 = (bf16[2,8,2048]{2,1,0:T(8,128)(2,1)S(1)}, bf16[2,8,2048]{2,1,0:T(8,128)(2,1)S(1)}, u32[]{:S(2)}, u32[]{:S(2)}) collective-permute-start(bf16[2,8,2048]{2,1,0:T(8,128)(2,1)S(1)} %get-tuple-element.23.first), channel_id=1, source_target_pairs={{0,4},{1,5},{2,6},{3,7},{4,0},{5,1},{6,2},{7,3},{8,12},{9,13},{10,... | collective-permute-start | bytes 196616 | tf_op jit(solution)/shard_map/ppermute | solution.py:32
  18.5 2.3 %collective-permute-done.2.second = bf16[2,8,2048]{2,1,0:T(8,128)(2,1)S(1)} collective-permute-done((bf16[2,8,2048]{2,1,0:T(8,128)(2,1)S(1)}, bf16[2,8,2048]{2,1,0:T(8,128)(2,1)S(1)}, u32[]{:S(2)}, u32[]{:S(2)}) %collective-permute-start.2) | collective-permute-done | bytes 65568 | tf_op jit(solution)/shard_map/ppermute | solution.py:32
  20.9 10.0 %collective-permute-start.3 = (bf16[2,16,2048]{2,1,0:T(8,128)(2,1)S(1)}, bf16[2,16,2048]{2,1,0:T(8,128)(2,1)S(1)}, u32[]{:S(2)}, u32[]{:S(2)}) collective-permute-start(bf16[2,16,2048]{2,1,0:T(8,128)(2,1)S(1)} %join.3.first), channel_id=1, source_target_pairs={{0,8},{1,9},{2,10},{3,11},{4,12},{5,13},{6,14},{7,15},{8,0},{9,1},... | collective-permute-start | bytes 393224 | tf_op jit(solution)/shard_map/ppermute | solution.py:32
  30.9 5.5 %collective-permute-done.3.second = bf16[2,16,2048]{2,1,0:T(8,128)(2,1)S(1)} collective-permute-done((bf16[2,16,2048]{2,1,0:T(8,128)(2,1)S(1)}, bf16[2,16,2048]{2,1,0:T(8,128)(2,1)S(1)}, u32[]{:S(2)}, u32[]{:S(2)}) %collective-permute-start.3) | collective-permute-done | bytes 131104 | tf_op jit(solution)/shard_map/ppermute | solution.py:32
  36.4 1.3 %collective-permute-start.6 = (bf16[136,2048]{1,0:T(8,128)(2,1)S(1)}, bf16[136,2048]{1,0:T(8,128)(2,1)S(1)}, u32[]{:S(2)}, u32[]{:S(2)}) collective-permute-start(bf16[136,2048]{1,0:T(8,128)(2,1)S(1)} %get-tuple-element.20.message), channel_id=1, source_target_pairs={{0,16},{1,17},{2,18},{3,19},{4,20},{5,21},{6,22},{7,23},{8,24},{9,... | collective-permute-start | bytes 1671176 | tf_op jit(solution)/shard_map/ppermute | solution.py:32
  37.7 4.6 %collective-permute-start.7 = (bf16[136,2048]{1,0:T(8,128)(2,1)S(1)}, bf16[136,2048]{1,0:T(8,128)(2,1)S(1)}, u32[]{:S(2)}, u32[]{:S(2)}) collective-permute-start(bf16[136,2048]{1,0:T(8,128)(2,1)S(1)} %get-tuple-element.20.message), channel_id=1, source_target_pairs={{16,0},{17,1},{18,2},{19,3},{20,4},{21,5},{22,6},{23,7},{24,8},{25... | collective-permute-start | bytes 1671176 | tf_op jit(solution)/shard_map/ppermute | solution.py:32
  42.7 1.9 %collective-permute-start.4 = (bf16[2,32,2048]{2,1,0:T(8,128)(2,1)S(1)}, bf16[2,32,2048]{2,1,0:T(8,128)(2,1)S(1)}, u32[]{:S(2)}, u32[]{:S(2)}) collective-permute-start(bf16[2,32,2048]{2,1,0:T(8,128)(2,1)S(1)} %join.4.first), channel_id=1, source_target_pairs={{0,386},{1,387},{2,384},{3,385},{4,390},{5,391},{6,388},{7,389},{8... | collective-permute-start | bytes 786440 | tf_op jit(solution)/shard_map/ppermute | solution.py:32
  44.6 26.8 %collective-permute-done.4.second = bf16[2,32,2048]{2,1,0:T(8,128)(2,1)S(1)} collective-permute-done((bf16[2,32,2048]{2,1,0:T(8,128)(2,1)S(1)}, bf16[2,32,2048]{2,1,0:T(8,128)(2,1)S(1)}, u32[]{:S(2)}, u32[]{:S(2)}) %collective-permute-start.4) | collective-permute-done | bytes 262176 | tf_op jit(solution)/shard_map/ppermute | solution.py:32
  71.4 1.3 %collective-permute-start.10 = (bf16[64,2048]{1,0:T(8,128)(2,1)S(1)}, bf16[64,2048]{1,0:T(8,128)(2,1)S(1)}, u32[]{:S(2)}, u32[]{:S(2)}) collective-permute-start(bf16[64,2048]{1,0:T(8,128)(2,1)S(1)} %collective-permute-done.9), channel_id=1, source_target_pairs={{0,112},{1,113},{2,114},{3,115},{4,116},{5,117},{6,118},{7,119},{8... | collective-permute-start | bytes 786440 | tf_op jit(solution)/shard_map/ppermute | solution.py:32
  73.4 9.3 %collective-permute-done.10.passed = bf16[64,2048]{1,0:T(8,128)(2,1)S(1)} collective-permute-done((bf16[64,2048]{1,0:T(8,128)(2,1)S(1)}, bf16[64,2048]{1,0:T(8,128)(2,1)S(1)}, u32[]{:S(2)}, u32[]{:S(2)}) %collective-permute-start.10) | collective-permute-done | bytes 262176 | tf_op jit(solution)/shard_map/ppermute | solution.py:32
  82.7 1.9 %collective-permute-start.5 = (bf16[2,64,2048]{2,1,0:T(8,128)(2,1)S(1)}, bf16[2,64,2048]{2,1,0:T(8,128)(2,1)S(1)}, u32[]{:S(2)}, u32[]{:S(2)}) collective-permute-start(bf16[2,64,2048]{2,1,0:T(8,128)(2,1)S(1)} %join.5.top_a), channel_id=1, source_target_pairs={{0,1},{1,0},{2,3},{3,2},{4,5},{5,4},{6,7},{7,6},{8,9},{9,8},{10,11... | collective-permute-start | bytes 1572872 | tf_op jit(solution)/shard_map/ppermute | solution.py:32
  84.7 3.6 %near_attention.1 = (bf16[256,2048]{1,0:T(8,128)(2,1)S(1)}, f32[256,2048]{1,0:T(8,128)S(1)}, f32[256,2048]{1,0:T(8,128)S(1)}, f32[256,2048]{1,0:T(8,128)S(1)}, f32[8,128]{1,0:T(8,128)S(1)}) custom-call(s32[2]{0:T(128)S(1)} %pad_add_fusion.position, bf16[136,2048]{1,0:T(8,128)(2,1)S(1)} %collective-permute-done.6.q_up, ...), custom_call_target="tpu_custom_call" | custom-call | flops 536870912 | bytes 4194304 | tf_op jit(solution)/shard_map/near_attention/pallas_call | solution.py:270
  88.3 2.8 %far_attention.1 = (bf16[128,2176]{1,0:T(8,128)(2,1)S(1)}, bf16[128,2176]{1,0:T(8,128)(2,1)S(1)}) custom-call(bf16[256,2048]{1,0:T(8,128)(2,1)S(1)} %get-tuple-element.28.qs, f32[256,2048]{1,0:T(8,128)S(1)} %get-tuple-element.29.sums, f32[256,2048]{1,0:T(8,128)S(1)} %get-tuple-element.30.tops, f32[256,2048]{1,0:T(8,128)S(1)} %get-tuple-element.31.norms, ...), custom_call_target="tpu_custom_call" | custom-call | flops 268435456 | bytes 4194304 | tf_op jit(solution)/shard_map/far_attention/pallas_call | solution.py:331
  91.1 1.9 %collective-permute-start.11 = (bf16[128,2176]{1,0:T(8,128)(2,1)S(1)}, bf16[128,2176]{1,0:T(8,128)(2,1)S(1)}, u32[]{:S(2)}, u32[]{:S(2)}) collective-permute-start(bf16[128,2176]{1,0:T(8,128)(2,1)S(1)} %get-tuple-element.33), channel_id=1, source_target_pairs={{0,16},{1,17},{2,18},{3,19},{4,20},{5,21},{6,22},{7,23},{8,24},{9,... | collective-permute-start | bytes 1671176 | tf_op jit(solution)/shard_map/ppermute | solution.py:32
  93.0 3.9 %collective-permute-start.12 = (bf16[128,2176]{1,0:T(8,128)(2,1)S(1)}, bf16[128,2176]{1,0:T(8,128)(2,1)S(1)}, u32[]{:S(2)}, u32[]{:S(2)}) collective-permute-start(bf16[128,2176]{1,0:T(8,128)(2,1)S(1)} %get-tuple-element.34), channel_id=1, source_target_pairs={{16,0},{17,1},{18,2},{19,3},{20,4},{21,5},{22,6},{23,7},{24,8},{25... | collective-permute-start | bytes 1671176 | tf_op jit(solution)/shard_map/ppermute | solution.py:32
  97.0 4.0 %own_attention.1 = (f32[128,2048]{1,0:T(8,128)S(1)}, f32[128,2048]{1,0:T(8,128)S(1)}) custom-call(s32[2]{0:T(128)S(1)} %pad_add_fusion.position, bf16[136,2048]{1,0:T(8,128)(2,1)S(1)} %get-tuple-element.20.message, bf16[128,2048]{1,0:T(8,128)(2,1)} %bitcast.17, bf16[128,2048]{1,0:T(8,128)(2,1)} %bitcast.21, bf16[32,2048]{1,0:T(8,128)(2,1)} %bitcast.27, ...), custom_call_target="tpu_custom_call" | custom-call | flops 536870912 | bytes 4194304 | tf_op jit(solution)/shard_map/own_attention/pallas_call | solution.py:394
  101.0 7.0 %collective-permute-done.11.above = bf16[128,2176]{1,0:T(8,128)(2,1)S(1)} collective-permute-done((bf16[128,2176]{1,0:T(8,128)(2,1)S(1)}, bf16[128,2176]{1,0:T(8,128)(2,1)S(1)}, u32[]{:S(2)}, u32[]{:S(2)}) %collective-permute-start.11) | collective-permute-done | bytes 557088 | tf_op jit(solution)/shard_map/ppermute | solution.py:32
  108.0 4.0 %collective-permute-done.12.below = bf16[128,2176]{1,0:T(8,128)(2,1)S(1)} collective-permute-done((bf16[128,2176]{1,0:T(8,128)(2,1)S(1)}, bf16[128,2176]{1,0:T(8,128)(2,1)S(1)}, u32[]{:S(2)}, u32[]{:S(2)}) %collective-permute-start.12) | collective-permute-done | bytes 557088 | tf_op jit(solution)/shard_map/ppermute | solution.py:32
  112.1 2.4 %merge.1 = bf16[128,2048]{1,0:T(8,128)(2,1)} custom-call(s32[2]{0:T(128)S(1)} %pad_add_fusion.position, f32[128,2048]{1,0:T(8,128)S(1)} %get-tuple-element.24.own, f32[128,2048]{1,0:T(8,128)S(1)} %get-tuple-element.25.own_logs, bf16[128,2176]{1,0:T(8,128)(2,1)S(1)} %collective-permute-done.11.above, bf16[128,2176]{1,0:T(8,128)(2,1)S(1)} %collective-permute-done.12.below), custom_call_target="tpu_custom_call" | custom-call | tf_op jit(solution)/shard_map/merge/pallas_call | solution.py:436
  (14 shorter events, 2.8 us)
Async XLA Ops:
  0.1 0.7 copy-start
  2.8 39.9 %collective-permute-start.8 = (bf16[72,2048]{1,0:T(8,128)(2,1)S(1)}, bf16[72,2048]{1,0:T(8,128)(2,1)S(1)}, u32[]{:S(2)}, u32[]{:S(2)}) collective-permute-start(bf16[72,2048]{1,0:T(8,128)(2,1)S(1)} %get-tuple-element.26), channel_id=1, source_target_pairs={{112,128},{113,129},{114,130},{115,131},{116,132},{117,133},{118,1... | collective-permute-start | bytes 884744 | tf_op jit(solution)/shard_map/ppermute | solution.py:32
  8.1 29.6 %collective-permute-start.9 = (bf16[64,2048]{1,0:T(8,128)(2,1)S(1)}, bf16[64,2048]{1,0:T(8,128)(2,1)S(1)}, u32[]{:S(2)}, u32[]{:S(2)}) collective-permute-start(bf16[64,2048]{1,0:T(8,128)(2,1)S(1)} %get-tuple-element.27), channel_id=1, source_target_pairs={{112,240},{113,241},{114,242},{115,243},{116,244},{117,245},{118,2... | collective-permute-start | bytes 786440 | tf_op jit(solution)/shard_map/ppermute | solution.py:32
  12.4 72.3 %collective-permute-start = (bf16[192,2048]{1,0:T(8,128)(2,1)S(1)}, bf16[192,2048]{1,0:T(8,128)(2,1)S(1)}, u32[]{:S(2)}, u32[]{:S(2)}) collective-permute-start(bf16[192,2048]{1,0:T(8,128)(2,1)S(1)} %get-tuple-element.21), channel_id=1, source_target_pairs={{0,1},{1,0},{2,3},{3,2},{4,5},{5,4},{6,7},{7,6},{8,9},{9,8},{10,11... | collective-permute-start | bytes 2359304 | tf_op jit(solution)/shard_map/ppermute | solution.py:32
  14.3 6.4 %collective-permute-start.2 = (bf16[2,8,2048]{2,1,0:T(8,128)(2,1)S(1)}, bf16[2,8,2048]{2,1,0:T(8,128)(2,1)S(1)}, u32[]{:S(2)}, u32[]{:S(2)}) collective-permute-start(bf16[2,8,2048]{2,1,0:T(8,128)(2,1)S(1)} %get-tuple-element.23.first), channel_id=1, source_target_pairs={{0,4},{1,5},{2,6},{3,7},{4,0},{5,1},{6,2},{7,3},{8,12},{9,13},{10,... | collective-permute-start | bytes 196616 | tf_op jit(solution)/shard_map/ppermute | solution.py:32
  17.7 70.5 %collective-permute-start.1 = (bf16[192,2048]{1,0:T(8,128)(2,1)S(1)}, bf16[192,2048]{1,0:T(8,128)(2,1)S(1)}, u32[]{:S(2)}, u32[]{:S(2)}) collective-permute-start(bf16[192,2048]{1,0:T(8,128)(2,1)S(1)} %get-tuple-element.22), channel_id=1, source_target_pairs={{1,2},{2,1},{3,4},{4,3},{5,6},{6,5},{7,8},{8,7},{9,10},{10,9},{11,... | collective-permute-start | bytes 2359304 | tf_op jit(solution)/shard_map/ppermute | solution.py:32
  20.9 15.5 %collective-permute-start.3 = (bf16[2,16,2048]{2,1,0:T(8,128)(2,1)S(1)}, bf16[2,16,2048]{2,1,0:T(8,128)(2,1)S(1)}, u32[]{:S(2)}, u32[]{:S(2)}) collective-permute-start(bf16[2,16,2048]{2,1,0:T(8,128)(2,1)S(1)} %join.3.first), channel_id=1, source_target_pairs={{0,8},{1,9},{2,10},{3,11},{4,12},{5,13},{6,14},{7,15},{8,0},{9,1},... | collective-permute-start | bytes 393224 | tf_op jit(solution)/shard_map/ppermute | solution.py:32
  36.4 48.2 %collective-permute-start.6 = (bf16[136,2048]{1,0:T(8,128)(2,1)S(1)}, bf16[136,2048]{1,0:T(8,128)(2,1)S(1)}, u32[]{:S(2)}, u32[]{:S(2)}) collective-permute-start(bf16[136,2048]{1,0:T(8,128)(2,1)S(1)} %get-tuple-element.20.message), channel_id=1, source_target_pairs={{0,16},{1,17},{2,18},{3,19},{4,20},{5,21},{6,22},{7,23},{8,24},{9,... | collective-permute-start | bytes 1671176 | tf_op jit(solution)/shard_map/ppermute | solution.py:32
  37.7 47.0 %collective-permute-start.7 = (bf16[136,2048]{1,0:T(8,128)(2,1)S(1)}, bf16[136,2048]{1,0:T(8,128)(2,1)S(1)}, u32[]{:S(2)}, u32[]{:S(2)}) collective-permute-start(bf16[136,2048]{1,0:T(8,128)(2,1)S(1)} %get-tuple-element.20.message), channel_id=1, source_target_pairs={{16,0},{17,1},{18,2},{19,3},{20,4},{21,5},{22,6},{23,7},{24,8},{25... | collective-permute-start | bytes 1671176 | tf_op jit(solution)/shard_map/ppermute | solution.py:32
  42.7 28.7 %collective-permute-start.4 = (bf16[2,32,2048]{2,1,0:T(8,128)(2,1)S(1)}, bf16[2,32,2048]{2,1,0:T(8,128)(2,1)S(1)}, u32[]{:S(2)}, u32[]{:S(2)}) collective-permute-start(bf16[2,32,2048]{2,1,0:T(8,128)(2,1)S(1)} %join.4.first), channel_id=1, source_target_pairs={{0,386},{1,387},{2,384},{3,385},{4,390},{5,391},{6,388},{7,389},{8... | collective-permute-start | bytes 786440 | tf_op jit(solution)/shard_map/ppermute | solution.py:32
  71.4 11.3 %collective-permute-start.10 = (bf16[64,2048]{1,0:T(8,128)(2,1)S(1)}, bf16[64,2048]{1,0:T(8,128)(2,1)S(1)}, u32[]{:S(2)}, u32[]{:S(2)}) collective-permute-start(bf16[64,2048]{1,0:T(8,128)(2,1)S(1)} %collective-permute-done.9), channel_id=1, source_target_pairs={{0,112},{1,113},{2,114},{3,115},{4,116},{5,117},{6,118},{7,119},{8... | collective-permute-start | bytes 786440 | tf_op jit(solution)/shard_map/ppermute | solution.py:32
  82.7 14.2 %collective-permute-start.5 = (bf16[2,64,2048]{2,1,0:T(8,128)(2,1)S(1)}, bf16[2,64,2048]{2,1,0:T(8,128)(2,1)S(1)}, u32[]{:S(2)}, u32[]{:S(2)}) collective-permute-start(bf16[2,64,2048]{2,1,0:T(8,128)(2,1)S(1)} %join.5.top_a), channel_id=1, source_target_pairs={{0,1},{1,0},{2,3},{3,2},{4,5},{5,4},{6,7},{7,6},{8,9},{9,8},{10,11... | collective-permute-start | bytes 1572872 | tf_op jit(solution)/shard_map/ppermute | solution.py:32
  91.1 16.9 %collective-permute-start.11 = (bf16[128,2176]{1,0:T(8,128)(2,1)S(1)}, bf16[128,2176]{1,0:T(8,128)(2,1)S(1)}, u32[]{:S(2)}, u32[]{:S(2)}) collective-permute-start(bf16[128,2176]{1,0:T(8,128)(2,1)S(1)} %get-tuple-element.33), channel_id=1, source_target_pairs={{0,16},{1,17},{2,18},{3,19},{4,20},{5,21},{6,22},{7,23},{8,24},{9,... | collective-permute-start | bytes 1671176 | tf_op jit(solution)/shard_map/ppermute | solution.py:32
  93.0 19.0 %collective-permute-start.12 = (bf16[128,2176]{1,0:T(8,128)(2,1)S(1)}, bf16[128,2176]{1,0:T(8,128)(2,1)S(1)}, u32[]{:S(2)}, u32[]{:S(2)}) collective-permute-start(bf16[128,2176]{1,0:T(8,128)(2,1)S(1)} %get-tuple-element.34), channel_id=1, source_target_pairs={{16,0},{17,1},{18,2},{19,3},{20,4},{21,5},{22,6},{23,7},{24,8},{25... | collective-permute-start | bytes 1671176 | tf_op jit(solution)/shard_map/ppermute | solution.py:32
